TPU v7x, 128 devices: a whole 4x4x4 slice. The times are simulated.
128 devices in a mesh: row: 16 (over x, y), col: 8 (over z, core).
Axes of the slice: x: 4, y: 4, z: 4, core: 2. Of those that a mesh axis runs over, the one named last changes fastest.
Arguments:
- trial_vectors: float32 [32768, 256], P(('row', 'col')), may hold values from -6 to 6
- tiles: float32 [16, 8, 128, 128, 128], P('row', 'col'), may hold values from 0.0012207031 to 0.024414062
- tile_rows: int32 [16, 8, 128], P('row', 'col'), may hold values from 0 to 15
- tile_cols: int32 [16, 8, 128], P('row', 'col'), may hold values from 0 to 31
- tile_count: int32 [16, 8], P('row', 'col'), may hold values from 1 to 128, as said below
Outputs:
- basis: float32 [32768, 256], P(('row', 'col'))
Inputs may be any that keep to these rules, and one draw needn't show every extreme that they name: `tile_count`: slots at or beyond a device's count are not part of the graph; some slab and column group holds exactly 128 live slots.
All inputs are finite; a program needn't handle non-finite values.
Results may differ from a plain program's by a relative error of at most 0.0003.
Values sent between devices are 32-bit elements; how exact they have to be, the bound alone decides.
No kernel may reach another device: no remote copies, remote signals or barrier semaphores. Data moves between devices by JAX's collectives and lax.ppermute only.
A program may use at most 128 MiB of HBM per device.

v0:
```python
import math

import jax
import jax.numpy as jnp
from jax import lax
from jax.sharding import PartitionSpec as P

ITERS = 2


HIGHEST = lax.Precision.HIGHEST


def apply_tiles(tiles_dev, put_index, take_index, live_count, source, out_blocks, adjoint):
    slot_total = tiles_dev.shape[0]
    slot_step = min(32, slot_total)
    size_block = tiles_dev.shape[-1]
    vector_width = source.shape[-1]
    targets = jnp.arange(out_blocks, dtype=jnp.int32)

    def one_block(block_number, running):
        first_slot = block_number * slot_step
        tiles_now = lax.dynamic_slice_in_dim(tiles_dev, first_slot, slot_step, 0)
        put_now = lax.dynamic_slice_in_dim(put_index, first_slot, slot_step, 0)
        take_now = lax.dynamic_slice_in_dim(take_index, first_slot, slot_step, 0)
        alive_mask = first_slot + jnp.arange(slot_step, dtype=jnp.int32) < live_count
        picked = source[take_now]
        if adjoint:
            product = jnp.einsum("sij,sik->sjk", tiles_now, picked, precision=HIGHEST)
        else:
            product = jnp.einsum("sij,sjk->sik", tiles_now, picked, precision=HIGHEST)
        placing = ((put_now[None, :] == targets[:, None]) & alive_mask[None, :]).astype(jnp.float32)
        return running + jnp.einsum("os,sik->oik", placing, product, precision=HIGHEST)

    initial = jnp.zeros((out_blocks, size_block, vector_width), jnp.float32)
    upper_bound = (live_count + slot_step - 1) // slot_step
    return lax.fori_loop(jnp.int32(0), upper_bound, one_block, initial)


def add_at(target, offset, addend):
    current = lax.dynamic_slice_in_dim(target, offset, addend.shape[0], 0)
    return lax.dynamic_update_slice_in_dim(target, current + addend, offset, 0)


def local(trial_vectors, tiles, tile_rows, tile_cols, tile_count):
    row_devices = lax.axis_size("row")
    col_devices = lax.axis_size("col")
    size_block = tiles.shape[-1]
    slot_total = tiles.shape[2]
    vector_width = trial_vectors.shape[1]
    own_blocks = trial_vectors.shape[0] // size_block
    slab_blocks = own_blocks * col_devices
    member_blocks = own_blocks * row_devices
    tiles_dev = tiles.reshape(slot_total, size_block, size_block)
    row_index = tile_rows.reshape(slot_total)
    col_index = tile_cols.reshape(slot_total)
    live_count = tile_count.reshape(())
    col_place = lax.axis_index("col") * own_blocks
    row_place = lax.axis_index("row") * own_blocks
    all_ones = jnp.ones((member_blocks, size_block, 1), jnp.float32)
    row_part = apply_tiles(
        tiles_dev, row_index, col_index, live_count, all_ones, slab_blocks, False
    )[..., 0]
    inverse_slab = 1.0 / (1.0 + lax.psum(row_part, "col"))
    inverse_own = lax.dynamic_slice_in_dim(inverse_slab, col_place, own_blocks, 0)
    vectors = trial_vectors.reshape(own_blocks, size_block, vector_width)
    inverse_cols, gathered = (
        lax.all_gather(inverse_own, "row", axis=0, tiled=True),
        lax.all_gather(vectors, "row", axis=0, tiled=True),
    )
    tilde_part = apply_tiles(
        tiles_dev, row_index, col_index, live_count, inverse_cols[..., None], slab_blocks, False
    )[..., 0]
    tilde_slab = inverse_slab * (inverse_slab + lax.psum(tilde_part, "col"))
    scale_slab = inverse_slab / tilde_slab
    scale_own = lax.dynamic_slice_in_dim(scale_slab, col_place, own_blocks, 0)
    for iteration in range(ITERS):
        if iteration > 0:
            gathered = lax.all_gather(vectors, "row", axis=0, tiled=True)
        forward = apply_tiles(
            tiles_dev,
            row_index,
            col_index,
            live_count,
            inverse_cols[..., None] * gathered,
            slab_blocks,
            False,
        )
        forward = add_at(forward, col_place, inverse_own[..., None] * vectors)
        summed = lax.psum_scatter(forward, "col", scatter_dimension=0, tiled=True)
        weighted_own = scale_own[..., None] * (scale_own[..., None] * summed)
        weighted_slab = lax.all_gather(weighted_own, "col", axis=0, tiled=True)
        backward = apply_tiles(
            tiles_dev, col_index, row_index, live_count, weighted_slab, member_blocks, True
        )
        backward = add_at(backward, row_place, weighted_own)
        reduced = lax.psum_scatter(backward, "row", scatter_dimension=0, tiled=True)
        node_rows = (inverse_own[..., None] * reduced).reshape(-1, vector_width)
        local_gram = jnp.dot(
            node_rows.T, node_rows, precision=HIGHEST, preferred_element_type=jnp.float32
        )
        gram_matrix = lax.psum(local_gram, ("row", "col"))
        factor_low = jnp.linalg.cholesky(gram_matrix)
        solved = lax.linalg.triangular_solve(
            factor_low, node_rows, left_side=False, lower=True, transpose_a=True
        )
        vectors = solved.reshape(own_blocks, size_block, vector_width)
    total_nodes = own_blocks * size_block * row_devices * col_devices
    return vectors.reshape(-1, vector_width) * math.sqrt(total_nodes)


def solution(mesh):
    in_specs = (
        P(("row", "col"), None),
        P("row", "col", None, None, None),
        P("row", "col", None),
        P("row", "col", None),
        P("row", "col"),
    )
    out_specs = P(("row", "col"), None)
    return jax.shard_map(local, mesh=mesh, in_specs=in_specs, out_specs=out_specs, check_vma=False)
```

profile of v0, /device:TPU:1, one launch (start us, length us, event | category | flops | bytes accessed | tf_op | source)
XLA Modules:
  0.0 1161.9 jit_solution(10338575145298387304)
XLA Ops:
  8.0 7.8 while.70
  9.3 4.9 fusion.167
  15.8 37.8 %psum.28 = f32[16,128]{1,0:T(8,128)S(1)} all-reduce(f32[16,128]{1,0:T(8,128)S(1)} %bitcast.189), channel_id=1, replica_groups=mesh['row'=16,'col'=8] {'col'}, use_global_device_ids=true, to_apply=%region_2.3 | all-reduce | flops 2048 | bytes 16384 | tf_op jit(solution)/shard_map/psum | solution.py:64
  53.7 19.4 %all-gather = f32[16,2,128]{2,1,0:T(2,128)S(1)} all-gather(f32[1,2,128]{2,1,0:T(2,128)S(1)} %fusion.124), channel_id=1, replica_groups=mesh['row'=16,'col'=8] {'row'}, dimensions={0}, use_global_device_ids=true | all-gather | bytes 17408 | tf_op jit(solution)/shard_map/all_gather | solution.py:68
  73.1 3.9 broadcast_multiply_fusion.1
  77.3 17.7 %while.72 = (s32[]{:T(128)}, f32[16,128,256]{2,0,1:T(8,128)S(1)}, s32[]{:T(128)}, s32[128]{0:T(128)S(1)}, s32[]{:T(128)}, /*index=5*/f32[128,128,128]{2,1,0:T(8,...) while((s32[]{:T(128)}, f32[16,128,256]{2,0,1:T(8,128)S(1)}, ...), condition=%wide.region_7.8_spmd.clone, body=%wide.region_6.7_spmd.clone.sunk | while | flops 1812465920 | bytes 27268216 | solution.py:37
  77.9 4.9 gather_fusion.2
  82.9 6.7 fusion.179
  90.3 4.7 fusion.180
  95.0 2.6 copy.50
  97.6 1.8 add_dynamic-update-slice_fusion.3
  99.5 6.7 while.71
  100.3 4.9 fusion.173
  106.1 82.7 %psum.29 = f32[16,128]{1,0:T(8,128)S(1)} all-reduce(f32[16,128]{1,0:T(8,128)S(1)} %bitcast.190), channel_id=1, replica_groups=mesh['row'=16,'col'=8] {'col'}, use_global_device_ids=true, to_apply=%region_5.6 | all-reduce | flops 2048 | bytes 16384 | tf_op jit(solution)/shard_map/psum | solution.py:74
  188.9 1.8 multiply_multiply_fusion.1
  190.8 9.0 copy.45
  199.8 19.4 %all-gather.8.cloned.1.call-done = f32[16,128,256]{2,1,0:T(8,128)} async-done(((f32[2,128,256]{2,1,0:T(8,128)}), f32[16,128,256]{2,1,0:T(8,128)}) %all-gather.8.cloned.1.call-update) | async-done | bytes 2097168 | tf_op jit(solution)/shard_map/all_gather | solution.py:92
  219.2 2.5 broadcast.184.clone
  221.7 19.2 %while.73 = (s32[]{:T(128)}, f32[32,128,256]{2,0,1:T(8,128)}, s32[]{:T(128)}, s32[128]{0:T(128)S(1)}, s32[]{:T(128)}, /*index=5*/f32[128,128,128]{1,2,0:T(8,128)...) while((s32[]{:T(128)}, f32[32,128,256]{2,0,1:T(8,128)}, ...), condition=%wide.region_10.11_spmd.clone, body=%wide.region_9.10_spmd.clone.sunk | while | flops 2014317824 | bytes 31462520 | solution.py:37
  221.8 2.7 gather_fusion.3
  224.6 6.7 fusion.185
  232.0 9.0 fusion.186
  241.0 6.6 copy.52
  247.6 1.8 add_dynamic-update-slice_fusion.2
  249.8 132.5 %reduce-scatter.7.cloned.1.call-done = f32[2,128,256]{2,1,0:T(8,128)} async-done(((f32[32,128,256]{2,1,0:T(8,128)}), f32[2,128,256]{2,1,0:T(8,128)}) %reduce-scatter.7.cloned.1.call-update) | async-done | bytes 262160 | tf_op jit(solution)/shard_map/reduce_scatter | solution.py:97
  383.3 1.3 convolution_bitcast_fusion.3
  384.7 145.5 %all-reduce.4.cloned.1.call-done = f32[256,256]{0,1:T(8,128)} async-done(((f32[256,256]{0,1:T(8,128)}), f32[256,256]{0,1:T(8,128)}) %all-reduce.4.cloned.1.call-update) | async-done | bytes 262160 | tf_op jit(solution)/shard_map/psum | solution.py:102
  530.2 1.1 copy.55
  532.3 11.7 %cholesky.130 = f32[128,128]{1,0:T(8,128)S(1)} custom-call(f32[128,128]{1,0:T(8,128)S(1)} %cholesky.194), custom_call_target="Cholesky" | custom-call | tf_op jit(solution)/shard_map/jit(cholesky)/cholesky | solution.py:103
  544.1 9.8 custom-call.13
  554.4 11.7 %cholesky.147 = f32[128,128]{1,0:T(8,128)S(1)} custom-call(f32[128,128]{1,0:T(8,128)S(1)} %convolution_subtract_fusion.3), custom_call_target="Cholesky" | custom-call | tf_op jit(solution)/shard_map/jit(cholesky)/cholesky | solution.py:103
  568.2 4.1 while.76
  569.0 1.4 bitcast_dynamic-update-slice_fusion.4
  571.0 1.4 bitcast_dynamic-update-slice_fusion.4
  572.4 19.7 %custom-call.14 = f32[2,128,128]{1,2,0:T(8,128)S(1)} custom-call(f32[2,128,128]{2,1,0:T(8,128)S(1)} %get-tuple-element.422), custom_call_target="InvertDiagBlocksLowerTriangular" | custom-call | tf_op jit(solution)/shard_map/triangular_solve/custom-call.0 | solution.py:104
  594.0 48.9 %all-gather.10.cloned.1.call-done = f32[32,128,256]{2,1,0:T(8,128)} async-done(((f32[2,128,256]{2,1,0:T(8,128)}), f32[32,128,256]{2,1,0:T(8,128)}) %all-gather.10.cloned.1.call-update) | async-done | bytes 4194320 | tf_op jit(solution)/shard_map/all_gather | solution.py:79
  642.9 3.9 broadcast_multiply_fusion
  647.1 17.6 %while.74 = (s32[]{:T(128)}, f32[16,128,256]{2,0,1:T(8,128)S(1)}, s32[]{:T(128)}, s32[128]{0:T(128)S(1)}, s32[]{:T(128)}, /*index=5*/f32[128,128,128]{2,1,0:T(8,...) while((s32[]{:T(128)}, f32[16,128,256]{2,0,1:T(8,128)S(1)}, ...), condition=%wide.region_18.21_spmd.clone, body=%wide.region_17.20_spmd.clone.sunk | while | flops 1812465920 | bytes 27268216 | solution.py:37
  647.2 4.9 gather_fusion.4
  652.1 6.7 fusion.191
  659.5 4.7 fusion.192
  664.7 2.6 copy.60
  667.3 1.8 add_dynamic-update-slice_fusion.1
  669.1 81.2 %reduce-scatter.9.cloned.1.call-done = f32[2,128,256]{2,1,0:T(8,128)} async-done(((f32[16,128,256]{2,1,0:T(8,128)}), f32[2,128,256]{2,1,0:T(8,128)}) %reduce-scatter.9.cloned.1.call-update) | async-done | bytes 262160 | tf_op jit(solution)/shard_map/reduce_scatter | solution.py:90
  750.3 1.8 multiply_multiply_fusion
  752.2 27.7 %all-gather.12.cloned.1.call-done = f32[16,128,256]{2,1,0:T(8,128)} async-done(((f32[2,128,256]{2,1,0:T(8,128)}), f32[16,128,256]{2,1,0:T(8,128)}) %all-gather.12.cloned.1.call-update) | async-done | bytes 2097168 | tf_op jit(solution)/shard_map/all_gather | solution.py:92
  779.9 2.5 broadcast.184
  782.4 19.4 %while.75 = (s32[]{:T(128)}, f32[32,128,256]{2,0,1:T(8,128)}, s32[]{:T(128)}, s32[128]{0:T(128)S(1)}, s32[]{:T(128)}, /*index=5*/f32[128,128,128]{1,2,0:T(8,128)...) while((s32[]{:T(128)}, f32[32,128,256]{2,0,1:T(8,128)}, ...), condition=%wide.region_21.24_spmd.clone, body=%wide.region_20.23_spmd.clone.sunk | while | flops 2014317824 | bytes 31462520 | solution.py:37
  782.4 2.7 gather_fusion.5
  785.2 6.7 fusion.197
  792.6 9.0 fusion.198
  801.7 6.6 copy.62
  808.3 1.7 add_dynamic-update-slice_fusion
  810.2 132.9 %reduce-scatter.11.cloned.1.call-done = f32[2,128,256]{2,1,0:T(8,128)} async-done(((f32[32,128,256]{2,1,0:T(8,128)}), f32[2,128,256]{2,1,0:T(8,128)}) %reduce-scatter.11.cloned.1.call-update) | async-done | bytes 262160 | tf_op jit(solution)/shard_map/reduce_scatter | solution.py:97
  944.2 1.3 convolution_bitcast_fusion.2
  945.5 144.9 %all-reduce.6.cloned.1.call-done = f32[256,256]{0,1:T(8,128)} async-done(((f32[256,256]{0,1:T(8,128)}), f32[256,256]{0,1:T(8,128)}) %all-reduce.6.cloned.1.call-update) | async-done | bytes 262160 | tf_op jit(solution)/shard_map/psum | solution.py:102
  1090.3 1.1 copy.65
  1092.4 11.7 %cholesky.164 = f32[128,128]{1,0:T(8,128)S(1)} custom-call(f32[128,128]{1,0:T(8,128)S(1)} %cholesky.197), custom_call_target="Cholesky" | custom-call | tf_op jit(solution)/shard_map/jit(cholesky)/cholesky | solution.py:103
  1104.2 9.8 custom-call.15
  1114.5 11.7 %cholesky.181 = f32[128,128]{1,0:T(8,128)S(1)} custom-call(f32[128,128]{1,0:T(8,128)S(1)} %convolution_subtract_fusion.2), custom_call_target="Cholesky" | custom-call | tf_op jit(solution)/shard_map/jit(cholesky)/cholesky | solution.py:103
  1129.0 4.3 while.77
  1129.8 1.4 bitcast_dynamic-update-slice_fusion.5
  1131.8 1.4 bitcast_dynamic-update-slice_fusion.5
  1133.3 19.7 %custom-call.16 = f32[2,128,128]{1,2,0:T(8,128)S(1)} custom-call(f32[2,128,128]{2,1,0:T(8,128)S(1)} %get-tuple-element.423), custom_call_target="InvertDiagBlocksLowerTriangular" | custom-call | tf_op jit(solution)/shard_map/triangular_solve/custom-call.0 | solution.py:104
  (118 shorter events, 23.4 us)
Async XLA Ops:
  6.5 66.5 %all-gather.6.cloned.1.call-start = ((), (), s32[]{:S(2)}) async-start(), calls=%async_computation.4 | async-start | bytes 4456448 | tf_op jit(solution)/shard_map/all_gather | solution.py:69
  7.3 181.7 %reduce-scatter.5.cloned.1.call-start = ((), (), s32[]{:S(2)}) async-start(), calls=%async_computation.5 | async-start | bytes 2359296 | tf_op jit(solution)/shard_map/reduce_scatter | solution.py:90
  73.1 4.2 copy-start.6
  73.1 4.2 copy-start.7
  95.0 2.6 copy-start.3
  99.4 119.8 %all-gather.8.cloned.1.call-start = ((), (), s32[]{:S(2)}) async-start(), calls=%async_computation.6 | async-start | bytes 2359296 | tf_op jit(solution)/shard_map/all_gather | solution.py:92
  190.7 191.6 %reduce-scatter.7.cloned.1.call-start = ((), (), s32[]{:S(2)}) async-start(), calls=%async_computation.7 | async-start | bytes 4456448 | tf_op jit(solution)/shard_map/reduce_scatter | solution.py:97
  219.2 2.5 copy-start
  241.0 6.6 copy-start.4
  249.3 280.9 %all-reduce.4.cloned.1.call-start = ((), (), s32[]{:S(2)}) async-start(), calls=%async_computation.8 | async-start | bytes 524288 | tf_op jit(solution)/shard_map/psum | solution.py:102
  384.7 258.3 %all-gather.10.cloned.1.call-start = ((), (), s32[]{:S(2)}) async-start(), calls=%async_computation.9 | async-start | bytes 4456448 | tf_op jit(solution)/shard_map/all_gather | solution.py:79
  594.0 156.4 %reduce-scatter.9.cloned.1.call-start = ((), (), s32[]{:S(2)}) async-start(), calls=%async_computation.10 | async-start | bytes 2359296 | tf_op jit(solution)/shard_map/reduce_scatter | solution.py:90
  664.7 2.6 copy-start.2
  669.1 110.8 %all-gather.12.cloned.1.call-start = ((), (), s32[]{:S(2)}) async-start(), calls=%async_computation.11 | async-start | bytes 2359296 | tf_op jit(solution)/shard_map/all_gather | solution.py:92
  752.1 191.0 %reduce-scatter.11.cloned.1.call-start = ((), (), s32[]{:S(2)}) async-start(), calls=%async_computation.12 | async-start | bytes 4456448 | tf_op jit(solution)/shard_map/reduce_scatter | solution.py:97
  779.9 2.5 copy-start.1
  801.7 6.6 copy-start.5
  810.1 280.2 %all-reduce.6.cloned.1.call-start = ((), (), s32[]{:S(2)}) async-start(), calls=%async_computation.13 | async-start | bytes 524288 | tf_op jit(solution)/shard_map/psum | solution.py:102
Sparse Core Ops, SparseCore 0:
  9.5 54.6 all-gather.5
  99.5 83.9 reduce-scatter.4
  190.8 28.3 all-gather.7
  249.5 132.7 reduce-scatter.6
  387.6 142.5 all-reduce.3
  594.1 48.7 all-gather.9
  669.2 81.0 reduce-scatter.8
  752.2 27.5 all-gather.11
  810.2 132.8 reduce-scatter.10
  947.7 142.5 all-reduce.5
where the time goes:
time: 1170 us; the launch traced here: 1160 us
  waiting for transfers between devices  734 us (63%)
  blocking collectives  140 us (12%)
  other arithmetic  136 us (12%)
  matrix products  69.8 us (6%)
  local copies, waits for them, and re-layouts  62.4 us (5%)
  between operations  17.5 us (1%)
    psum x2, waiting for transfers between devices, local(): gram_matrix = lax.psum(local_gram, ('row', 'col'))  290 us
    reduce_scatter x2, waiting for transfers between devices, local(): reduced = lax.psum_scatter(backward, 'row', scatter_dimension=0, tiled=True)  265 us
    psum x1, blocking collectives, local(): tilde_slab = inverse_slab * (inverse_slab + lax.psum(tilde_part, 'col'))  82.7 us
    reduce_scatter x2, waiting for transfers between devices, local(): summed = lax.psum_scatter(forward, 'col', scatter_dimension=0, tiled=True)  81.2 us
    another operation x13, other arithmetic, local(): factor_low = jnp.linalg.cholesky(gram_matrix)  68.6 us
    all_gather x1, waiting for transfers between devices, local(): gathered = lax.all_gather(vectors, 'row', axis=0, tiled=True)  48.9 us
    all_gather x2, waiting for transfers between devices, local(): weighted_slab = lax.all_gather(weighted_own, 'col', axis=0, tiled=True)  47.1 us
    another operation x6, other arithmetic, local(): lax.linalg.triangular_solve(factor_low, node_rows, left_side=False, lower...  39.4 us
  transfers between devices with their start and end apart: 10, of which 8 were waited for; matrix products, arithmetic and copies ran while one was open for 2% of the time, Pallas kernels for 0%

commit v1 on v0

v1 whole, which is shorter than its diff:
```python
import functools
import math

import jax
import jax.numpy as jnp
from jax import lax
from jax.experimental import pallas as pl
from jax.experimental.pallas import tpu as pltpu
from jax.sharding import Mesh
from jax.sharding import PartitionSpec as P

ITERS = 2
HIGHEST = lax.Precision.HIGHEST
F32 = jnp.float32
BF16 = jnp.bfloat16
BLK = 128
CHUNK = 16
RING = range(4)


def shift(value, axis, amount):
    return lax.ppermute(value, axis, [(i, (i + amount) % 4) for i in RING])


def swap(value):
    return lax.ppermute(value, "c", [(0, 1), (1, 0)])


def ring_all(value, axis):
    return [value] + [shift(value, axis, k) for k in (1, 2, 3)]


def ring_sum(value, axis):
    a, b, c, d = ring_all(value, axis)
    return (a + b) + (c + d)


def ring_scatter(pieces, axis):
    a = pieces[0]
    b, c, d = [shift(pieces[k], axis, k) for k in (1, 2, 3)]
    return (a + b) + (c + d)


def split(value):
    high = value.astype(BF16)
    return high, (value - high.astype(F32)).astype(BF16)


def nt_dot(a, b, precision=HIGHEST):
    return lax.dot_general(
        a, b, (((1,), (1,)), ((), ())), precision=precision, preferred_element_type=F32
    )


def lane_sums(block):
    return nt_dot(jnp.ones((8, block.shape[1]), F32), block)[0:1, :]


def live_tile(tiles_ref, slot, first, count):
    return jnp.where(first + slot < count, tiles_ref[slot], 0.0)


def rowsum_kernel(count_ref, put_ref, tiles_ref, out_ref, total):
    step = pl.program_id(0)
    count = count_ref[0]

    @pl.when(step == 0)
    def _():
        total[...] = jnp.zeros_like(total)

    first = step * CHUNK

    @pl.when(first < count)
    def _():
        def one(slot, carry):
            block = put_ref[first + slot]
            total[block] += live_tile(tiles_ref, slot, first, count)
            return carry

        lax.fori_loop(0, CHUNK, one, 0)

    @pl.when(step == pl.num_programs(0) - 1)
    def _():
        for block in range(total.shape[0]):
            out_ref[block : block + 1, :] = lane_sums(total[block])


def chunk_map(step, count_ref, *_):
    return (jnp.minimum(step, (count_ref[0] + CHUNK - 1) // CHUNK - 1), 0, 0)


def rowsum_call(count, put, tiles, out_blocks):
    slots = tiles.shape[0]
    return pl.pallas_call(
        rowsum_kernel,
        out_shape=jax.ShapeDtypeStruct((out_blocks, BLK), F32),
        grid_spec=pltpu.PrefetchScalarGridSpec(
            num_scalar_prefetch=2,
            grid=(slots // CHUNK,),
            in_specs=[pl.BlockSpec((CHUNK, BLK, BLK), chunk_map)],
            out_specs=pl.BlockSpec((out_blocks, BLK), lambda s, *_: (0, 0)),
            scratch_shapes=[pltpu.VMEM((out_blocks, BLK, BLK), F32)],
        ),
        cost_estimate=pl.CostEstimate(flops=10**6, bytes_accessed=2**23, transcendentals=0),
    )(count, put, tiles)


def apply_loop(
    count, first, put_ref, take_ref, tiles_ref, source, total, adjoint, tilde, inverse_ref
):
    def one(slot, carry):
        tile = live_tile(tiles_ref, slot, first, count)
        take = take_ref[first + slot]
        put = pl.multiple_of(put_ref[first + slot], 8)
        if tilde is not None:
            tilde_block = carry_block = put_ref[tiles_total(put_ref) + first + slot]
            tilde[tilde_block] += tile * inverse_ref[pl.ds(take, 1), :]
        if adjoint:
            tile = tile.T
        high, low = split(tile)
        product = jnp.dot(
            jnp.concatenate([high, high], axis=1), source[take], preferred_element_type=F32
        ) + jnp.dot(low, source[take, :BLK], preferred_element_type=F32)
        total[pl.ds(put, BLK), :] += product
        return carry

    lax.fori_loop(0, CHUNK, one, 0, unroll=4)


def tiles_total(put_ref):
    return put_ref.shape[0] // 2


def put_source(source, index, value):
    high, low = split(value)
    source[index, :BLK] = high
    source[index, BLK:] = low


def forward_kernel(first_pass, *refs):
    count_ref, put_ref, take_ref, tiles_ref, inverse_ref = refs[:5]
    factor_ref = None
    refs = refs[5:]
    if not first_pass:
        factor_ref, refs = refs[0], refs[1:]
    pieces, (keep_ref, send_ref), refs = refs[:8], refs[8:10], refs[10:]
    source, total = refs[:2]
    tilde = refs[2] if first_pass else None
    step = pl.program_id(0)
    count = count_ref[0]
    first = step * CHUNK

    @pl.when(step == 0)
    def _():
        total[...] = jnp.zeros_like(total)
        if first_pass:
            tilde[...] = jnp.zeros_like(tilde)
        inverse = inverse_ref[...].T
        for number, piece in enumerate(pieces):
            if first_pass:
                values = None
            else:
                values = nt_dot(piece[...].reshape(4 * BLK, -1), factor_ref[...])
            for part in RING:
                index = number * 4 + part
                value = piece[part] if first_pass else values[part * BLK : (part + 1) * BLK]
                put_source(source, index, value * inverse[:, index : index + 1])

    @pl.when(first < count)
    def _():
        apply_loop(
            count, first, put_ref, take_ref, tiles_ref, source, total, False, tilde, inverse_ref
        )

    @pl.when(step == pl.num_programs(0) - 1)
    def _():
        rows = keep_ref.shape[1]
        for number in range(8):
            if first_pass:
                line = jnp.concatenate(
                    [lane_sums(tilde[2 * number]), lane_sums(tilde[2 * number + 1])], axis=1
                )
                total[number * rows + 2 * BLK : (number + 1) * rows, :] = jnp.broadcast_to(
                    line, (rows - 2 * BLK, line.shape[1])
                )
            target = keep_ref if number < 4 else send_ref
            target[number % 4] = total[number * rows : (number + 1) * rows, :]


def whole(shape):
    return pl.BlockSpec(shape, lambda s, *_: (0,) * len(shape), pipeline_mode=pl.Buffered(1))


def forward_call(count, put, take, tiles, inverse, factor, pieces):
    first_pass = factor is None
    slots = tiles.shape[0]
    width = pieces[0].shape[-1]
    rows = 2 * BLK + (8 if first_pass else 0)
    extra = [] if first_pass else [factor]
    out = jax.ShapeDtypeStruct((4, rows, width), F32)
    scratch = [pltpu.VMEM((32, 2 * BLK, width), BF16), pltpu.VMEM((8 * rows, width), F32)]
    if first_pass:
        scratch.append(pltpu.VMEM((16, BLK, BLK), F32))
    return pl.pallas_call(
        functools.partial(forward_kernel, first_pass),
        out_shape=(out, out),
        grid_spec=pltpu.PrefetchScalarGridSpec(
            num_scalar_prefetch=3,
            grid=(slots // CHUNK,),
            in_specs=[pl.BlockSpec((CHUNK, BLK, BLK), chunk_map)]
            + [whole(a.shape) for a in [inverse] + extra + list(pieces)],
            out_specs=(whole(out.shape), whole(out.shape)),
            scratch_shapes=scratch,
        ),
        cost_estimate=pl.CostEstimate(
            flops=6 * 2**30, bytes_accessed=2**24, transcendentals=0
        ),
    )(count, put, take, tiles, inverse, *extra, *pieces)


def backward_kernel(*refs):
    count_ref, put_ref, take_ref, tiles_ref = refs[:4]
    pieces, outs, (source, total) = refs[4:12], refs[12:20], refs[20:]
    step = pl.program_id(0)
    count = count_ref[0]
    first = step * CHUNK

    @pl.when(step == 0)
    def _():
        total[...] = jnp.zeros_like(total)
        for number, piece in enumerate(pieces):
            for part in range(2):
                put_source(source, number * 2 + part, piece[part * BLK : (part + 1) * BLK])

    @pl.when(first < count)
    def _():
        apply_loop(count, first, put_ref, take_ref, tiles_ref, source, total, True, None, None)

    @pl.when(step == pl.num_programs(0) - 1)
    def _():
        for number, out in enumerate(outs):
            for part in RING:
                start = (number * 4 + part) * BLK
                out[part] = total[start : start + BLK, :]


def backward_call(count, put, take, tiles, pieces):
    slots = tiles.shape[0]
    width = pieces[0].shape[-1]
    out = jax.ShapeDtypeStruct((4, BLK, width), F32)
    return pl.pallas_call(
        backward_kernel,
        out_shape=(out,) * 8,
        grid_spec=pltpu.PrefetchScalarGridSpec(
            num_scalar_prefetch=3,
            grid=(slots // CHUNK,),
            in_specs=[pl.BlockSpec((CHUNK, BLK, BLK), chunk_map)]
            + [whole(a.shape) for a in pieces],
            out_specs=(whole(out.shape),) * 8,
            scratch_shapes=[
                pltpu.VMEM((16, 2 * BLK, width), BF16),
                pltpu.VMEM((32 * BLK, width), F32),
            ],
        ),
        cost_estimate=pl.CostEstimate(
            flops=6 * 2**30, bytes_accessed=2**24, transcendentals=0
        ),
    )(count, put, take, tiles, *pieces)


PANEL = 32


def inverse_factor_kernel(gram_ref, out_ref, work):
    size = gram_ref.shape[0]
    work[:, :size] = gram_ref[...]
    row_at = lax.broadcasted_iota(jnp.int32, (size, size), 0)
    lane_at = lax.broadcasted_iota(jnp.int32, (size, size), 1)
    work[:, size:] = (row_at == lane_at).astype(F32)
    rows = lax.broadcasted_iota(jnp.int32, (PANEL, 1), 0)
    rows_small = lax.broadcasted_iota(jnp.int32, (PANEL, PANEL), 0)
    lanes_small = lax.broadcasted_iota(jnp.int32, (PANEL, PANEL), 1)
    unit = (rows_small == lanes_small).astype(F32)
    for start in range(0, size, PANEL):
        end = start + PANEL
        pair = jnp.concatenate([work[start:end, start:end], unit], axis=1)
        for j in range(PANEL - 1):
            row = pair[j : j + 1, :] / pair[j : j + 1, j : j + 1]
            pair = pair - jnp.where(rows > j, pair[:, j : j + 1], 0.0) * row
        pivots = jnp.sum(pair[:, :PANEL] * unit, axis=1, keepdims=True)
        corner = pair[:, PANEL:] * (1.0 / jnp.sqrt(pivots))
        panel = jnp.dot(corner, work[start:end, :], precision=HIGHEST, preferred_element_type=F32)
        work[start:end, :] = panel
        if end < size:
            update = lax.dot_general(
                panel[:, :size],
                panel,
                (((0,), (0,)), ((), ())),
                precision=HIGHEST,
                preferred_element_type=F32,
            )
            work[end:, :] -= update[end:, :]
    out_ref[...] = work[:, size:]


def inverse_factor(gram):
    size = gram.shape[0]
    return pl.pallas_call(
        inverse_factor_kernel,
        out_shape=jax.ShapeDtypeStruct((size, size), F32),
        in_specs=[pl.BlockSpec(memory_space=pltpu.VMEM)],
        out_specs=pl.BlockSpec(memory_space=pltpu.VMEM),
        scratch_shapes=[pltpu.VMEM((size, 2 * size), F32)],
        cost_estimate=pl.CostEstimate(flops=2**34, bytes_accessed=2**19, transcendentals=0),
    )(gram)


def gather_row(first, second):
    first = jnp.stack(ring_all(first, "x"))
    second = jnp.stack(ring_all(second, "y"))
    return ring_all(first, "y") + ring_all(second, "x")


def scatter_row(outs):
    first, second = outs[:4], outs[4:]
    first_in = [first[0]] + [shift(first[k], "x", k) for k in (1, 2, 3)]
    second_in = [second[0]] + [shift(second[k], "y", k) for k in (1, 2, 3)]

    def add(parts, i):
        return (parts[0][i] + parts[1][i]) + (parts[2][i] + parts[3][i])

    one = ring_scatter([add(first_in, i) for i in RING], "y")
    two = ring_scatter([add(second_in, i) for i in RING], "x")
    return jnp.concatenate([one, two], axis=0)


def gram_sum(gram):
    half = gram.shape[0] // 2
    core = lax.axis_index("c")
    kept = lax.dynamic_slice_in_dim(gram, core * half, half, 0)
    sent = lax.dynamic_slice_in_dim(gram, (1 - core) * half, half, 0)
    value = kept + swap(sent)
    for axis in "xyz":
        value = ring_sum(value, axis)
    other = swap(value)
    return jnp.where(
        core == 0, jnp.concatenate([value, other]), jnp.concatenate([other, value])
    )


def local(trial_vectors, tiles, tile_rows, tile_cols, tile_count):
    x, y, z, core = [lax.axis_index(a) for a in ("x", "y", "z", "c")]
    slots = tiles.shape[2]
    width = trial_vectors.shape[1]
    tiles = tiles.reshape(slots, BLK, BLK)
    count = tile_count.reshape(1)

    row = tile_rows.reshape(slots)
    col = tile_cols.reshape(slots)
    row_other = ((row // 2) % 2) ^ core
    row_z, row_part = row // 4, row % 2
    put_forward = (row_other * 4 + (row_z - z) % 4) * 2 + row_part
    take_backward = (row_other * 4 + (z - row_z) % 4) * 2 + row_part
    col_x, col_y, col_part = col // 8, (col // 2) % 4, col % 2
    back_x, back_y = (x - col_x) % 4, (y - col_y) % 4
    take_forward = jnp.where(col_part == 0, back_y * 4 + back_x, 16 + back_x * 4 + back_y)
    to_x, to_y = (col_x - x) % 4, (col_y - y) % 4
    put_backward = BLK * jnp.where(col_part == 0, to_x * 4 + to_y, 16 + to_y * 4 + to_x)
    put_first = jnp.concatenate(
        [(put_forward // 2) * (2 * BLK + 8) + (put_forward % 2) * BLK, put_forward]
    )
    put_later = put_forward * BLK

    pieces = gather_row(trial_vectors[:BLK], trial_vectors[BLK:])

    sums = rowsum_call(count, put_forward, tiles, 16)
    sums = (sums[:8] + swap(sums[8:])).reshape(4, 2, BLK)
    inverse_own = 1.0 / (1.0 + ring_scatter(list(sums), "z"))
    gathered = jnp.stack(ring_all(jnp.stack(ring_all(inverse_own, "x")), "y"))
    inverse = jnp.concatenate(
        [gathered[:, :, 0].reshape(16, BLK), gathered[:, :, 1].swapaxes(0, 1).reshape(16, BLK)]
    )
    inverse_own = inverse_own.reshape(2 * BLK, 1)

    vectors = trial_vectors
    factor = None
    scale = None
    for iteration in range(ITERS):
        keep, send = forward_call(
            count,
            put_first if iteration == 0 else put_later,
            take_forward,
            tiles,
            inverse,
            factor,
            pieces,
        )
        summed = ring_scatter(list(keep + swap(send)), "z")
        if iteration == 0:
            tilde = inverse_own * (inverse_own + summed[2 * BLK].reshape(2 * BLK, 1))
            scale = inverse_own / tilde
            summed = summed[: 2 * BLK]
        weighted = scale * (scale * (summed + inverse_own * vectors))
        mine = ring_all(weighted, "z")
        outs = backward_call(
            count, put_backward, take_backward, tiles, mine + [swap(v) for v in mine]
        )
        reduced = inverse_own * (scatter_row(outs) + weighted)
        gram = lax.dot_general(
            reduced,
            reduced,
            (((0,), (0,)), ((), ())),
            precision=HIGHEST,
            preferred_element_type=F32,
        )
        if iteration + 1 < ITERS:
            pieces = gather_row(reduced[:BLK], reduced[BLK:])
        factor = inverse_factor(gram_sum(gram))
        vectors = nt_dot(reduced, factor)
    total_nodes = 2 * BLK * 128
    return vectors * math.sqrt(total_nodes)


def solution(mesh):
    fine = Mesh(mesh.devices.reshape(4, 4, 4, 2), ("x", "y", "z", "c"))
    row, column = ("x", "y"), ("z", "c")
    in_specs = (
        P(row + column, None),
        P(row, column, None, None, None),
        P(row, column, None),
        P(row, column, None),
        P(row, column),
    )
    return jax.shard_map(
        local, mesh=fine, in_specs=in_specs, out_specs=P(row + column, None), check_vma=False
    )
```

time: 1170 us -> 490 us (0.42)
  waiting for transfers between devices: 734 us -> 170 us
  starting transfers between devices: 0.78 us -> 146 us
  blocking collectives: 140 us -> 0 us
  Pallas kernels: 0 us -> 139 us
  other arithmetic: 136 us -> 15.6 us
  matrix products: 69.8 us -> 3.8 us
  local copies, waits for them, and re-layouts: 62.4 us -> 4.01 us
  between operations: 17.5 us -> 1.8 us
    reduce_scatter x4 -> x0, waiting for transfers between devices: 347 us -> none  [the longest x2 265 us: local(): reduced = lax.psum_scatter(backward, 'row', scatter_dimension=0, tiled=True)]
    psum x2 -> x0, waiting for transfers between devices: 290 us -> none  [local(): gram_matrix = lax.psum(local_gram, ('row', 'col'))]
    ppermute x0 -> x102, waiting for transfers between devices: none -> 170 us  [the longest x87 159 us: shift(): return lax.ppermute(value, axis, [(i, (i + amount) % 4) for i in RING])]
    ppermute x0 -> x102, starting transfers between devices: none -> 146 us  [the longest x87 118 us: shift(): return lax.ppermute(value, axis, [(i, (i + amount) % 4) for i in RING])]
    pallas_call x0 -> x7, Pallas kernels: none -> 139 us  [the longest x2 58.3 us: inverse_factor(): pl.pallas_call(inverse_factor_kernel, out_shape=jax.ShapeDtypeStruct((siz...]
    psum x2 -> x0, blocking collectives: 121 us -> none  [the longest x1 82.7 us: local(): tilde_slab = inverse_slab * (inverse_slab + lax.psum(tilde_part, 'col'))]
    another operation x19 -> x7, other arithmetic: 108 us -> 0.16 us  [the longest x2 0.07 us: gather_row(): second = jnp.stack(ring_all(second, 'y'))]
    all_gather x4 -> x0, waiting for transfers between devices: 96 us -> none  [the longest x1 48.9 us: local(): gathered = lax.all_gather(vectors, 'row', axis=0, tiled=True)]
  transfers between devices with their start and end apart: 10 -> 102, of which waited for: 8 -> 52; matrix products, arithmetic and copies ran while one was open for 2% -> 2% of each run, Pallas kernels for 0% -> 6%
where the time goes in v1:
time: 490 us; the launch traced here: 480 us
  waiting for transfers between devices  170 us (35%)
  starting transfers between devices  146 us (30%)
  Pallas kernels  139 us (28%)
  other arithmetic  15.6 us (3%)
    ppermute x87, waiting for transfers between devices, shift(): return lax.ppermute(value, axis, [(i, (i + amount) % 4) for i in RING])  159 us
    ppermute x87, starting transfers between devices, shift(): return lax.ppermute(value, axis, [(i, (i + amount) % 4) for i in RING])  118 us
    pallas_call x2, Pallas kernels, inverse_factor(): pl.pallas_call(inverse_factor_kernel, out_shape=jax.ShapeDtypeStruct((siz...  58.3 us
    pallas_call x2, Pallas kernels, forward_call(): pl.pallas_call(functools.partial(forward_kernel, first_pass), out_shape=(...  36.5 us
    pallas_call x2, Pallas kernels, backward_call(): pl.pallas_call(backward_kernel, out_shape=(out,) * 8, grid_spec=pltpu.Pre...  34.6 us
    ppermute x15, starting transfers between devices, swap(): return lax.ppermute(value, 'c', [(0, 1), (1, 0)])  27.7 us
    ppermute x15, waiting for transfers between devices, swap(): return lax.ppermute(value, 'c', [(0, 1), (1, 0)])  11 us
  transfers between devices with their start and end apart: 102, of which 52 were waited for; matrix products, arithmetic and copies ran while one was open for 2% of the time, Pallas kernels for 6%

profile of v1, /device:TPU:1, one launch (start us, length us, event | category | flops | bytes accessed | tf_op | source)
XLA Modules:
  0.0 480.4 jit_solution(16950843471022347657)
XLA Ops:
  3.1 9.5 %shard_map.55 = f32[16,128]{1,0:T(8,128)} custom-call(s32[1]{0:T(128)} %bitcast.183.count_ref, s32[128]{0:T(128)} %get-tuple-element.52.put_ref, f32[128,128,128]{2,1,0:T(8,128)} %bitcast.188), custom_call_target="tpu_custom_call" | custom-call | flops 1000000 | bytes 8388608 | tf_op jit(solution)/shard_map/pallas_call | solution.py:94
  13.3 4.3 collective-permute-start.11
  28.9 2.7 collective-permute-start.6
  31.6 2.9 collective-permute-start.5
  37.9 2.0 collective-permute-done.4
  39.9 2.4 collective-permute-start.8
  45.0 3.8 collective-permute-done.12
  51.6 2.9 collective-permute-start.15
  56.4 4.5 collective-permute-done.20.refs_11_
  60.9 14.5 %collective-permute-done.19.refs_10_ = f32[4,128,256]{2,1,0:T(8,128)S(1)} collective-permute-done((f32[4,128,256]{2,1,0:T(8,128)S(1)}, f32[4,128,256]{2,1,0:T(8,128)S(1)}, u32[]{:S(2)}, u32[]{:S(2)}) %collective-permute-start.19) | collective-permute-done | bytes 524320 | tf_op jit(solution)/shard_map/ppermute | solution.py:22
  75.4 5.7 %collective-permute-done.13.refs_6_ = f32[4,128,256]{2,1,0:T(8,128)S(1)} collective-permute-done((f32[4,128,256]{2,1,0:T(8,128)S(1)}, f32[4,128,256]{2,1,0:T(8,128)S(1)}, u32[]{:S(2)}, u32[]{:S(2)}) %collective-permute-start.13) | collective-permute-done | bytes 524320 | tf_op jit(solution)/shard_map/ppermute | solution.py:22
  82.0 17.6 %shard_map.56 = (f32[4,264,256]{2,1,0:T(8,128)}, f32[4,264,256]{2,1,0:T(8,128)}) custom-call(s32[1]{0:T(128)} %bitcast.184.refs_0_, s32[256]{0:T(256)} %pad_add_fusion.refs_1_, s32[128]{0:T(128)} %compare_select_fusion.19.refs_2_, f32[128,128,128]{2,1,0:T(8,128)} %bitcast.189, f32[32,128]{1,0:T(8,128)} %pad_maximum_fusion.5.refs_4_, ...), custom_call_target="tpu_custom_call" | custom-call | flops 6442450944 | bytes 16777216 | tf_op jit(solution)/shard_map/pallas_call | solution.py:204
  99.6 2.9 collective-permute-done.22
  106.4 5.9 %collective-permute-done.25 = f32[264,256]{1,0:T(8,128)S(1)} collective-permute-done((f32[264,256]{1,0:T(8,128)S(1)}, f32[264,256]{1,0:T(8,128)S(1)}, u32[]{:S(2)}, u32[]{:S(2)}) %collective-permute-start.25) | collective-permute-done | bytes 270368 | tf_op jit(solution)/shard_map/ppermute | solution.py:22
  113.9 6.2 %collective-permute-done.23 = f32[264,256]{1,0:T(8,128)S(1)} collective-permute-done((f32[264,256]{1,0:T(8,128)S(1)}, f32[264,256]{1,0:T(8,128)S(1)}, u32[]{:S(2)}, u32[]{:S(2)}) %collective-permute-start.23) | collective-permute-done | bytes 270368 | tf_op jit(solution)/shard_map/ppermute | solution.py:22
  123.8 4.0 collective-permute-done.28.refs_7_
  127.8 2.3 collective-permute-start.32
  130.1 2.7 collective-permute-start.31
  132.8 3.3 collective-permute-done.26.refs_5_
  138.5 17.3 %shard_map.57 = (f32[4,128,256]{2,1,0:T(8,128)}, f32[4,128,256]{2,1,0:T(8,128)}, f32[4,128,256]{2,1,0:T(8,128)}, f32[4,128,256]{2,1,0:T(8,128)}, f32[4,128,256]{...) custom-call(s32[1]{0:T(128)} %bitcast.185.refs_0_, ...), custom_call_target="tpu_custom_call" | custom-call | flops 6442450944 | bytes 16777216 | tf_op jit(solution)/shard_map/pallas_call | solution.py:251
  156.7 2.0 collective-permute-start.35
  159.6 7.1 %collective-permute-done.33 = f32[4,128,256]{2,1,0:T(8,128)S(1)} collective-permute-done((f32[4,128,256]{2,1,0:T(8,128)}, f32[4,128,256]{2,1,0:T(8,128)S(1)}, u32[]{:S(2)}, u32[]{:S(2)}) %collective-permute-start.33) | collective-permute-done | bytes 524320 | tf_op jit(solution)/shard_map/ppermute | solution.py:22
  167.3 12.7 %collective-permute-done.34 = f32[4,128,256]{2,1,0:T(8,128)S(1)} collective-permute-done((f32[4,128,256]{2,1,0:T(8,128)}, f32[4,128,256]{2,1,0:T(8,128)S(1)}, u32[]{:S(2)}, u32[]{:S(2)}) %collective-permute-start.34) | collective-permute-done | bytes 524320 | tf_op jit(solution)/shard_map/ppermute | solution.py:22
  186.5 3.2 collective-permute-start.43
  195.5 6.3 %collective-permute-start.45 = (f32[128,256]{1,0:T(8,128)S(1)}, f32[128,256]{1,0:T(8,128)S(1)}, u32[]{:S(2)}, u32[]{:S(2)}) collective-permute-start(f32[128,256]{1,0:T(8,128)S(1)} %constant_dynamic-slice_fusion.1), channel_id=1, source_target_pairs={{0,1},{1,0},{2,3},{3,2},{4,5},{5,4},{6,7},{7,6},{8,9},{9,8},{10,11... | collective-permute-start | bytes 393224 | tf_op jit(solution)/shard_map/ppermute | solution.py:26
  205.2 2.4 collective-permute-done.48
  209.3 3.6 collective-permute-done.46
  213.0 5.2 %collective-permute-start.50 = (f32[128,256]{1,0:T(8,128)S(1)}, f32[128,256]{1,0:T(8,128)S(1)}, u32[]{:S(2)}, u32[]{:S(2)}) collective-permute-start(f32[128,256]{1,0:T(8,128)S(1)} %add_add_fusion.5), channel_id=1, source_target_pairs={{0,16},{8,24},{16,0},{24,8},{1,17},{9,25},{17,1},{25,9},{2,18},{10... | collective-permute-start | bytes 393224 | tf_op jit(solution)/shard_map/ppermute | solution.py:22
  219.9 2.7 collective-permute-start.58
  224.3 4.4 collective-permute-start.54
  230.2 3.6 collective-permute-done.54
  234.1 3.3 collective-permute-done.52
  243.0 5.7 %collective-permute-done.61.refs_9_ = f32[4,128,256]{2,1,0:T(8,128)S(1)} collective-permute-done((f32[4,128,256]{2,1,0:T(8,128)S(1)}, f32[4,128,256]{2,1,0:T(8,128)S(1)}, u32[]{:S(2)}, u32[]{:S(2)}) %collective-permute-start.61) | collective-permute-done | bytes 524320 | tf_op jit(solution)/shard_map/ppermute | solution.py:22
  248.9 29.2 %shard_map.58.refs_5_ = f32[256,256]{1,0:T(8,128)} custom-call(f32[256,256]{1,0:T(8,128)} %maximum_select_fusion.gram_ref), custom_call_target="tpu_custom_call" | custom-call | flops 17179869184 | bytes 524288 | tf_op jit(solution)/shard_map/pallas_call | solution.py:308
  278.9 19.0 %shard_map.59 = (f32[4,256,256]{2,1,0:T(8,128)}, f32[4,256,256]{2,1,0:T(8,128)}) custom-call(s32[1]{0:T(128)} %bitcast.186.refs_0_, s32[128]{0:T(128)} %broadcast_multiply_fusion.refs_1_, s32[128]{0:T(128)} %compare_select_fusion.19.refs_2_, f32[128,128,128]{2,1,0:T(8,128)} %bitcast.191, f32[32,128]{1,0:T(8,128)} %pad_maximum_fusion.5.refs_4_, ...), custom_call_target="tpu_custom_call" | custom-call | flops 6442450944 | bytes 16777216 | tf_op jit(solution)/shard_map/pallas_call | solution.py:204
  297.9 2.9 collective-permute-done.68
  302.3 13.4 %collective-permute-start.70 = (f32[256,256]{1,0:T(8,128)S(1)}, f32[256,256]{1,0:T(8,128)S(1)}, u32[]{:S(2)}, u32[]{:S(2)}) collective-permute-start(f32[256,256]{1,0:T(8,128)S(1)} %get-tuple-element.69), channel_id=1, source_target_pairs={{0,4},{2,6},{4,0},{6,2},{1,5},{3,7},{5,1},{7,3},{8,12},{10,14},{12... | collective-permute-start | bytes 786440 | tf_op jit(solution)/shard_map/ppermute | solution.py:22
  316.5 5.7 %collective-permute-done.70 = f32[256,256]{1,0:T(8,128)S(1)} collective-permute-done((f32[256,256]{1,0:T(8,128)S(1)}, f32[256,256]{1,0:T(8,128)S(1)}, u32[]{:S(2)}, u32[]{:S(2)}) %collective-permute-start.70) | collective-permute-done | bytes 262176 | tf_op jit(solution)/shard_map/ppermute | solution.py:22
  322.2 6.0 %collective-permute-done.69 = f32[256,256]{1,0:T(8,128)S(1)} collective-permute-done((f32[256,256]{1,0:T(8,128)S(1)}, f32[256,256]{1,0:T(8,128)S(1)}, u32[]{:S(2)}, u32[]{:S(2)}) %collective-permute-start.69) | collective-permute-done | bytes 262176 | tf_op jit(solution)/shard_map/ppermute | solution.py:22
  328.7 2.6 collective-permute-start.73
  333.4 2.7 collective-permute-done.74.refs_7_
  336.0 2.3 collective-permute-start.78
  338.3 2.2 collective-permute-start.77
  340.5 3.5 collective-permute-done.72.refs_5_
  346.5 17.3 %shard_map.60 = (f32[4,128,256]{2,1,0:T(8,128)}, f32[4,128,256]{2,1,0:T(8,128)}, f32[4,128,256]{2,1,0:T(8,128)}, f32[4,128,256]{2,1,0:T(8,128)}, f32[4,128,256]{...) custom-call(s32[1]{0:T(128)} %bitcast.187.refs_0_, ...), custom_call_target="tpu_custom_call" | custom-call | flops 6442450944 | bytes 16777216 | tf_op jit(solution)/shard_map/pallas_call | solution.py:251
  363.8 2.9 collective-permute-start.80
  366.7 2.0 collective-permute-start.81
  368.7 4.9 %collective-permute-start.86 = (f32[4,128,256]{2,1,0:T(8,128)}, f32[4,128,256]{2,1,0:T(8,128)S(1)}, u32[]{:S(2)}, u32[]{:S(2)}) collective-permute-start(f32[4,128,256]{2,1,0:T(8,128)} %get-tuple-element.43), channel_id=1, source_target_pairs={{0,16},{8,24},{16,0},{24,8},{1,17},{9,25},{17,1},{25,9},{2,18},{10... | collective-permute-start | bytes 1572872 | tf_op jit(solution)/shard_map/ppermute | solution.py:22
  373.6 2.3 collective-permute-done.79
  375.9 5.3 %collective-permute-start.87 = (f32[4,128,256]{2,1,0:T(8,128)}, f32[4,128,256]{2,1,0:T(8,128)S(1)}, u32[]{:S(2)}, u32[]{:S(2)}) collective-permute-start(f32[4,128,256]{2,1,0:T(8,128)} %get-tuple-element.44), channel_id=1, source_target_pairs={{0,24},{8,0},{16,8},{24,16},{1,25},{9,1},{17,9},{25,17},{2,26},{10... | collective-permute-start | bytes 1572872 | tf_op jit(solution)/shard_map/ppermute | solution.py:22
  381.2 8.8 %collective-permute-done.80 = f32[4,128,256]{2,1,0:T(8,128)S(1)} collective-permute-done((f32[4,128,256]{2,1,0:T(8,128)}, f32[4,128,256]{2,1,0:T(8,128)S(1)}, u32[]{:S(2)}, u32[]{:S(2)}) %collective-permute-start.80) | collective-permute-done | bytes 524320 | tf_op jit(solution)/shard_map/ppermute | solution.py:22
  392.3 3.4 collective-permute-done.85
  397.7 6.2 %collective-permute-start.89 = (f32[128,256]{1,0:T(8,128)S(1)}, f32[128,256]{1,0:T(8,128)S(1)}, u32[]{:S(2)}, u32[]{:S(2)}) collective-permute-start(f32[128,256]{1,0:T(8,128)S(1)} %get-tuple-element.57), channel_id=1, source_target_pairs={{0,64},{32,96},{64,0},{96,32},{1,65},{33,97},{65,1},{97,33},{2,66}... | collective-permute-start | bytes 393224 | tf_op jit(solution)/shard_map/ppermute | solution.py:22
  406.3 3.0 collective-permute-done.88
  410.0 5.0 %collective-permute-start.91 = (f32[128,256]{1,0:T(8,128)S(1)}, f32[128,256]{1,0:T(8,128)S(1)}, u32[]{:S(2)}, u32[]{:S(2)}) collective-permute-start(f32[128,256]{1,0:T(8,128)S(1)} %constant_dynamic-slice_fusion), channel_id=1, source_target_pairs={{0,1},{1,0},{2,3},{3,2},{4,5},{5,4},{6,7},{7,6},{8,9},{9,8},{10,11... | collective-permute-start | bytes 393224 | tf_op jit(solution)/shard_map/ppermute | solution.py:26
  418.4 2.4 collective-permute-done.94
  422.6 3.6 collective-permute-done.92
  427.2 1.9 collective-permute-start.96
  430.6 1.9 collective-permute-done.96
  432.5 3.7 collective-permute-done.95
  438.1 2.3 collective-permute-done.100
  442.1 3.5 collective-permute-done.98
  448.7 29.1 %shard_map.61 = f32[256,256]{1,0:T(8,128)} custom-call(f32[256,256]{1,0:T(8,128)} %maximum_select_fusion.1.gram_ref), custom_call_target="tpu_custom_call" | custom-call | flops 17179869184 | bytes 524288 | tf_op jit(solution)/shard_map/pallas_call | solution.py:308
  477.9 2.1 convolution_multiply_fusion
  (274 shorter events, 97.9 us)
Async XLA Ops:
  13.3 29.0 %collective-permute-start.11 = (f32[128,256]{1,0:T(8,128)S(1)}, f32[128,256]{1,0:T(8,128)S(1)}, u32[]{:S(2)}, u32[]{:S(2)}) collective-permute-start(f32[128,256]{1,0:T(8,128)S(1)} %get-tuple-element.77), channel_id=1, source_target_pairs={{0,64},{32,96},{64,0},{96,32},{1,65},{33,97},{65,1},{97,33},{2,66}... | collective-permute-start | bytes 393224 | tf_op jit(solution)/shard_map/ppermute | solution.py:22
  17.6 25.7 %collective-permute-start.10 = (f32[128,256]{1,0:T(8,128)S(1)}, f32[128,256]{1,0:T(8,128)S(1)}, u32[]{:S(2)}, u32[]{:S(2)}) collective-permute-start(f32[128,256]{1,0:T(8,128)S(1)} %get-tuple-element.77), channel_id=1, source_target_pairs={{0,32},{32,64},{64,96},{96,0},{1,33},{33,65},{65,97},{97,1},{2,34}... | collective-permute-start | bytes 393224 | tf_op jit(solution)/shard_map/ppermute | solution.py:22
  34.6 20.4 %collective-permute-start.21 = (f32[4,128,256]{2,1,0:T(8,128)S(1)}, f32[4,128,256]{2,1,0:T(8,128)S(1)}, u32[]{:S(2)}, u32[]{:S(2)}) collective-permute-start(f32[4,128,256]{2,1,0:T(8,128)S(1)} %pad_maximum_fusion.1.refs_9_), channel_id=1, source_target_pairs={{0,96},{32,0},{64,32},{96,64},{1,97},{33,1},{65,33},{97,65},{2,98}... | collective-permute-start | bytes 1572872 | tf_op jit(solution)/shard_map/ppermute | solution.py:22
  35.9 13.0 %collective-permute-start.12 = (f32[128,256]{1,0:T(8,128)S(1)}, f32[128,256]{1,0:T(8,128)S(1)}, u32[]{:S(2)}, u32[]{:S(2)}) collective-permute-start(f32[128,256]{1,0:T(8,128)S(1)} %get-tuple-element.77), channel_id=1, source_target_pairs={{0,96},{32,0},{64,32},{96,64},{1,97},{33,1},{65,33},{97,65},{2,98}... | collective-permute-start | bytes 393224 | tf_op jit(solution)/shard_map/ppermute | solution.py:22
  39.9 9.9 %collective-permute-start.8 = (f32[4,2,128]{2,1,0:T(2,128)S(1)}, f32[4,2,128]{2,1,0:T(2,128)S(1)}, u32[]{:S(2)}, u32[]{:S(2)}) collective-permute-start(f32[4,2,128]{2,1,0:T(2,128)S(1)} %pad_maximum_fusion.6), channel_id=1, source_target_pairs={{0,16},{8,24},{16,0},{24,8},{1,17},{9,25},{17,1},{25,9},{2,18},{10... | collective-permute-start | bytes 12296 | tf_op jit(solution)/shard_map/ppermute | solution.py:22
  42.4 9.3 %collective-permute-start.7 = (f32[4,2,128]{2,1,0:T(2,128)S(1)}, f32[4,2,128]{2,1,0:T(2,128)S(1)}, u32[]{:S(2)}, u32[]{:S(2)}) collective-permute-start(f32[4,2,128]{2,1,0:T(2,128)S(1)} %pad_maximum_fusion.6), channel_id=1, source_target_pairs={{0,8},{8,16},{16,24},{24,0},{1,9},{9,17},{17,25},{25,1},{2,10},{10... | collective-permute-start | bytes 12296 | tf_op jit(solution)/shard_map/ppermute | solution.py:22
  43.4 11.2 %collective-permute-start.9 = (f32[4,2,128]{2,1,0:T(2,128)S(1)}, f32[4,2,128]{2,1,0:T(2,128)S(1)}, u32[]{:S(2)}, u32[]{:S(2)}) collective-permute-start(f32[4,2,128]{2,1,0:T(2,128)S(1)} %pad_maximum_fusion.6), channel_id=1, source_target_pairs={{0,24},{8,0},{16,8},{24,16},{1,25},{9,1},{17,9},{25,17},{2,26},{10... | collective-permute-start | bytes 12296 | tf_op jit(solution)/shard_map/ppermute | solution.py:22
  48.8 12.0 %collective-permute-start.20 = (f32[4,128,256]{2,1,0:T(8,128)S(1)}, f32[4,128,256]{2,1,0:T(8,128)S(1)}, u32[]{:S(2)}, u32[]{:S(2)}) collective-permute-start(f32[4,128,256]{2,1,0:T(8,128)S(1)} %pad_maximum_fusion.1.refs_9_), channel_id=1, source_target_pairs={{0,64},{32,96},{64,0},{96,32},{1,65},{33,97},{65,1},{97,33},{2,66}... | collective-permute-start | bytes 1572872 | tf_op jit(solution)/shard_map/ppermute | solution.py:22
  49.9 25.6 %collective-permute-start.19 = (f32[4,128,256]{2,1,0:T(8,128)S(1)}, f32[4,128,256]{2,1,0:T(8,128)S(1)}, u32[]{:S(2)}, u32[]{:S(2)}) collective-permute-start(f32[4,128,256]{2,1,0:T(8,128)S(1)} %pad_maximum_fusion.1.refs_9_), channel_id=1, source_target_pairs={{0,32},{32,64},{64,96},{96,0},{1,33},{33,65},{65,97},{97,1},{2,34}... | collective-permute-start | bytes 1572872 | tf_op jit(solution)/shard_map/ppermute | solution.py:22
  51.6 23.8 %collective-permute-start.15 = (f32[4,128,256]{2,1,0:T(8,128)S(1)}, f32[4,128,256]{2,1,0:T(8,128)S(1)}, u32[]{:S(2)}, u32[]{:S(2)}) collective-permute-start(f32[4,128,256]{2,1,0:T(8,128)S(1)} %pad_maximum_fusion.refs_5_), channel_id=1, source_target_pairs={{0,24},{8,0},{16,8},{24,16},{1,25},{9,1},{17,9},{25,17},{2,26},{10... | collective-permute-start | bytes 1572872 | tf_op jit(solution)/shard_map/ppermute | solution.py:22
  54.6 20.9 %collective-permute-start.14 = (f32[4,128,256]{2,1,0:T(8,128)S(1)}, f32[4,128,256]{2,1,0:T(8,128)S(1)}, u32[]{:S(2)}, u32[]{:S(2)}) collective-permute-start(f32[4,128,256]{2,1,0:T(8,128)S(1)} %pad_maximum_fusion.refs_5_), channel_id=1, source_target_pairs={{0,16},{8,24},{16,0},{24,8},{1,17},{9,25},{17,1},{25,9},{2,18},{10... | collective-permute-start | bytes 1572872 | tf_op jit(solution)/shard_map/ppermute | solution.py:22
  55.0 26.1 %collective-permute-start.13 = (f32[4,128,256]{2,1,0:T(8,128)S(1)}, f32[4,128,256]{2,1,0:T(8,128)S(1)}, u32[]{:S(2)}, u32[]{:S(2)}) collective-permute-start(f32[4,128,256]{2,1,0:T(8,128)S(1)} %pad_maximum_fusion.refs_5_), channel_id=1, source_target_pairs={{0,8},{8,16},{16,24},{24,0},{1,9},{9,17},{17,25},{25,1},{2,10},{10... | collective-permute-start | bytes 1572872 | tf_op jit(solution)/shard_map/ppermute | solution.py:22
  103.9 8.4 %collective-permute-start.25 = (f32[264,256]{1,0:T(8,128)S(1)}, f32[264,256]{1,0:T(8,128)S(1)}, u32[]{:S(2)}, u32[]{:S(2)}) collective-permute-start(f32[264,256]{1,0:T(8,128)S(1)} %get-tuple-element.65), channel_id=1, source_target_pairs={{0,6},{2,0},{4,2},{6,4},{1,7},{3,1},{5,3},{7,5},{8,14},{10,8},{12,... | collective-permute-start | bytes 811016 | tf_op jit(solution)/shard_map/ppermute | solution.py:22
  104.3 9.6 %collective-permute-start.24 = (f32[264,256]{1,0:T(8,128)S(1)}, f32[264,256]{1,0:T(8,128)S(1)}, u32[]{:S(2)}, u32[]{:S(2)}) collective-permute-start(f32[264,256]{1,0:T(8,128)S(1)} %get-tuple-element.66), channel_id=1, source_target_pairs={{0,4},{2,6},{4,0},{6,2},{1,5},{3,7},{5,1},{7,3},{8,12},{10,14},{12... | collective-permute-start | bytes 811016 | tf_op jit(solution)/shard_map/ppermute | solution.py:22
  105.6 14.5 %collective-permute-start.23 = (f32[264,256]{1,0:T(8,128)S(1)}, f32[264,256]{1,0:T(8,128)S(1)}, u32[]{:S(2)}, u32[]{:S(2)}) collective-permute-start(f32[264,256]{1,0:T(8,128)S(1)} %get-tuple-element.67), channel_id=1, source_target_pairs={{0,2},{2,4},{4,6},{6,0},{1,3},{3,5},{5,7},{7,1},{8,10},{10,12},{12... | collective-permute-start | bytes 811016 | tf_op jit(solution)/shard_map/ppermute | solution.py:22
  120.3 7.5 %collective-permute-start.28 = (f32[256,256]{1,0:T(8,128)S(1)}, f32[256,256]{1,0:T(8,128)S(1)}, u32[]{:S(2)}, u32[]{:S(2)}) collective-permute-start(f32[256,256]{1,0:T(8,128)S(1)} %fusion.8.refs_4_), channel_id=1, source_target_pairs={{0,6},{2,0},{4,2},{6,4},{1,7},{3,1},{5,3},{7,5},{8,14},{10,8},{12,... | collective-permute-start | bytes 786440 | tf_op jit(solution)/shard_map/ppermute | solution.py:22
  120.8 9.3 %collective-permute-start.27 = (f32[256,256]{1,0:T(8,128)S(1)}, f32[256,256]{1,0:T(8,128)S(1)}, u32[]{:S(2)}, u32[]{:S(2)}) collective-permute-start(f32[256,256]{1,0:T(8,128)S(1)} %fusion.8.refs_4_), channel_id=1, source_target_pairs={{0,4},{2,6},{4,0},{6,2},{1,5},{3,7},{5,1},{7,3},{8,12},{10,14},{12... | collective-permute-start | bytes 786440 | tf_op jit(solution)/shard_map/ppermute | solution.py:22
  121.7 14.4 %collective-permute-start.26 = (f32[256,256]{1,0:T(8,128)S(1)}, f32[256,256]{1,0:T(8,128)S(1)}, u32[]{:S(2)}, u32[]{:S(2)}) collective-permute-start(f32[256,256]{1,0:T(8,128)S(1)} %fusion.8.refs_4_), channel_id=1, source_target_pairs={{0,2},{2,4},{4,6},{6,0},{1,3},{3,5},{5,7},{7,1},{8,10},{10,12},{12... | collective-permute-start | bytes 786440 | tf_op jit(solution)/shard_map/ppermute | solution.py:22
  122.5 14.1 %collective-permute-start.29 = (f32[256,256]{1,0:T(8,128)S(1)}, f32[256,256]{1,0:T(8,128)S(1)}, u32[]{:S(2)}, u32[]{:S(2)}) collective-permute-start(f32[256,256]{1,0:T(8,128)S(1)} %fusion.8.refs_4_), channel_id=1, source_target_pairs={{0,1},{1,0},{2,3},{3,2},{4,5},{5,4},{6,7},{7,6},{8,9},{9,8},{10,11... | collective-permute-start | bytes 786440 | tf_op jit(solution)/shard_map/ppermute | solution.py:26
  127.8 8.8 %collective-permute-start.32 = (f32[256,256]{1,0:T(8,128)S(1)}, f32[256,256]{1,0:T(8,128)S(1)}, u32[]{:S(2)}, u32[]{:S(2)}) collective-permute-start(f32[256,256]{1,0:T(8,128)S(1)} %collective-permute-done.28.refs_7_), channel_id=1, source_target_pairs={{0,1},{1,0},{2,3},{3,2},{4,5},{5,4},{6,7},{7,6},{8,9},{9,8},{10,11... | collective-permute-start | bytes 786440 | tf_op jit(solution)/shard_map/ppermute | solution.py:26
  155.8 10.9 %collective-permute-start.33 = (f32[4,128,256]{2,1,0:T(8,128)}, f32[4,128,256]{2,1,0:T(8,128)S(1)}, u32[]{:S(2)}, u32[]{:S(2)}) collective-permute-start(f32[4,128,256]{2,1,0:T(8,128)} %get-tuple-element.28), channel_id=1, source_target_pairs={{0,32},{32,64},{64,96},{96,0},{1,33},{33,65},{65,97},{97,1},{2,34}... | collective-permute-start | bytes 1572872 | tf_op jit(solution)/shard_map/ppermute | solution.py:22
  155.9 24.1 %collective-permute-start.34 = (f32[4,128,256]{2,1,0:T(8,128)}, f32[4,128,256]{2,1,0:T(8,128)S(1)}, u32[]{:S(2)}, u32[]{:S(2)}) collective-permute-start(f32[4,128,256]{2,1,0:T(8,128)} %get-tuple-element.29), channel_id=1, source_target_pairs={{0,64},{32,96},{64,0},{96,32},{1,65},{33,97},{65,1},{97,33},{2,66}... | collective-permute-start | bytes 1572872 | tf_op jit(solution)/shard_map/ppermute | solution.py:22
  156.7 24.4 %collective-permute-start.35 = (f32[4,128,256]{2,1,0:T(8,128)}, f32[4,128,256]{2,1,0:T(8,128)}, u32[]{:S(2)}, u32[]{:S(2)}) collective-permute-start(f32[4,128,256]{2,1,0:T(8,128)} %get-tuple-element.30), channel_id=1, source_target_pairs={{0,96},{32,0},{64,32},{96,64},{1,97},{33,1},{65,33},{97,65},{2,98}... | collective-permute-start | bytes 1572872 | tf_op jit(solution)/shard_map/ppermute | solution.py:22
  158.6 24.9 %collective-permute-start.39 = (f32[4,128,256]{2,1,0:T(8,128)}, f32[4,128,256]{2,1,0:T(8,128)S(1)}, u32[]{:S(2)}, u32[]{:S(2)}) collective-permute-start(f32[4,128,256]{2,1,0:T(8,128)} %get-tuple-element.32), channel_id=1, source_target_pairs={{0,8},{8,16},{16,24},{24,0},{1,9},{9,17},{17,25},{25,1},{2,10},{10... | collective-permute-start | bytes 1572872 | tf_op jit(solution)/shard_map/ppermute | solution.py:22
  158.6 25.3 %collective-permute-start.40 = (f32[4,128,256]{2,1,0:T(8,128)}, f32[4,128,256]{2,1,0:T(8,128)S(1)}, u32[]{:S(2)}, u32[]{:S(2)}) collective-permute-start(f32[4,128,256]{2,1,0:T(8,128)} %get-tuple-element.33), channel_id=1, source_target_pairs={{0,16},{8,24},{16,0},{24,8},{1,17},{9,25},{17,1},{25,9},{2,18},{10... | collective-permute-start | bytes 1572872 | tf_op jit(solution)/shard_map/ppermute | solution.py:22
  166.7 18.1 %collective-permute-start.41 = (f32[4,128,256]{2,1,0:T(8,128)}, f32[4,128,256]{2,1,0:T(8,128)S(1)}, u32[]{:S(2)}, u32[]{:S(2)}) collective-permute-start(f32[4,128,256]{2,1,0:T(8,128)} %get-tuple-element.34), channel_id=1, source_target_pairs={{0,24},{8,0},{16,8},{24,16},{1,25},{9,1},{17,9},{25,17},{2,26},{10... | collective-permute-start | bytes 1572872 | tf_op jit(solution)/shard_map/ppermute | solution.py:22
  182.5 8.0 %collective-permute-start.37 = (f32[128,256]{1,0:T(8,128)S(1)}, f32[128,256]{1,0:T(8,128)S(1)}, u32[]{:S(2)}, u32[]{:S(2)}) collective-permute-start(f32[128,256]{1,0:T(8,128)S(1)} %get-tuple-element.60), channel_id=1, source_target_pairs={{0,16},{8,24},{16,0},{24,8},{1,17},{9,25},{17,1},{25,9},{2,18},{10... | collective-permute-start | bytes 393224 | tf_op jit(solution)/shard_map/ppermute | solution.py:22
  183.5 8.3 %collective-permute-start.36 = (f32[128,256]{1,0:T(8,128)S(1)}, f32[128,256]{1,0:T(8,128)S(1)}, u32[]{:S(2)}, u32[]{:S(2)}) collective-permute-start(f32[128,256]{1,0:T(8,128)S(1)} %get-tuple-element.61), channel_id=1, source_target_pairs={{0,8},{8,16},{16,24},{24,0},{1,9},{9,17},{17,25},{25,1},{2,10},{10... | collective-permute-start | bytes 393224 | tf_op jit(solution)/shard_map/ppermute | solution.py:22
  184.9 8.0 %collective-permute-start.44 = (f32[128,256]{1,0:T(8,128)S(1)}, f32[128,256]{1,0:T(8,128)S(1)}, u32[]{:S(2)}, u32[]{:S(2)}) collective-permute-start(f32[128,256]{1,0:T(8,128)S(1)} %get-tuple-element.62), channel_id=1, source_target_pairs={{0,96},{32,0},{64,32},{96,64},{1,97},{33,1},{65,33},{97,65},{2,98}... | collective-permute-start | bytes 393224 | tf_op jit(solution)/shard_map/ppermute | solution.py:22
  204.6 8.3 %collective-permute-start.46 = (f32[128,256]{1,0:T(8,128)S(1)}, f32[128,256]{1,0:T(8,128)S(1)}, u32[]{:S(2)}, u32[]{:S(2)}) collective-permute-start(f32[128,256]{1,0:T(8,128)S(1)} %dynamic-slice_add_fusion.1), channel_id=1, source_target_pairs={{0,32},{32,64},{64,96},{96,0},{1,33},{33,65},{65,97},{97,1},{2,34}... | collective-permute-start | bytes 393224 | tf_op jit(solution)/shard_map/ppermute | solution.py:22
  213.0 9.5 %collective-permute-start.50 = (f32[128,256]{1,0:T(8,128)S(1)}, f32[128,256]{1,0:T(8,128)S(1)}, u32[]{:S(2)}, u32[]{:S(2)}) collective-permute-start(f32[128,256]{1,0:T(8,128)S(1)} %add_add_fusion.5), channel_id=1, source_target_pairs={{0,16},{8,24},{16,0},{24,8},{1,17},{9,25},{17,1},{25,9},{2,18},{10... | collective-permute-start | bytes 393224 | tf_op jit(solution)/shard_map/ppermute | solution.py:22
  218.3 10.4 %collective-permute-start.57 = (f32[128,256]{1,0:T(8,128)S(1)}, f32[128,256]{1,0:T(8,128)S(1)}, u32[]{:S(2)}, u32[]{:S(2)}) collective-permute-start(f32[128,256]{1,0:T(8,128)S(1)} %get-tuple-element.74), channel_id=1, source_target_pairs={{0,64},{32,96},{64,0},{96,32},{1,65},{33,97},{65,1},{97,33},{2,66}... | collective-permute-start | bytes 393224 | tf_op jit(solution)/shard_map/ppermute | solution.py:22
  219.9 9.5 %collective-permute-start.56 = (f32[128,256]{1,0:T(8,128)S(1)}, f32[128,256]{1,0:T(8,128)S(1)}, u32[]{:S(2)}, u32[]{:S(2)}) collective-permute-start(f32[128,256]{1,0:T(8,128)S(1)} %get-tuple-element.74), channel_id=1, source_target_pairs={{0,32},{32,64},{64,96},{96,0},{1,33},{33,65},{65,97},{97,1},{2,34}... | collective-permute-start | bytes 393224 | tf_op jit(solution)/shard_map/ppermute | solution.py:22
  219.9 9.5 %collective-permute-start.58 = (f32[128,256]{1,0:T(8,128)S(1)}, f32[128,256]{1,0:T(8,128)S(1)}, u32[]{:S(2)}, u32[]{:S(2)}) collective-permute-start(f32[128,256]{1,0:T(8,128)S(1)} %get-tuple-element.74), channel_id=1, source_target_pairs={{0,96},{32,0},{64,32},{96,64},{1,97},{33,1},{65,33},{97,65},{2,98}... | collective-permute-start | bytes 393224 | tf_op jit(solution)/shard_map/ppermute | solution.py:22
  224.3 9.5 %collective-permute-start.54 = (f32[128,256]{1,0:T(8,128)S(1)}, f32[128,256]{1,0:T(8,128)S(1)}, u32[]{:S(2)}, u32[]{:S(2)}) collective-permute-start(f32[128,256]{1,0:T(8,128)S(1)} %add_add_fusion.4), channel_id=1, source_target_pairs={{0,6},{2,0},{4,2},{6,4},{1,7},{3,1},{5,3},{7,5},{8,14},{10,8},{12,... | collective-permute-start | bytes 393224 | tf_op jit(solution)/shard_map/ppermute | solution.py:22
  228.7 8.7 %collective-permute-start.52 = (f32[128,256]{1,0:T(8,128)S(1)}, f32[128,256]{1,0:T(8,128)S(1)}, u32[]{:S(2)}, u32[]{:S(2)}) collective-permute-start(f32[128,256]{1,0:T(8,128)S(1)} %add_add_fusion.4), channel_id=1, source_target_pairs={{0,2},{2,4},{4,6},{6,0},{1,3},{3,5},{5,7},{7,1},{8,10},{10,12},{12... | collective-permute-start | bytes 393224 | tf_op jit(solution)/shard_map/ppermute | solution.py:22
  229.4 9.9 %collective-permute-start.63 = (f32[128,256]{1,0:T(8,128)S(1)}, f32[128,256]{1,0:T(8,128)S(1)}, u32[]{:S(2)}, u32[]{:S(2)}) collective-permute-start(f32[128,256]{1,0:T(8,128)S(1)} %get-tuple-element.73), channel_id=1, source_target_pairs={{0,16},{8,24},{16,0},{24,8},{1,17},{9,25},{17,1},{25,9},{2,18},{10... | collective-permute-start | bytes 393224 | tf_op jit(solution)/shard_map/ppermute | solution.py:22
  229.4 10.3 %collective-permute-start.62 = (f32[128,256]{1,0:T(8,128)S(1)}, f32[128,256]{1,0:T(8,128)S(1)}, u32[]{:S(2)}, u32[]{:S(2)}) collective-permute-start(f32[128,256]{1,0:T(8,128)S(1)} %get-tuple-element.73), channel_id=1, source_target_pairs={{0,8},{8,16},{16,24},{24,0},{1,9},{9,17},{17,25},{25,1},{2,10},{10... | collective-permute-start | bytes 393224 | tf_op jit(solution)/shard_map/ppermute | solution.py:22
  234.1 14.6 %collective-permute-start.61 = (f32[4,128,256]{2,1,0:T(8,128)S(1)}, f32[4,128,256]{2,1,0:T(8,128)S(1)}, u32[]{:S(2)}, u32[]{:S(2)}) collective-permute-start(f32[4,128,256]{2,1,0:T(8,128)S(1)} %pad_maximum_fusion.2.refs_6_), channel_id=1, source_target_pairs={{0,24},{8,0},{16,8},{24,16},{1,25},{9,1},{17,9},{25,17},{2,26},{10... | collective-permute-start | bytes 1572872 | tf_op jit(solution)/shard_map/ppermute | solution.py:22
  239.3 38.8 %collective-permute-start.60 = (f32[4,128,256]{2,1,0:T(8,128)S(1)}, f32[4,128,256]{2,1,0:T(8,128)S(1)}, u32[]{:S(2)}, u32[]{:S(2)}) collective-permute-start(f32[4,128,256]{2,1,0:T(8,128)S(1)} %pad_maximum_fusion.2.refs_6_), channel_id=1, source_target_pairs={{0,16},{8,24},{16,0},{24,8},{1,17},{9,25},{17,1},{25,9},{2,18},{10... | collective-permute-start | bytes 1572872 | tf_op jit(solution)/shard_map/ppermute | solution.py:22
  239.7 38.4 %collective-permute-start.59 = (f32[4,128,256]{2,1,0:T(8,128)S(1)}, f32[4,128,256]{2,1,0:T(8,128)}, u32[]{:S(2)}, u32[]{:S(2)}) collective-permute-start(f32[4,128,256]{2,1,0:T(8,128)S(1)} %pad_maximum_fusion.2.refs_6_), channel_id=1, source_target_pairs={{0,8},{8,16},{16,24},{24,0},{1,9},{9,17},{17,25},{25,1},{2,10},{10... | collective-permute-start | bytes 1572872 | tf_op jit(solution)/shard_map/ppermute | solution.py:22
  240.1 38.0 %collective-permute-start.67 = (f32[4,128,256]{2,1,0:T(8,128)S(1)}, f32[4,128,256]{2,1,0:T(8,128)}, u32[]{:S(2)}, u32[]{:S(2)}) collective-permute-start(f32[4,128,256]{2,1,0:T(8,128)S(1)} %pad_maximum_fusion.3.refs_10_), channel_id=1, source_target_pairs={{0,96},{32,0},{64,32},{96,64},{1,97},{33,1},{65,33},{97,65},{2,98}... | collective-permute-start | bytes 1572872 | tf_op jit(solution)/shard_map/ppermute | solution.py:22
  240.7 37.4 %collective-permute-start.66 = (f32[4,128,256]{2,1,0:T(8,128)S(1)}, f32[4,128,256]{2,1,0:T(8,128)}, u32[]{:S(2)}, u32[]{:S(2)}) collective-permute-start(f32[4,128,256]{2,1,0:T(8,128)S(1)} %pad_maximum_fusion.3.refs_10_), channel_id=1, source_target_pairs={{0,64},{32,96},{64,0},{96,32},{1,65},{33,97},{65,1},{97,33},{2,66}... | collective-permute-start | bytes 1572872 | tf_op jit(solution)/shard_map/ppermute | solution.py:22
  248.7 29.4 %collective-permute-start.65 = (f32[4,128,256]{2,1,0:T(8,128)S(1)}, f32[4,128,256]{2,1,0:T(8,128)}, u32[]{:S(2)}, u32[]{:S(2)}) collective-permute-start(f32[4,128,256]{2,1,0:T(8,128)S(1)} %pad_maximum_fusion.3.refs_10_), channel_id=1, source_target_pairs={{0,32},{32,64},{64,96},{96,0},{1,33},{33,65},{65,97},{97,1},{2,34}... | collective-permute-start | bytes 1572872 | tf_op jit(solution)/shard_map/ppermute | solution.py:22
  302.2 14.2 %collective-permute-start.71 = (f32[256,256]{1,0:T(8,128)S(1)}, f32[256,256]{1,0:T(8,128)S(1)}, u32[]{:S(2)}, u32[]{:S(2)}) collective-permute-start(f32[256,256]{1,0:T(8,128)S(1)} %get-tuple-element.68), channel_id=1, source_target_pairs={{0,6},{2,0},{4,2},{6,4},{1,7},{3,1},{5,3},{7,5},{8,14},{10,8},{12,... | collective-permute-start | bytes 786440 | tf_op jit(solution)/shard_map/ppermute | solution.py:22
  302.3 19.8 %collective-permute-start.70 = (f32[256,256]{1,0:T(8,128)S(1)}, f32[256,256]{1,0:T(8,128)S(1)}, u32[]{:S(2)}, u32[]{:S(2)}) collective-permute-start(f32[256,256]{1,0:T(8,128)S(1)} %get-tuple-element.69), channel_id=1, source_target_pairs={{0,4},{2,6},{4,0},{6,2},{1,5},{3,7},{5,1},{7,3},{8,12},{10,14},{12... | collective-permute-start | bytes 786440 | tf_op jit(solution)/shard_map/ppermute | solution.py:22
  315.7 12.4 %collective-permute-start.69 = (f32[256,256]{1,0:T(8,128)S(1)}, f32[256,256]{1,0:T(8,128)S(1)}, u32[]{:S(2)}, u32[]{:S(2)}) collective-permute-start(f32[256,256]{1,0:T(8,128)S(1)} %get-tuple-element.70), channel_id=1, source_target_pairs={{0,2},{2,4},{4,6},{6,0},{1,3},{3,5},{5,7},{7,1},{8,10},{10,12},{12... | collective-permute-start | bytes 786440 | tf_op jit(solution)/shard_map/ppermute | solution.py:22
  328.7 9.7 %collective-permute-start.73 = (f32[256,256]{1,0:T(8,128)S(1)}, f32[256,256]{1,0:T(8,128)S(1)}, u32[]{:S(2)}, u32[]{:S(2)}) collective-permute-start(f32[256,256]{1,0:T(8,128)S(1)} %fusion.6.refs_4_), channel_id=1, source_target_pairs={{0,4},{2,6},{4,0},{6,2},{1,5},{3,7},{5,1},{7,3},{8,12},{10,14},{12... | collective-permute-start | bytes 786440 | tf_op jit(solution)/shard_map/ppermute | solution.py:22
  331.2 12.8 %collective-permute-start.72 = (f32[256,256]{1,0:T(8,128)S(1)}, f32[256,256]{1,0:T(8,128)S(1)}, u32[]{:S(2)}, u32[]{:S(2)}) collective-permute-start(f32[256,256]{1,0:T(8,128)S(1)} %fusion.6.refs_4_), channel_id=1, source_target_pairs={{0,2},{2,4},{4,6},{6,0},{1,3},{3,5},{5,7},{7,1},{8,10},{10,12},{12... | collective-permute-start | bytes 786440 | tf_op jit(solution)/shard_map/ppermute | solution.py:22
  331.6 13.0 %collective-permute-start.75 = (f32[256,256]{1,0:T(8,128)S(1)}, f32[256,256]{1,0:T(8,128)S(1)}, u32[]{:S(2)}, u32[]{:S(2)}) collective-permute-start(f32[256,256]{1,0:T(8,128)S(1)} %fusion.6.refs_4_), channel_id=1, source_target_pairs={{0,1},{1,0},{2,3},{3,2},{4,5},{5,4},{6,7},{7,6},{8,9},{9,8},{10,11... | collective-permute-start | bytes 786440 | tf_op jit(solution)/shard_map/ppermute | solution.py:26
  336.0 8.6 %collective-permute-start.78 = (f32[256,256]{1,0:T(8,128)S(1)}, f32[256,256]{1,0:T(8,128)S(1)}, u32[]{:S(2)}, u32[]{:S(2)}) collective-permute-start(f32[256,256]{1,0:T(8,128)S(1)} %collective-permute-done.74.refs_7_), channel_id=1, source_target_pairs={{0,1},{1,0},{2,3},{3,2},{4,5},{5,4},{6,7},{7,6},{8,9},{9,8},{10,11... | collective-permute-start | bytes 786440 | tf_op jit(solution)/shard_map/ppermute | solution.py:26
  363.8 12.2 %collective-permute-start.79 = (f32[4,128,256]{2,1,0:T(8,128)}, f32[4,128,256]{2,1,0:T(8,128)S(1)}, u32[]{:S(2)}, u32[]{:S(2)}) collective-permute-start(f32[4,128,256]{2,1,0:T(8,128)} %get-tuple-element.38), channel_id=1, source_target_pairs={{0,32},{32,64},{64,96},{96,0},{1,33},{33,65},{65,97},{97,1},{2,34}... | collective-permute-start | bytes 1572872 | tf_op jit(solution)/shard_map/ppermute | solution.py:22
  363.8 26.2 %collective-permute-start.80 = (f32[4,128,256]{2,1,0:T(8,128)}, f32[4,128,256]{2,1,0:T(8,128)S(1)}, u32[]{:S(2)}, u32[]{:S(2)}) collective-permute-start(f32[4,128,256]{2,1,0:T(8,128)} %get-tuple-element.39), channel_id=1, source_target_pairs={{0,64},{32,96},{64,0},{96,32},{1,65},{33,97},{65,1},{97,33},{2,66}... | collective-permute-start | bytes 1572872 | tf_op jit(solution)/shard_map/ppermute | solution.py:22
  366.7 24.3 %collective-permute-start.81 = (f32[4,128,256]{2,1,0:T(8,128)}, f32[4,128,256]{2,1,0:T(8,128)S(1)}, u32[]{:S(2)}, u32[]{:S(2)}) collective-permute-start(f32[4,128,256]{2,1,0:T(8,128)} %get-tuple-element.40), channel_id=1, source_target_pairs={{0,96},{32,0},{64,32},{96,64},{1,97},{33,1},{65,33},{97,65},{2,98}... | collective-permute-start | bytes 1572872 | tf_op jit(solution)/shard_map/ppermute | solution.py:22
  368.7 27.0 %collective-permute-start.85 = (f32[4,128,256]{2,1,0:T(8,128)}, f32[4,128,256]{2,1,0:T(8,128)S(1)}, u32[]{:S(2)}, u32[]{:S(2)}) collective-permute-start(f32[4,128,256]{2,1,0:T(8,128)} %get-tuple-element.42), channel_id=1, source_target_pairs={{0,8},{8,16},{16,24},{24,0},{1,9},{9,17},{17,25},{25,1},{2,10},{10... | collective-permute-start | bytes 1572872 | tf_op jit(solution)/shard_map/ppermute | solution.py:22
  368.7 27.0 %collective-permute-start.86 = (f32[4,128,256]{2,1,0:T(8,128)}, f32[4,128,256]{2,1,0:T(8,128)S(1)}, u32[]{:S(2)}, u32[]{:S(2)}) collective-permute-start(f32[4,128,256]{2,1,0:T(8,128)} %get-tuple-element.43), channel_id=1, source_target_pairs={{0,16},{8,24},{16,0},{24,8},{1,17},{9,25},{17,1},{25,9},{2,18},{10... | collective-permute-start | bytes 1572872 | tf_op jit(solution)/shard_map/ppermute | solution.py:22
  375.9 20.2 %collective-permute-start.87 = (f32[4,128,256]{2,1,0:T(8,128)}, f32[4,128,256]{2,1,0:T(8,128)S(1)}, u32[]{:S(2)}, u32[]{:S(2)}) collective-permute-start(f32[4,128,256]{2,1,0:T(8,128)} %get-tuple-element.44), channel_id=1, source_target_pairs={{0,24},{8,0},{16,8},{24,16},{1,25},{9,1},{17,9},{25,17},{2,26},{10... | collective-permute-start | bytes 1572872 | tf_op jit(solution)/shard_map/ppermute | solution.py:22
  392.1 11.8 %collective-permute-start.84 = (f32[128,256]{1,0:T(8,128)S(1)}, f32[128,256]{1,0:T(8,128)S(1)}, u32[]{:S(2)}, u32[]{:S(2)}) collective-permute-start(f32[128,256]{1,0:T(8,128)S(1)} %get-tuple-element.53), channel_id=1, source_target_pairs={{0,24},{8,0},{16,8},{24,16},{1,25},{9,1},{17,9},{25,17},{2,26},{10... | collective-permute-start | bytes 393224 | tf_op jit(solution)/shard_map/ppermute | solution.py:22
  392.2 12.5 %collective-permute-start.83 = (f32[128,256]{1,0:T(8,128)S(1)}, f32[128,256]{1,0:T(8,128)S(1)}, u32[]{:S(2)}, u32[]{:S(2)}) collective-permute-start(f32[128,256]{1,0:T(8,128)S(1)} %get-tuple-element.54), channel_id=1, source_target_pairs={{0,16},{8,24},{16,0},{24,8},{1,17},{9,25},{17,1},{25,9},{2,18},{10... | collective-permute-start | bytes 393224 | tf_op jit(solution)/shard_map/ppermute | solution.py:22
  395.7 9.0 %collective-permute-start.82 = (f32[128,256]{1,0:T(8,128)S(1)}, f32[128,256]{1,0:T(8,128)S(1)}, u32[]{:S(2)}, u32[]{:S(2)}) collective-permute-start(f32[128,256]{1,0:T(8,128)S(1)} %get-tuple-element.55), channel_id=1, source_target_pairs={{0,8},{8,16},{16,24},{24,0},{1,9},{9,17},{17,25},{25,1},{2,10},{10... | collective-permute-start | bytes 393224 | tf_op jit(solution)/shard_map/ppermute | solution.py:22
  396.2 9.5 %collective-permute-start.90 = (f32[128,256]{1,0:T(8,128)S(1)}, f32[128,256]{1,0:T(8,128)S(1)}, u32[]{:S(2)}, u32[]{:S(2)}) collective-permute-start(f32[128,256]{1,0:T(8,128)S(1)} %get-tuple-element.56), channel_id=1, source_target_pairs={{0,96},{32,0},{64,32},{96,64},{1,97},{33,1},{65,33},{97,65},{2,98}... | collective-permute-start | bytes 393224 | tf_op jit(solution)/shard_map/ppermute | solution.py:22
  397.7 8.6 %collective-permute-start.89 = (f32[128,256]{1,0:T(8,128)S(1)}, f32[128,256]{1,0:T(8,128)S(1)}, u32[]{:S(2)}, u32[]{:S(2)}) collective-permute-start(f32[128,256]{1,0:T(8,128)S(1)} %get-tuple-element.57), channel_id=1, source_target_pairs={{0,64},{32,96},{64,0},{96,32},{1,65},{33,97},{65,1},{97,33},{2,66}... | collective-permute-start | bytes 393224 | tf_op jit(solution)/shard_map/ppermute | solution.py:22
  417.9 8.3 %collective-permute-start.92 = (f32[128,256]{1,0:T(8,128)S(1)}, f32[128,256]{1,0:T(8,128)S(1)}, u32[]{:S(2)}, u32[]{:S(2)}) collective-permute-start(f32[128,256]{1,0:T(8,128)S(1)} %dynamic-slice_add_fusion), channel_id=1, source_target_pairs={{0,32},{32,64},{64,96},{96,0},{1,33},{33,65},{65,97},{97,1},{2,34}... | collective-permute-start | bytes 393224 | tf_op jit(solution)/shard_map/ppermute | solution.py:22
  436.7 8.9 %collective-permute-start.98 = (f32[128,256]{1,0:T(8,128)S(1)}, f32[128,256]{1,0:T(8,128)S(1)}, u32[]{:S(2)}, u32[]{:S(2)}) collective-permute-start(f32[128,256]{1,0:T(8,128)S(1)} %add_add_fusion.1), channel_id=1, source_target_pairs={{0,2},{2,4},{4,6},{6,0},{1,3},{3,5},{5,7},{7,1},{8,10},{10,12},{12... | collective-permute-start | bytes 393224 | tf_op jit(solution)/shard_map/ppermute | solution.py:22
  (74 other events, 674.0 us)

commit v2 on v1

v2 whole, which is shorter than its diff:
```python
import functools
import math

import jax
import jax.numpy as jnp
from jax import lax
from jax.experimental import pallas as pl
from jax.experimental.pallas import tpu as pltpu
from jax.sharding import Mesh
from jax.sharding import PartitionSpec as P

ITERS = 2
HIGHEST = lax.Precision.HIGHEST
F32 = jnp.float32
BF16 = jnp.bfloat16
BLK = 128
HALF = 64
CHUNK = 32
UNROLL = 8


def flip(value, step):
    axis, mask = step
    return lax.ppermute(value, axis, [(i, i ^ mask) for i in range(2 if axis == "c" else 4)])


def gather(value, steps):
    for step in steps[:-1]:
        value = jnp.concatenate([value, flip(value, step)])
    return [value, flip(value, steps[-1])]


def scatter(keep, send, steps):
    for step in reversed(steps[1:]):
        got = flip(send, step)
        half = keep.shape[0] // 2
        keep, send = keep[:half] + got[:half], keep[half:] + got[half:]
    return keep + flip(send, steps[0])


X1, X3, Y1, Y3, Z1, Z3 = [(axis, mask) for axis in "xyz" for mask in (1, 3)]
CORE = ("c", 1)
ROW_STEPS = [[X1, X3, Y1, Y3], [X3, X1, Y3, Y1], [Y1, Y3, X1, X3], [Y3, Y1, X3, X1]]
COL_STEPS = [[Z1, Z3], [Z3, Z1]]


def shift(value, axis, amount):
    return lax.ppermute(value, axis, [(i, (i + amount) % 4) for i in range(4)])


def ring_sum(value, axis):
    return (value + shift(value, axis, 1)) + (shift(value, axis, 2) + shift(value, axis, 3))


def flip_bits(mine, other):
    offset = mine ^ other
    return jnp.where((offset == 1) | (offset == 2), 1, 0), jnp.where(offset >= 2, 1, 0)


def swapped(index):
    return (index & 5) * 2 + (index & 10) // 2


def split(value):
    high = value.astype(BF16)
    return high, (value - high.astype(F32)).astype(BF16)


def nt_dot(a, b, precision=HIGHEST):
    return lax.dot_general(
        a, b, (((1,), (1,)), ((), ())), precision=precision, preferred_element_type=F32
    )


def lane_sums(block):
    return nt_dot(jnp.ones((8, block.shape[1]), F32), block)[0:1, :]


def live_tile(tiles_ref, slot, first, count):
    return jnp.where(first + slot < count, tiles_ref[slot], 0.0)


def rowsum_kernel(count_ref, put_ref, tiles_ref, *refs):
    out_ref, total = refs[-2:]
    step = pl.program_id(0)
    count = count_ref[0]

    @pl.when(step == 0)
    def _():
        total[...] = jnp.zeros_like(total)

    first = step * CHUNK

    @pl.when(first < count)
    def _():
        def one(slot, carry):
            block = put_ref[first + slot]
            total[block] += live_tile(tiles_ref, slot, first, count)
            return carry

        lax.fori_loop(0, CHUNK, one, 0, unroll=UNROLL)

    @pl.when(step == pl.num_programs(0) - 1)
    def _():
        for block in range(total.shape[0]):
            out_ref[block : block + 1, :] = lane_sums(total[block])


def chunk_map(step, count_ref, *_):
    return (jnp.minimum(step, (count_ref[0] + CHUNK - 1) // CHUNK - 1), 0, 0)


def rowsum_call(count, put, tiles, out_blocks, after):
    slots = tiles.shape[0]
    return pl.pallas_call(
        rowsum_kernel,
        out_shape=jax.ShapeDtypeStruct((out_blocks, BLK), F32),
        grid_spec=pltpu.PrefetchScalarGridSpec(
            num_scalar_prefetch=2,
            grid=(slots // CHUNK,),
            in_specs=[pl.BlockSpec((CHUNK, BLK, BLK), chunk_map)]
            + [pl.BlockSpec(memory_space=pl.ANY)] * len(after),
            out_specs=pl.BlockSpec((out_blocks, BLK), lambda s, *_: (0, 0)),
            scratch_shapes=[pltpu.VMEM((out_blocks, BLK, BLK), F32)],
        ),
        cost_estimate=pl.CostEstimate(flops=10**10, bytes_accessed=2**23, transcendentals=0),
    )(count, put, tiles, *after)


def apply_loop(
    count, first, put_ref, take_ref, tiles_ref, source, total, adjoint, tilde, inverse_ref
):
    def one(slot, carry):
        tile = live_tile(tiles_ref, slot, first, count)
        take = take_ref[first + slot]
        put = pl.multiple_of(put_ref[first + slot], 8)
        if tilde is not None:
            tilde_block = put_ref[put_ref.shape[0] // 2 + first + slot]
            tilde[tilde_block] += tile * inverse_ref[pl.ds(take, 1), :]
        if adjoint:
            tile = tile.T
        high, low = split(tile)
        product = jnp.dot(
            jnp.concatenate([high, high], axis=1), source[take], preferred_element_type=F32
        ) + jnp.dot(low, source[take, :BLK], preferred_element_type=F32)
        total[pl.ds(put, BLK), :] += product
        return carry

    lax.fori_loop(0, CHUNK, one, 0, unroll=UNROLL)


def put_source(source, index, row, value):
    high, low = split(value)
    rows = value.shape[0]
    source[index, row : row + rows] = high
    source[index, BLK + row : BLK + row + rows] = low


def piece_place(quarter, index):
    place = index if quarter % 2 == 0 else swapped(index)
    return (quarter // 2) * 16 + place, (quarter % 2) * HALF


def forward_kernel(first_pass, *refs):
    count_ref, put_ref, take_ref, tiles_ref, inverse_ref = refs[:5]
    factor_ref = None
    refs = refs[5:]
    if not first_pass:
        factor_ref, refs = refs[0], refs[1:]
    pieces, (keep_ref, send_ref), refs = refs[:8], refs[8:10], refs[10:]
    source, total = refs[:2]
    tilde = refs[2] if first_pass else None
    step = pl.program_id(0)
    count = count_ref[0]
    first = step * CHUNK

    @pl.when(step == 0)
    def _():
        total[...] = jnp.zeros_like(total)
        if first_pass:
            tilde[...] = jnp.zeros_like(tilde)
        inverse = inverse_ref[...].T
        for number, piece in enumerate(pieces):
            quarter, half = number // 2, number % 2
            if not first_pass:
                values = nt_dot(piece[...].reshape(8 * HALF, -1), factor_ref[...])
            for part in range(8):
                index, row = piece_place(quarter, half * 8 + part)
                value = piece[part] if first_pass else values[part * HALF : (part + 1) * HALF]
                put_source(source, index, row, value * inverse[row : row + HALF, index : index + 1])

    @pl.when(first < count)
    def _():
        apply_loop(
            count, first, put_ref, take_ref, tiles_ref, source, total, False, tilde, inverse_ref
        )

    @pl.when(step == pl.num_programs(0) - 1)
    def _():
        rows = keep_ref.shape[1]
        for number in range(16):
            if first_pass:
                line = lane_sums(tilde[number])
                total[number * rows + BLK : (number + 1) * rows, :BLK] = jnp.broadcast_to(
                    line, (rows - BLK, BLK)
                )
            target = keep_ref if number < 8 else send_ref
            target[number % 8] = total[number * rows : (number + 1) * rows, :]


def whole(shape):
    return pl.BlockSpec(shape, lambda s, *_: (0,) * len(shape), pipeline_mode=pl.Buffered(1))


def forward_call(count, put, take, tiles, inverse, factor, pieces):
    first_pass = factor is None
    slots = tiles.shape[0]
    width = pieces[0].shape[-1]
    rows = BLK + (8 if first_pass else 0)
    extra = [] if first_pass else [factor]
    out = jax.ShapeDtypeStruct((8, rows, width), F32)
    scratch = [pltpu.VMEM((32, 2 * BLK, width), BF16), pltpu.VMEM((16 * rows, width), F32)]
    if first_pass:
        scratch.append(pltpu.VMEM((16, BLK, BLK), F32))
    return pl.pallas_call(
        functools.partial(forward_kernel, first_pass),
        out_shape=(out, out),
        grid_spec=pltpu.PrefetchScalarGridSpec(
            num_scalar_prefetch=3,
            grid=(slots // CHUNK,),
            in_specs=[pl.BlockSpec((CHUNK, BLK, BLK), chunk_map)]
            + [whole(a.shape) for a in [inverse] + extra + list(pieces)],
            out_specs=(whole(out.shape), whole(out.shape)),
            scratch_shapes=scratch,
        ),
        cost_estimate=pl.CostEstimate(
            flops=6 * 2**30, bytes_accessed=2**24, transcendentals=0
        ),
    )(count, put, take, tiles, inverse, *extra, *pieces)


def backward_kernel(*refs):
    count_ref, put_ref, take_ref, tiles_ref = refs[:4]
    pieces, outs, (source, total) = refs[4:12], refs[12:20], refs[20:]
    step = pl.program_id(0)
    count = count_ref[0]
    first = step * CHUNK

    @pl.when(step == 0)
    def _():
        total[...] = jnp.zeros_like(total)
        for number, piece in enumerate(pieces):
            for part in range(2):
                put_source(source, number * 2 + part, 0, piece[part])

    @pl.when(first < count)
    def _():
        apply_loop(count, first, put_ref, take_ref, tiles_ref, source, total, True, None, None)

    @pl.when(step == pl.num_programs(0) - 1)
    def _():
        for number, out in enumerate(outs):
            for part in range(8):
                index, row = piece_place(number // 2, number % 2 * 8 + part)
                out[part] = total[index * BLK + row : index * BLK + row + HALF, :]


def backward_call(count, put, take, tiles, pieces):
    slots = tiles.shape[0]
    width = pieces[0].shape[-1]
    out = jax.ShapeDtypeStruct((8, HALF, width), F32)
    return pl.pallas_call(
        backward_kernel,
        out_shape=(out,) * 8,
        grid_spec=pltpu.PrefetchScalarGridSpec(
            num_scalar_prefetch=3,
            grid=(slots // CHUNK,),
            in_specs=[pl.BlockSpec((CHUNK, BLK, BLK), chunk_map)]
            + [whole(a.shape) for a in pieces],
            out_specs=(whole(out.shape),) * 8,
            scratch_shapes=[
                pltpu.VMEM((16, 2 * BLK, width), BF16),
                pltpu.VMEM((32 * BLK, width), F32),
            ],
        ),
        cost_estimate=pl.CostEstimate(
            flops=6 * 2**30, bytes_accessed=2**24, transcendentals=0
        ),
    )(count, put, take, tiles, *pieces)


PANEL = 32


def inverse_factor_kernel(gram_ref, out_ref, work, columns, multiplier, right):
    size = gram_ref.shape[0]
    lanes = columns.shape[-1]
    work[:, :size] = gram_ref[...]
    row_at = lax.broadcasted_iota(jnp.int32, (size, size), 0)
    lane_at = lax.broadcasted_iota(jnp.int32, (size, size), 1)
    work[:, size:] = (row_at == lane_at).astype(F32)
    row_small = lax.broadcasted_iota(jnp.int32, (PANEL, lanes), 0)
    lane_small = lax.broadcasted_iota(jnp.int32, (PANEL, lanes), 1)
    unit = (row_small == lane_small).astype(F32)
    for start in range(0, size, PANEL):
        end = start + PANEL
        corner = work[start:end, start:end]
        for k in range(PANEL):
            columns[k] = jnp.broadcast_to(corner[:, k : k + 1], (PANEL, lanes))
        right[...] = unit
        for j in range(PANEL - 1):
            low = 8 * ((j + 1) // 8)
            column = columns[j, low:, :]
            factor = jnp.where(row_small[low:] > j, column, 0.0) * (1.0 / columns[j, j : j + 1, :])
            multiplier[low:, :] = factor
            for k in range(j + 1, PANEL):
                k_low = 8 * (k // 8)
                columns[k, k_low:, :] -= column[k_low - low :] * multiplier[k : k + 1, :]
            right[low:, :] -= factor * right[j : j + 1, :]
        pivots = jnp.concatenate([columns[k, k : k + 1, :] for k in range(PANEL)], axis=0)
        corner = (right[...] * (1.0 / jnp.sqrt(pivots)))[:, :PANEL]
        left = lanes * (start // lanes)
        used = size + lanes * ((end + lanes - 1) // lanes)
        panel = jnp.dot(
            corner, work[start:end, left:used], precision=HIGHEST, preferred_element_type=F32
        )
        work[start:end, left:used] = panel
        if end < size:
            update = lax.dot_general(
                panel[:, : size - left],
                panel,
                (((0,), (0,)), ((), ())),
                precision=HIGHEST,
                preferred_element_type=F32,
            )
            work[end:, left:used] -= update[end - left :, :]
    out_ref[...] = work[:, size:]


def inverse_factor(gram):
    size = gram.shape[0]
    return pl.pallas_call(
        inverse_factor_kernel,
        out_shape=jax.ShapeDtypeStruct((size, size), F32),
        in_specs=[pl.BlockSpec(memory_space=pltpu.VMEM)],
        out_specs=pl.BlockSpec(memory_space=pltpu.VMEM),
        scratch_shapes=[
            pltpu.VMEM((size, 2 * size), F32),
            pltpu.VMEM((PANEL, PANEL, BLK), F32),
            pltpu.VMEM((PANEL, BLK), F32),
            pltpu.VMEM((PANEL, BLK), F32),
        ],
        cost_estimate=pl.CostEstimate(flops=2**34, bytes_accessed=2**19, transcendentals=0),
    )(gram)


def quarters(value):
    return [value[None, q * HALF : (q + 1) * HALF] for q in range(4)]


def gather_row(value):
    return sum([gather(part, steps) for part, steps in zip(quarters(value), ROW_STEPS)], [])


def gather_two(value, steps):
    return jnp.concatenate(gather(value, steps[:2]))


def scatter_row(outs):
    parts = [scatter(outs[2 * q], outs[2 * q + 1], ROW_STEPS[q])[0] for q in range(4)]
    return jnp.concatenate(parts, axis=0)


def scatter_col(keep, send):
    got = flip(send, CORE)
    parts = []
    for half, steps in enumerate(COL_STEPS):
        low, high = slice(4 * half, 4 * half + 2), slice(4 * half + 2, 4 * half + 4)
        parts.append(scatter(keep[low] + got[low], keep[high] + got[high], steps)[0])
    return parts


def gather_col(value):
    pieces = []
    for half, steps in enumerate(COL_STEPS):
        pieces += gather(value[None, half * BLK : (half + 1) * BLK], steps)
    return pieces + [flip(piece, CORE) for piece in pieces]


def gram_sum(gram):
    half = gram.shape[0] // 2
    core = lax.axis_index("c")
    kept = lax.dynamic_slice_in_dim(gram, core * half, half, 0)
    sent = lax.dynamic_slice_in_dim(gram, (1 - core) * half, half, 0)
    value = kept + flip(sent, CORE)
    for axis in "xyz":
        value = ring_sum(value, axis)
    other = flip(value, CORE)
    return jnp.where(
        core == 0, jnp.concatenate([value, other]), jnp.concatenate([other, value])
    )


def local(trial_vectors, tiles, tile_rows, tile_cols, tile_count):
    x, y, z, core = [lax.axis_index(a) for a in ("x", "y", "z", "c")]
    slots = tiles.shape[2]
    width = trial_vectors.shape[1]
    tiles = tiles.reshape(slots, BLK, BLK)
    count = tile_count.reshape(1)

    row = tile_rows.reshape(slots)
    col = tile_cols.reshape(slots)
    near, far = flip_bits(z, row // 4)
    slab = (((row // 2) % 2) ^ core) * 8 + jnp.where(row % 2 == 0, near + 2 * far, 4 + far + 2 * near)
    near_x, far_x = flip_bits(x, col // 8)
    near_y, far_y = flip_bits(y, (col // 2) % 4)
    at_x, at_y = near_x + 2 * far_x, near_y + 2 * far_y
    member = jnp.where(col % 2 == 0, at_x + 4 * at_y, 16 + at_y + 4 * at_x)
    put_first = jnp.concatenate([slab * (BLK + 8), slab])
    put_later = slab * BLK
    put_backward = member * BLK

    begun = [gather_two(part, steps) for part, steps in zip(quarters(trial_vectors), ROW_STEPS)]
    pieces = sum([gather(part, steps[2:]) for part, steps in zip(begun, ROW_STEPS)], [])

    sums = rowsum_call(
        count, (slab // 8) * 8 + (near + 2 * far) * 2 + row % 2, tiles, 16, begun
    ).reshape(2, 2, 2, 2, BLK)
    got = sums[0] + flip(sums[1], CORE)
    inverse_own = 1.0 / (1.0 + scatter(got[0], got[1], COL_STEPS[0])[0])
    gathered = jnp.concatenate(gather(inverse_own[None], ROW_STEPS[0]))
    inverse = jnp.concatenate(
        [gathered[:, 0], gathered[:, 1].reshape(4, 4, BLK).swapaxes(0, 1).reshape(16, BLK)]
    )
    inverse_own = inverse_own.reshape(2 * BLK, 1)

    vectors = trial_vectors
    factor = None
    scale = None
    for iteration in range(ITERS):
        keep, send = forward_call(
            count,
            put_first if iteration == 0 else put_later,
            member,
            tiles,
            inverse,
            factor,
            pieces,
        )
        one, two = scatter_col(keep, send)
        if iteration == 0:
            tilde = jnp.concatenate([one[BLK, :BLK], two[BLK, :BLK]]).reshape(2 * BLK, 1)
            scale = inverse_own / (inverse_own * (inverse_own + tilde))
        summed = jnp.concatenate([one[:BLK], two[:BLK]])
        weighted = scale * (scale * (summed + inverse_own * vectors))
        outs = backward_call(count, put_backward, slab, tiles, gather_col(weighted))
        reduced = inverse_own * (scatter_row(outs) + weighted)
        gram = lax.dot_general(
            reduced,
            reduced,
            (((0,), (0,)), ((), ())),
            precision=HIGHEST,
            preferred_element_type=F32,
        )
        if iteration + 1 < ITERS:
            pieces = gather_row(reduced)
        factor = inverse_factor(gram_sum(gram))
        vectors = nt_dot(reduced, factor)
    total_nodes = 2 * BLK * 128
    return vectors * math.sqrt(total_nodes)


def solution(mesh):
    fine = Mesh(mesh.devices.reshape(4, 4, 4, 2), ("x", "y", "z", "c"))
    row, column = ("x", "y"), ("z", "c")
    in_specs = (
        P(row + column, None),
        P(row, column, None, None, None),
        P(row, column, None),
        P(row, column, None),
        P(row, column),
    )
    return jax.shard_map(
        local, mesh=fine, in_specs=in_specs, out_specs=P(row + column, None), check_vma=False
    )
```

time: 490 us -> 406 us (0.83)
  Pallas kernels: 139 us -> 76.6 us
  waiting for transfers between devices: 170 us -> 110 us
  starting transfers between devices: 146 us -> 186 us
    ppermute x102 -> x119, waiting for transfers between devices: 170 us -> 110 us  [the longest x101 74.7 us: flip(): lax.ppermute(value, axis, [(i, i ^ mask) for i in range(2 if axis == 'c'...]
    ppermute x102 -> x119, starting transfers between devices: 146 us -> 186 us  [the longest x101 168 us: flip(): lax.ppermute(value, axis, [(i, i ^ mask) for i in range(2 if axis == 'c'...]
    pallas_call x2, Pallas kernels: 58.3 us -> 26.6 us  [inverse_factor(): pl.pallas_call(inverse_factor_kernel, out_shape=jax.ShapeDtypeStruct((siz...]
    pallas_call x2, Pallas kernels: 34.6 us -> 19.6 us  [backward_call(): pl.pallas_call(backward_kernel, out_shape=(out,) * 8, grid_spec=pltpu.Pre...]
    pallas_call x2, Pallas kernels: 36.5 us -> 24.7 us  [forward_call(): pl.pallas_call(functools.partial(forward_kernel, first_pass), out_shape=(...]
    add x22 -> x43, other arithmetic: 11 us -> 7.28 us  [the longest x29 3.09 us: scatter(): keep, send = (keep[:half] + got[:half], keep[half:] + got[half:])]
  transfers between devices with their start and end apart: 102 -> 119, of which waited for: 52 -> 60; matrix products, arithmetic and copies ran while one was open for 2% -> 3% of each run, Pallas kernels for 6% -> 3%
where the time goes in v2:
time: 406 us; the launch traced here: 398 us
  starting transfers between devices  186 us (46%)
  waiting for transfers between devices  110 us (27%)
  Pallas kernels  76.6 us (19%)
  other arithmetic  15 us (4%)
  local copies, waits for them, and re-layouts  4.92 us (1%)
    ppermute x101, starting transfers between devices, flip(): lax.ppermute(value, axis, [(i, i ^ mask) for i in range(2 if axis == 'c'...  168 us
    ppermute x101, waiting for transfers between devices, flip(): lax.ppermute(value, axis, [(i, i ^ mask) for i in range(2 if axis == 'c'...  74.7 us
    ppermute x18, waiting for transfers between devices, shift(): return lax.ppermute(value, axis, [(i, (i + amount) % 4) for i in range(4)])  34.9 us
    pallas_call x2, Pallas kernels, inverse_factor(): pl.pallas_call(inverse_factor_kernel, out_shape=jax.ShapeDtypeStruct((siz...  26.6 us
    pallas_call x2, Pallas kernels, forward_call(): pl.pallas_call(functools.partial(forward_kernel, first_pass), out_shape=(...  24.7 us
    pallas_call x2, Pallas kernels, backward_call(): pl.pallas_call(backward_kernel, out_shape=(out,) * 8, grid_spec=pltpu.Pre...  19.6 us
    ppermute x18, starting transfers between devices, shift(): return lax.ppermute(value, axis, [(i, (i + amount) % 4) for i in range(4)])  18.2 us
  transfers between devices with their start and end apart: 119, of which 60 were waited for; matrix products, arithmetic and copies ran while one was open for 3% of the time, Pallas kernels for 3%

profile of v2, /device:TPU:1, one launch (start us, length us, event | category | flops | bytes accessed | tf_op | source)
XLA Modules:
  0.0 398.5 jit_solution(2697422200453647833)
XLA Ops:
  1.0 3.6 collective-permute-start.6
  4.6 2.5 collective-permute-start.2
  13.1 3.3 collective-permute-done.1
  19.8 5.7 %shard_map.55 = f32[16,128]{1,0:T(8,128)} custom-call(s32[1]{0:T(128)} %bitcast.121.count_ref, s32[128]{0:T(128)} %get-tuple-element.112.put_ref, f32[128,128,128]{2,1,0:T(8,128)} %bitcast.135, f32[4,64,256]{2,1,0:T(8,128)} %pad_maximum_fusion.8.refs_0_, f32[4,64,256]{2,1,0:T(8,128)} %pad_maximum_fusion.9.refs_1_, f32[4,64,256]{2,1,0:T(8,128)} %pad_maximum_fusion.10.refs_2_, ...), custom_call_target="tpu_custom_call" | custom-call | flops 10000000000 | bytes 8388608 | tf_op jit(solution)/shard_map/pallas_call | solution.py:115
  26.2 2.7 collective-permute-start.8
  29.7 4.4 %collective-permute-start.9 = (f32[2,2,128]{2,0,1:T(2,128)S(1)}, f32[2,2,128]{2,0,1:T(2,128)S(1)}, u32[]{:S(2)}, u32[]{:S(2)}) collective-permute-start(f32[2,2,128]{2,0,1:T(2,128)S(1)} %copy.6), channel_id=1, source_target_pairs={{0,6},{2,4},{4,2},{6,0},{1,7},{3,5},{5,3},{7,1},{8,14},{10,12},{12... | collective-permute-start | bytes 6152 | tf_op jit(solution)/shard_map/ppermute | solution.py:24
  35.1 2.4 collective-permute-done.10
  39.9 4.4 %collective-permute-start.12 = (f32[2,2,128]{2,0,1:T(2,128)S(1)}, f32[2,2,128]{2,0,1:T(2,128)S(1)}, u32[]{:S(2)}, u32[]{:S(2)}) collective-permute-start(f32[2,2,128]{2,0,1:T(2,128)S(1)} %pad_maximum_fusion.31), channel_id=1, source_target_pairs={{0,96},{32,64},{64,32},{96,0},{1,97},{33,65},{65,33},{97,1},{2,98}... | collective-permute-start | bytes 6152 | tf_op jit(solution)/shard_map/ppermute | solution.py:24
  45.4 2.4 collective-permute-start.16
  50.2 3.0 collective-permute-start.20
  54.9 2.8 collective-permute-done.14
  58.3 3.5 collective-permute-done.20.refs_10_
  62.7 11.5 %shard_map.56 = (f32[8,136,256]{2,1,0:T(8,128)}, f32[8,136,256]{2,1,0:T(8,128)}) custom-call(s32[1]{0:T(128)} %bitcast.122.refs_0_, s32[256]{0:T(256)} %pad_add_fusion.refs_1_, s32[128]{0:T(128)} %get-tuple-element.46.refs_2_, f32[128,128,128]{2,1,0:T(8,128)} %bitcast.136, f32[32,128]{1,0:T(8,128)} %pad_maximum_fusion.28.refs_4_, f32[8,64,256]{2,1,0:T(8,128)} %copy-done.8, ...), custom_call_target="tpu_custom_call" | custom-call | flops 6442450944 | bytes 16777216 | tf_op jit(solution)/shard_map/pallas_call | solution.py:225
  74.3 5.5 %collective-permute-start.23 = (f32[8,136,256]{2,1,0:T(8,128)}, f32[8,136,256]{2,1,0:T(8,128)S(1)}, u32[]{:S(2)}, u32[]{:S(2)}) collective-permute-start(f32[8,136,256]{2,1,0:T(8,128)} %get-tuple-element.26), channel_id=1, source_target_pairs={{0,1},{1,0},{2,3},{3,2},{4,5},{5,4},{6,7},{7,6},{8,9},{9,8},{10,11... | collective-permute-start | bytes 3342344 | tf_op jit(solution)/shard_map/ppermute | solution.py:24
  79.7 2.6 collective-permute-done.23
  85.0 4.0 collective-permute-start.24
  88.9 2.7 collective-permute-done.26
  91.7 5.4 %collective-permute-start.27 = (f32[1,136,256]{2,1,0:T(8,128)S(1)}, f32[1,136,256]{2,1,0:T(8,128)S(1)}, u32[]{:S(2)}, u32[]{:S(2)}) collective-permute-start(f32[1,136,256]{2,1,0:T(8,128)S(1)} %slice_add_fusion.24), channel_id=1, source_target_pairs={{0,6},{2,4},{4,2},{6,0},{1,7},{3,5},{5,3},{7,1},{8,14},{10,12},{12... | collective-permute-start | bytes 417800 | tf_op jit(solution)/shard_map/ppermute | solution.py:24
  97.2 2.7 collective-permute-done.27
  102.7 2.8 collective-permute-done.28
  107.3 5.2 %collective-permute-start.32 = (f32[2,128,256]{2,1,0:T(8,128)S(1)}, f32[2,128,256]{2,1,0:T(8,128)S(1)}, u32[]{:S(2)}, u32[]{:S(2)}) collective-permute-start(f32[2,128,256]{2,1,0:T(8,128)S(1)} %pad_maximum_fusion.12.refs_4_), channel_id=1, source_target_pairs={{0,1},{1,0},{2,3},{3,2},{4,5},{5,4},{6,7},{7,6},{8,9},{9,8},{10,11... | collective-permute-start | bytes 786440 | tf_op jit(solution)/shard_map/ppermute | solution.py:24
  112.5 4.2 %collective-permute-start.33 = (f32[2,128,256]{2,1,0:T(8,128)S(1)}, f32[2,128,256]{2,1,0:T(8,128)S(1)}, u32[]{:S(2)}, u32[]{:S(2)}) collective-permute-start(f32[2,128,256]{2,1,0:T(8,128)S(1)} %collective-permute-done.29.refs_5_), channel_id=1, source_target_pairs={{0,1},{1,0},{2,3},{3,2},{4,5},{5,4},{6,7},{7,6},{8,9},{9,8},{10,11... | collective-permute-start | bytes 786440 | tf_op jit(solution)/shard_map/ppermute | solution.py:24
  119.1 9.8 %shard_map.57 = (f32[8,64,256]{2,1,0:T(8,128)}, f32[8,64,256]{2,1,0:T(8,128)}, f32[8,64,256]{2,1,0:T(8,128)}, f32[8,64,256]{2,1,0:T(8,128)}, f32[8,64,256]{2,1,0...) custom-call(s32[1]{0:T(128)} %bitcast.123.refs_0_, s32[128]{0:T(128)} %get-tuple-element.45.refs_1_, ...), custom_call_target="tpu_custom_call" | custom-call | flops 6442450944 | bytes 16777216 | tf_op jit(solution)/shard_map/pallas_call | solution.py:272
  128.9 3.2 collective-permute-start.36
  132.1 5.6 %collective-permute-start.40 = (f32[8,64,256]{2,1,0:T(8,128)}, f32[8,64,256]{2,1,0:T(8,128)S(1)}, u32[]{:S(2)}, u32[]{:S(2)}) collective-permute-start(f32[8,64,256]{2,1,0:T(8,128)} %get-tuple-element.30), channel_id=1, source_target_pairs={{0,8},{8,0},{16,24},{24,16},{1,9},{9,1},{17,25},{25,17},{2,10},{10... | collective-permute-start | bytes 1572872 | tf_op jit(solution)/shard_map/ppermute | solution.py:24
  137.7 6.6 %collective-permute-done.36 = f32[8,64,256]{2,1,0:T(8,128)S(1)} collective-permute-done((f32[8,64,256]{2,1,0:T(8,128)}, f32[8,64,256]{2,1,0:T(8,128)S(1)}, u32[]{:S(2)}, u32[]{:S(2)}) %collective-permute-start.36) | collective-permute-done | bytes 524320 | tf_op jit(solution)/shard_map/ppermute | solution.py:24
  145.4 2.8 collective-permute-start.37
  148.3 2.4 collective-permute-start.41
  152.6 2.4 collective-permute-done.37
  172.6 3.0 collective-permute-start.52
  189.2 3.9 collective-permute-start.77
  194.6 2.3 collective-permute-start.57
  196.9 2.8 collective-permute-start.69
  202.0 3.8 collective-permute-start.61
  212.4 8.1 %collective-permute-start.62 = (f32[128,256]{1,0:T(8,128)S(1)}, f32[128,256]{1,0:T(8,128)S(1)}, u32[]{:S(2)}, u32[]{:S(2)}) collective-permute-start(f32[128,256]{1,0:T(8,128)S(1)} %add_add_fusion.3), channel_id=1, source_target_pairs={{0,1},{1,0},{2,3},{3,2},{4,5},{5,4},{6,7},{7,6},{8,9},{9,8},{10,11... | collective-permute-start | bytes 393224 | tf_op jit(solution)/shard_map/ppermute | solution.py:24
  222.2 13.3 %shard_map.58.refs_5_ = f32[256,256]{1,0:T(8,128)} custom-call(f32[256,256]{1,0:T(8,128)} %maximum_select_fusion.gram_ref), custom_call_target="tpu_custom_call" | custom-call | flops 17179869184 | bytes 524288 | tf_op jit(solution)/shard_map/pallas_call | solution.py:342
  236.4 13.2 %shard_map.59 = (f32[8,128,256]{2,1,0:T(8,128)}, f32[8,128,256]{2,1,0:T(8,128)}) custom-call(s32[1]{0:T(128)} %bitcast.124.refs_0_, s32[128]{0:T(128)} %get-tuple-element.113.refs_1_, s32[128]{0:T(128)} %get-tuple-element.46.refs_2_, f32[128,128,128]{2,1,0:T(8,128)} %bitcast.138, f32[32,128]{1,0:T(8,128)} %pad_maximum_fusion.28.refs_4_, ...), custom_call_target="tpu_custom_call" | custom-call | flops 6442450944 | bytes 16777216 | tf_op jit(solution)/shard_map/pallas_call | solution.py:225
  249.5 2.9 collective-permute-done.79
  255.5 4.3 %collective-permute-start.80 = (f32[2,128,256]{2,1,0:T(8,128)S(1)}, f32[2,128,256]{2,1,0:T(8,128)S(1)}, u32[]{:S(2)}, u32[]{:S(2)}) collective-permute-start(f32[2,128,256]{2,1,0:T(8,128)S(1)} %get-tuple-element.59), channel_id=1, source_target_pairs={{0,6},{2,4},{4,2},{6,0},{1,7},{3,5},{5,3},{7,1},{8,14},{10,12},{12... | collective-permute-start | bytes 786440 | tf_op jit(solution)/shard_map/ppermute | solution.py:24
  261.9 5.7 %collective-permute-start.83 = (f32[1,128,256]{2,1,0:T(8,128)S(1)}, f32[1,128,256]{2,1,0:T(8,128)S(1)}, u32[]{:S(2)}, u32[]{:S(2)}) collective-permute-start(f32[1,128,256]{2,1,0:T(8,128)S(1)} %slice_add_fusion.36), channel_id=1, source_target_pairs={{0,6},{2,4},{4,2},{6,0},{1,7},{3,5},{5,3},{7,1},{8,14},{10,12},{12... | collective-permute-start | bytes 393224 | tf_op jit(solution)/shard_map/ppermute | solution.py:24
  267.7 2.8 collective-permute-done.83
  273.7 2.4 collective-permute-done.84
  277.9 5.0 %collective-permute-start.88 = (f32[2,128,256]{2,1,0:T(8,128)S(1)}, f32[2,128,256]{2,1,0:T(8,128)S(1)}, u32[]{:S(2)}, u32[]{:S(2)}) collective-permute-start(f32[2,128,256]{2,1,0:T(8,128)S(1)} %pad_maximum_fusion.18.refs_4_), channel_id=1, source_target_pairs={{0,1},{1,0},{2,3},{3,2},{4,5},{5,4},{6,7},{7,6},{8,9},{9,8},{10,11... | collective-permute-start | bytes 786440 | tf_op jit(solution)/shard_map/ppermute | solution.py:24
  282.9 4.2 %collective-permute-start.89 = (f32[2,128,256]{2,1,0:T(8,128)S(1)}, f32[2,128,256]{2,1,0:T(8,128)S(1)}, u32[]{:S(2)}, u32[]{:S(2)}) collective-permute-start(f32[2,128,256]{2,1,0:T(8,128)S(1)} %collective-permute-done.85.refs_5_), channel_id=1, source_target_pairs={{0,1},{1,0},{2,3},{3,2},{4,5},{5,4},{6,7},{7,6},{8,9},{9,8},{10,11... | collective-permute-start | bytes 786440 | tf_op jit(solution)/shard_map/ppermute | solution.py:24
  289.4 9.8 %shard_map.60 = (f32[8,64,256]{2,1,0:T(8,128)}, f32[8,64,256]{2,1,0:T(8,128)}, f32[8,64,256]{2,1,0:T(8,128)}, f32[8,64,256]{2,1,0:T(8,128)}, f32[8,64,256]{2,1,0...) custom-call(s32[1]{0:T(128)} %bitcast.125.refs_0_, s32[128]{0:T(128)} %get-tuple-element.45.refs_1_, ...), custom_call_target="tpu_custom_call" | custom-call | flops 6442450944 | bytes 16777216 | tf_op jit(solution)/shard_map/pallas_call | solution.py:272
  299.2 2.3 collective-permute-start.92
  301.6 3.3 collective-permute-start.96
  305.6 3.0 collective-permute-start.104
  308.5 6.0 %collective-permute-done.92 = f32[8,64,256]{2,1,0:T(8,128)S(1)} collective-permute-done((f32[8,64,256]{2,1,0:T(8,128)}, f32[8,64,256]{2,1,0:T(8,128)S(1)}, u32[]{:S(2)}, u32[]{:S(2)}) %collective-permute-start.92) | collective-permute-done | bytes 524320 | tf_op jit(solution)/shard_map/ppermute | solution.py:24
  318.2 2.8 collective-permute-start.101
  321.0 2.6 collective-permute-start.105
  323.6 3.8 collective-permute-start.94
  332.1 2.3 collective-permute-start.99
  334.4 2.7 collective-permute-start.103
  339.1 2.5 collective-permute-done.107
  342.3 2.7 collective-permute-start.108
  351.0 3.1 collective-permute-done.110
  354.1 3.8 collective-permute-done.109
  359.8 2.7 collective-permute-done.114
  362.5 2.5 collective-permute-done.113
  365.0 3.3 collective-permute-done.112
  373.3 2.5 collective-permute-done.116
  375.9 4.0 %collective-permute-done.115 = f32[128,256]{1,0:T(8,128)S(1)} collective-permute-done((f32[128,256]{1,0:T(8,128)S(1)}, f32[128,256]{1,0:T(8,128)S(1)}, u32[]{:S(2)}, u32[]{:S(2)}) %collective-permute-start.115) | collective-permute-done | bytes 131104 | tf_op jit(solution)/shard_map/ppermute | solution.py:48
  382.6 13.3 %shard_map.61 = f32[256,256]{1,0:T(8,128)} custom-call(f32[256,256]{1,0:T(8,128)} %maximum_select_fusion.1.gram_ref), custom_call_target="tpu_custom_call" | custom-call | flops 17179869184 | bytes 524288 | tf_op jit(solution)/shard_map/pallas_call | solution.py:342
  (375 shorter events, 120.0 us)
Async XLA Ops:
  1.0 8.7 %collective-permute-start.6 = (f32[1,64,256]{2,1,0:T(8,128)S(1)}, f32[1,64,256]{2,1,0:T(8,128)S(1)}, u32[]{:S(2)}, u32[]{:S(2)}) collective-permute-start(f32[1,64,256]{2,1,0:T(8,128)S(1)} %get-tuple-element.100), channel_id=1, source_target_pairs={{0,24},{8,16},{16,8},{24,0},{1,25},{9,17},{17,9},{25,1},{2,26},{10... | collective-permute-start | bytes 196616 | tf_op jit(solution)/shard_map/ppermute | solution.py:24
  4.6 8.3 %collective-permute-start.4 = (f32[1,64,256]{2,1,0:T(8,128)S(1)}, f32[1,64,256]{2,1,0:T(8,128)S(1)}, u32[]{:S(2)}, u32[]{:S(2)}) collective-permute-start(f32[1,64,256]{2,1,0:T(8,128)S(1)} %get-tuple-element.101), channel_id=1, source_target_pairs={{0,8},{8,0},{16,24},{24,16},{1,9},{9,1},{17,25},{25,17},{2,10},{10... | collective-permute-start | bytes 196616 | tf_op jit(solution)/shard_map/ppermute | solution.py:24
  4.6 7.5 %collective-permute-start.2 = (f32[1,64,256]{2,1,0:T(8,128)S(1)}, f32[1,64,256]{2,1,0:T(8,128)S(1)}, u32[]{:S(2)}, u32[]{:S(2)}) collective-permute-start(f32[1,64,256]{2,1,0:T(8,128)S(1)} %get-tuple-element.102), channel_id=1, source_target_pairs={{0,96},{32,64},{64,32},{96,0},{1,97},{33,65},{65,33},{97,1},{2,98}... | collective-permute-start | bytes 196616 | tf_op jit(solution)/shard_map/ppermute | solution.py:24
  9.7 9.4 %collective-permute-start.7 = (f32[2,64,256]{2,1,0:T(8,128)S(1)}, f32[2,64,256]{2,1,0:T(8,128)S(1)}, u32[]{:S(2)}, u32[]{:S(2)}) collective-permute-start(f32[2,64,256]{2,1,0:T(8,128)S(1)} %pad_maximum_fusion.23), channel_id=1, source_target_pairs={{0,8},{8,0},{16,24},{24,16},{1,9},{9,1},{17,25},{25,17},{2,10},{10... | collective-permute-start | bytes 393224 | tf_op jit(solution)/shard_map/ppermute | solution.py:24
  38.6 9.3 %collective-permute-start.17 = (f32[4,64,256]{2,1,0:T(8,128)S(1)}, f32[4,64,256]{2,1,0:T(8,128)S(1)}, u32[]{:S(2)}, u32[]{:S(2)}) collective-permute-start(f32[4,64,256]{2,1,0:T(8,128)S(1)} %copy-done.17), channel_id=1, source_target_pairs={{0,24},{8,16},{16,8},{24,0},{1,25},{9,17},{17,9},{25,1},{2,26},{10... | collective-permute-start | bytes 786440 | tf_op jit(solution)/shard_map/ppermute | solution.py:24
  38.6 6.8 %collective-permute-start.15 = (f32[4,64,256]{2,1,0:T(8,128)S(1)}, f32[4,64,256]{2,1,0:T(8,128)S(1)}, u32[]{:S(2)}, u32[]{:S(2)}) collective-permute-start(f32[4,64,256]{2,1,0:T(8,128)S(1)} %copy-done.18), channel_id=1, source_target_pairs={{0,8},{8,0},{16,24},{24,16},{1,9},{9,1},{17,25},{25,17},{2,10},{10... | collective-permute-start | bytes 786440 | tf_op jit(solution)/shard_map/ppermute | solution.py:24
  44.8 8.3 %collective-permute-start.21 = (f32[4,64,256]{2,1,0:T(8,128)S(1)}, f32[4,64,256]{2,1,0:T(8,128)S(1)}, u32[]{:S(2)}, u32[]{:S(2)}) collective-permute-start(f32[4,64,256]{2,1,0:T(8,128)S(1)} %copy-done.15), channel_id=1, source_target_pairs={{0,96},{32,64},{64,32},{96,0},{1,97},{33,65},{65,33},{97,1},{2,98}... | collective-permute-start | bytes 786440 | tf_op jit(solution)/shard_map/ppermute | solution.py:24
  45.3 8.1 %collective-permute-start.13 = (f32[4,2,128]{2,0,1:T(4,128)S(1)}, f32[4,2,128]{2,0,1:T(4,128)S(1)}, u32[]{:S(2)}, u32[]{:S(2)}) collective-permute-start(f32[4,2,128]{2,0,1:T(4,128)S(1)} %pad_maximum_fusion.30), channel_id=1, source_target_pairs={{0,8},{8,0},{16,24},{24,16},{1,9},{9,1},{17,25},{25,17},{2,10},{10... | collective-permute-start | bytes 12296 | tf_op jit(solution)/shard_map/ppermute | solution.py:24
  45.4 12.9 %collective-permute-start.16 = (f32[8,64,256]{2,1,0:T(8,128)S(1)}, f32[8,64,256]{2,1,0:T(8,128)}, u32[]{:S(2)}, u32[]{:S(2)}) collective-permute-start(f32[8,64,256]{2,1,0:T(8,128)S(1)} %pad_maximum_fusion.refs_5_), channel_id=1, source_target_pairs={{0,24},{8,16},{16,8},{24,0},{1,25},{9,17},{17,9},{25,1},{2,26},{10... | collective-permute-start | bytes 1572872 | tf_op jit(solution)/shard_map/ppermute | solution.py:24
  47.9 10.5 %collective-permute-start.18 = (f32[8,64,256]{2,1,0:T(8,128)S(1)}, f32[8,64,256]{2,1,0:T(8,128)}, u32[]{:S(2)}, u32[]{:S(2)}) collective-permute-start(f32[8,64,256]{2,1,0:T(8,128)S(1)} %pad_maximum_fusion.1.refs_7_), channel_id=1, source_target_pairs={{0,8},{8,0},{16,24},{24,16},{1,9},{9,1},{17,25},{25,17},{2,10},{10... | collective-permute-start | bytes 1572872 | tf_op jit(solution)/shard_map/ppermute | solution.py:24
  50.2 11.7 %collective-permute-start.20 = (f32[8,64,256]{2,1,0:T(8,128)S(1)}, f32[8,64,256]{2,1,0:T(8,128)}, u32[]{:S(2)}, u32[]{:S(2)}) collective-permute-start(f32[8,64,256]{2,1,0:T(8,128)S(1)} %pad_maximum_fusion.2.refs_9_), channel_id=1, source_target_pairs={{0,96},{32,64},{64,32},{96,0},{1,97},{33,65},{65,33},{97,1},{2,98}... | collective-permute-start | bytes 1572872 | tf_op jit(solution)/shard_map/ppermute | solution.py:24
  53.2 8.7 %collective-permute-start.22 = (f32[8,64,256]{2,1,0:T(8,128)S(1)}, f32[8,64,256]{2,1,0:T(8,128)S(1)}, u32[]{:S(2)}, u32[]{:S(2)}) collective-permute-start(f32[8,64,256]{2,1,0:T(8,128)S(1)} %pad_maximum_fusion.3.refs_11_), channel_id=1, source_target_pairs={{0,32},{32,0},{64,96},{96,64},{1,33},{33,1},{65,97},{97,65},{2,34}... | collective-permute-start | bytes 1572872 | tf_op jit(solution)/shard_map/ppermute | solution.py:24
  74.3 8.1 %collective-permute-start.23 = (f32[8,136,256]{2,1,0:T(8,128)}, f32[8,136,256]{2,1,0:T(8,128)S(1)}, u32[]{:S(2)}, u32[]{:S(2)}) collective-permute-start(f32[8,136,256]{2,1,0:T(8,128)} %get-tuple-element.26), channel_id=1, source_target_pairs={{0,1},{1,0},{2,3},{3,2},{4,5},{5,4},{6,7},{7,6},{8,9},{9,8},{10,11... | collective-permute-start | bytes 3342344 | tf_op jit(solution)/shard_map/ppermute | solution.py:24
  83.7 8.0 %collective-permute-start.26 = (f32[2,136,256]{2,1,0:T(8,128)S(1)}, f32[2,136,256]{2,1,0:T(8,128)S(1)}, u32[]{:S(2)}, u32[]{:S(2)}) collective-permute-start(f32[2,136,256]{2,1,0:T(8,128)S(1)} %get-tuple-element.53), channel_id=1, source_target_pairs={{0,2},{2,0},{4,6},{6,4},{1,3},{3,1},{5,7},{7,5},{8,10},{10,8},{12,... | collective-permute-start | bytes 835592 | tf_op jit(solution)/shard_map/ppermute | solution.py:24
  85.0 12.1 %collective-permute-start.24 = (f32[2,136,256]{2,1,0:T(8,128)S(1)}, f32[2,136,256]{2,1,0:T(8,128)S(1)}, u32[]{:S(2)}, u32[]{:S(2)}) collective-permute-start(f32[2,136,256]{2,1,0:T(8,128)S(1)} %get-tuple-element.55), channel_id=1, source_target_pairs={{0,6},{2,4},{4,2},{6,0},{1,7},{3,5},{5,3},{7,1},{8,14},{10,12},{12... | collective-permute-start | bytes 835592 | tf_op jit(solution)/shard_map/ppermute | solution.py:24
  91.7 8.2 %collective-permute-start.27 = (f32[1,136,256]{2,1,0:T(8,128)S(1)}, f32[1,136,256]{2,1,0:T(8,128)S(1)}, u32[]{:S(2)}, u32[]{:S(2)}) collective-permute-start(f32[1,136,256]{2,1,0:T(8,128)S(1)} %slice_add_fusion.24), channel_id=1, source_target_pairs={{0,6},{2,4},{4,2},{6,0},{1,7},{3,5},{5,3},{7,1},{8,14},{10,12},{12... | collective-permute-start | bytes 417800 | tf_op jit(solution)/shard_map/ppermute | solution.py:24
  105.5 7.0 %collective-permute-start.29 = (f32[2,128,256]{2,1,0:T(8,128)S(1)}, f32[2,128,256]{2,1,0:T(8,128)S(1)}, u32[]{:S(2)}, u32[]{:S(2)}) collective-permute-start(f32[2,128,256]{2,1,0:T(8,128)S(1)} %pad_maximum_fusion.12.refs_4_), channel_id=1, source_target_pairs={{0,6},{2,4},{4,2},{6,0},{1,7},{3,5},{5,3},{7,1},{8,14},{10,12},{12... | collective-permute-start | bytes 786440 | tf_op jit(solution)/shard_map/ppermute | solution.py:24
  106.8 9.9 %collective-permute-start.31 = (f32[2,128,256]{2,1,0:T(8,128)S(1)}, f32[2,128,256]{2,1,0:T(8,128)S(1)}, u32[]{:S(2)}, u32[]{:S(2)}) collective-permute-start(f32[2,128,256]{2,1,0:T(8,128)S(1)} %pad_maximum_fusion.13.refs_6_), channel_id=1, source_target_pairs={{0,2},{2,0},{4,6},{6,4},{1,3},{3,1},{5,7},{7,5},{8,10},{10,8},{12,... | collective-permute-start | bytes 786440 | tf_op jit(solution)/shard_map/ppermute | solution.py:24
  107.3 9.9 %collective-permute-start.32 = (f32[2,128,256]{2,1,0:T(8,128)S(1)}, f32[2,128,256]{2,1,0:T(8,128)S(1)}, u32[]{:S(2)}, u32[]{:S(2)}) collective-permute-start(f32[2,128,256]{2,1,0:T(8,128)S(1)} %pad_maximum_fusion.12.refs_4_), channel_id=1, source_target_pairs={{0,1},{1,0},{2,3},{3,2},{4,5},{5,4},{6,7},{7,6},{8,9},{9,8},{10,11... | collective-permute-start | bytes 786440 | tf_op jit(solution)/shard_map/ppermute | solution.py:24
  128.9 15.4 %collective-permute-start.36 = (f32[8,64,256]{2,1,0:T(8,128)}, f32[8,64,256]{2,1,0:T(8,128)S(1)}, u32[]{:S(2)}, u32[]{:S(2)}) collective-permute-start(f32[8,64,256]{2,1,0:T(8,128)} %get-tuple-element.28), channel_id=1, source_target_pairs={{0,24},{8,16},{16,8},{24,0},{1,25},{9,17},{17,9},{25,1},{2,26},{10... | collective-permute-start | bytes 1572872 | tf_op jit(solution)/shard_map/ppermute | solution.py:24
  132.1 16.2 %collective-permute-start.40 = (f32[8,64,256]{2,1,0:T(8,128)}, f32[8,64,256]{2,1,0:T(8,128)S(1)}, u32[]{:S(2)}, u32[]{:S(2)}) collective-permute-start(f32[8,64,256]{2,1,0:T(8,128)} %get-tuple-element.30), channel_id=1, source_target_pairs={{0,8},{8,0},{16,24},{24,16},{1,9},{9,1},{17,25},{25,17},{2,10},{10... | collective-permute-start | bytes 1572872 | tf_op jit(solution)/shard_map/ppermute | solution.py:24
  137.7 13.0 %collective-permute-start.44 = (f32[8,64,256]{2,1,0:T(8,128)}, f32[8,64,256]{2,1,0:T(8,128)S(1)}, u32[]{:S(2)}, u32[]{:S(2)}) collective-permute-start(f32[8,64,256]{2,1,0:T(8,128)} %get-tuple-element.32), channel_id=1, source_target_pairs={{0,96},{32,64},{64,32},{96,0},{1,97},{33,65},{65,33},{97,1},{2,98}... | collective-permute-start | bytes 1572872 | tf_op jit(solution)/shard_map/ppermute | solution.py:24
  137.7 13.2 %collective-permute-start.48 = (f32[8,64,256]{2,1,0:T(8,128)}, f32[8,64,256]{2,1,0:T(8,128)S(1)}, u32[]{:S(2)}, u32[]{:S(2)}) collective-permute-start(f32[8,64,256]{2,1,0:T(8,128)} %get-tuple-element.34), channel_id=1, source_target_pairs={{0,32},{32,0},{64,96},{96,64},{1,33},{33,1},{65,97},{97,65},{2,34}... | collective-permute-start | bytes 1572872 | tf_op jit(solution)/shard_map/ppermute | solution.py:24
  145.4 9.6 %collective-permute-start.37 = (f32[4,64,256]{2,1,0:T(8,128)S(1)}, f32[4,64,256]{2,1,0:T(8,128)S(1)}, u32[]{:S(2)}, u32[]{:S(2)}) collective-permute-start(f32[4,64,256]{2,1,0:T(8,128)S(1)} %get-tuple-element.69), channel_id=1, source_target_pairs={{0,8},{8,0},{16,24},{24,16},{1,9},{9,1},{17,25},{25,17},{2,10},{10... | collective-permute-start | bytes 786440 | tf_op jit(solution)/shard_map/ppermute | solution.py:24
  148.3 8.7 %collective-permute-start.41 = (f32[4,64,256]{2,1,0:T(8,128)S(1)}, f32[4,64,256]{2,1,0:T(8,128)S(1)}, u32[]{:S(2)}, u32[]{:S(2)}) collective-permute-start(f32[4,64,256]{2,1,0:T(8,128)S(1)} %get-tuple-element.71), channel_id=1, source_target_pairs={{0,24},{8,16},{16,8},{24,0},{1,25},{9,17},{17,9},{25,1},{2,26},{10... | collective-permute-start | bytes 786440 | tf_op jit(solution)/shard_map/ppermute | solution.py:24
  150.8 8.3 %collective-permute-start.45 = (f32[4,64,256]{2,1,0:T(8,128)S(1)}, f32[4,64,256]{2,1,0:T(8,128)S(1)}, u32[]{:S(2)}, u32[]{:S(2)}) collective-permute-start(f32[4,64,256]{2,1,0:T(8,128)S(1)} %get-tuple-element.73), channel_id=1, source_target_pairs={{0,32},{32,0},{64,96},{96,64},{1,33},{33,1},{65,97},{97,65},{2,34}... | collective-permute-start | bytes 786440 | tf_op jit(solution)/shard_map/ppermute | solution.py:24
  151.0 8.5 %collective-permute-start.49 = (f32[4,64,256]{2,1,0:T(8,128)S(1)}, f32[4,64,256]{2,1,0:T(8,128)S(1)}, u32[]{:S(2)}, u32[]{:S(2)}) collective-permute-start(f32[4,64,256]{2,1,0:T(8,128)S(1)} %get-tuple-element.75), channel_id=1, source_target_pairs={{0,96},{32,64},{64,32},{96,0},{1,97},{33,65},{65,33},{97,1},{2,98}... | collective-permute-start | bytes 786440 | tf_op jit(solution)/shard_map/ppermute | solution.py:24
  155.1 6.9 %collective-permute-start.38 = (f32[2,64,256]{2,1,0:T(8,128)S(1)}, f32[2,64,256]{2,1,0:T(8,128)S(1)}, u32[]{:S(2)}, u32[]{:S(2)}) collective-permute-start(f32[2,64,256]{2,1,0:T(8,128)S(1)} %get-tuple-element.85), channel_id=1, source_target_pairs={{0,96},{32,64},{64,32},{96,0},{1,97},{33,65},{65,33},{97,1},{2,98}... | collective-permute-start | bytes 393224 | tf_op jit(solution)/shard_map/ppermute | solution.py:24
  170.6 6.9 %collective-permute-start.75 = (f32[1,64,256]{2,1,0:T(8,128)S(1)}, f32[1,64,256]{2,1,0:T(8,128)S(1)}, u32[]{:S(2)}, u32[]{:S(2)}) collective-permute-start(f32[1,64,256]{2,1,0:T(8,128)S(1)} %get-tuple-element.94), channel_id=1, source_target_pairs={{0,24},{8,16},{16,8},{24,0},{1,25},{9,17},{17,9},{25,1},{2,26},{10... | collective-permute-start | bytes 196616 | tf_op jit(solution)/shard_map/ppermute | solution.py:24
  172.6 9.6 %collective-permute-start.52 = (f32[128,256]{1,0:T(8,128)S(1)}, f32[128,256]{1,0:T(8,128)S(1)}, u32[]{:S(2)}, u32[]{:S(2)}) collective-permute-start(f32[128,256]{1,0:T(8,128)S(1)} %constant_dynamic-slice_fusion.1), channel_id=1, source_target_pairs={{0,1},{1,0},{2,3},{3,2},{4,5},{5,4},{6,7},{7,6},{8,9},{9,8},{10,11... | collective-permute-start | bytes 393224 | tf_op jit(solution)/shard_map/ppermute | solution.py:24
  177.5 8.9 %collective-permute-start.76 = (f32[2,64,256]{2,1,0:T(8,128)S(1)}, f32[2,64,256]{2,1,0:T(8,128)S(1)}, u32[]{:S(2)}, u32[]{:S(2)}) collective-permute-start(f32[2,64,256]{2,1,0:T(8,128)S(1)} %pad_maximum_fusion.27), channel_id=1, source_target_pairs={{0,8},{8,0},{16,24},{24,16},{1,9},{9,1},{17,25},{25,17},{2,10},{10... | collective-permute-start | bytes 393224 | tf_op jit(solution)/shard_map/ppermute | solution.py:24
  179.3 17.7 %collective-permute-start.72 = (f32[2,64,256]{2,1,0:T(8,128)S(1)}, f32[2,64,256]{2,1,0:T(8,128)S(1)}, u32[]{:S(2)}, u32[]{:S(2)}) collective-permute-start(f32[2,64,256]{2,1,0:T(8,128)S(1)} %pad_maximum_fusion.26), channel_id=1, source_target_pairs={{0,24},{8,16},{16,8},{24,0},{1,25},{9,17},{17,9},{25,1},{2,26},{10... | collective-permute-start | bytes 393224 | tf_op jit(solution)/shard_map/ppermute | solution.py:24
  182.2 6.9 %collective-permute-start.55 = (f32[128,256]{1,0:T(8,128)S(1)}, f32[128,256]{1,0:T(8,128)S(1)}, u32[]{:S(2)}, u32[]{:S(2)}) collective-permute-start(f32[128,256]{1,0:T(8,128)S(1)} %dynamic-slice_add_fusion.1), channel_id=1, source_target_pairs={{0,96},{32,0},{64,32},{96,64},{1,97},{33,1},{65,33},{97,65},{2,98}... | collective-permute-start | bytes 393224 | tf_op jit(solution)/shard_map/ppermute | solution.py:48
  184.2 8.9 %collective-permute-start.54 = (f32[128,256]{1,0:T(8,128)S(1)}, f32[128,256]{1,0:T(8,128)S(1)}, u32[]{:S(2)}, u32[]{:S(2)}) collective-permute-start(f32[128,256]{1,0:T(8,128)S(1)} %dynamic-slice_add_fusion.1), channel_id=1, source_target_pairs={{0,64},{32,96},{64,0},{96,32},{1,65},{33,97},{65,1},{97,33},{2,66}... | collective-permute-start | bytes 393224 | tf_op jit(solution)/shard_map/ppermute | solution.py:48
  186.4 10.5 %collective-permute-start.68 = (f32[2,64,256]{2,1,0:T(8,128)S(1)}, f32[2,64,256]{2,1,0:T(8,128)S(1)}, u32[]{:S(2)}, u32[]{:S(2)}) collective-permute-start(f32[2,64,256]{2,1,0:T(8,128)S(1)} %pad_maximum_fusion.25), channel_id=1, source_target_pairs={{0,32},{32,0},{64,96},{96,64},{1,33},{33,1},{65,97},{97,65},{2,34}... | collective-permute-start | bytes 393224 | tf_op jit(solution)/shard_map/ppermute | solution.py:24
  189.2 31.8 %collective-permute-start.77 = (f32[4,64,256]{2,1,0:T(8,128)S(1)}, f32[4,64,256]{2,1,0:T(8,128)S(1)}, u32[]{:S(2)}, u32[]{:S(2)}) collective-permute-start(f32[4,64,256]{2,1,0:T(8,128)S(1)} %pad_maximum_fusion.17), channel_id=1, source_target_pairs={{0,96},{32,64},{64,32},{96,0},{1,97},{33,65},{65,33},{97,1},{2,98}... | collective-permute-start | bytes 786440 | tf_op jit(solution)/shard_map/ppermute | solution.py:24
  196.9 9.0 %collective-permute-start.69 = (f32[4,64,256]{2,1,0:T(8,128)S(1)}, f32[4,64,256]{2,1,0:T(8,128)S(1)}, u32[]{:S(2)}, u32[]{:S(2)}) collective-permute-start(f32[4,64,256]{2,1,0:T(8,128)S(1)} %pad_maximum_fusion.15), channel_id=1, source_target_pairs={{0,24},{8,16},{16,8},{24,0},{1,25},{9,17},{17,9},{25,1},{2,26},{10... | collective-permute-start | bytes 786440 | tf_op jit(solution)/shard_map/ppermute | solution.py:24
  199.7 7.2 %collective-permute-start.65 = (f32[4,64,256]{2,1,0:T(8,128)S(1)}, f32[4,64,256]{2,1,0:T(8,128)S(1)}, u32[]{:S(2)}, u32[]{:S(2)}) collective-permute-start(f32[4,64,256]{2,1,0:T(8,128)S(1)} %pad_maximum_fusion.14), channel_id=1, source_target_pairs={{0,8},{8,0},{16,24},{24,16},{1,9},{9,1},{17,25},{25,17},{2,10},{10... | collective-permute-start | bytes 786440 | tf_op jit(solution)/shard_map/ppermute | solution.py:24
  202.0 7.2 %collective-permute-start.61 = (f32[128,256]{1,0:T(8,128)S(1)}, f32[128,256]{1,0:T(8,128)S(1)}, u32[]{:S(2)}, u32[]{:S(2)}) collective-permute-start(f32[128,256]{1,0:T(8,128)S(1)} %add_add_fusion.4), channel_id=1, source_target_pairs={{0,6},{2,0},{4,2},{6,4},{1,7},{3,1},{5,3},{7,5},{8,14},{10,8},{12,... | collective-permute-start | bytes 393224 | tf_op jit(solution)/shard_map/ppermute | solution.py:48
  207.0 13.5 %collective-permute-start.73 = (f32[4,64,256]{2,1,0:T(8,128)S(1)}, f32[4,64,256]{2,1,0:T(8,128)S(1)}, u32[]{:S(2)}, u32[]{:S(2)}) collective-permute-start(f32[4,64,256]{2,1,0:T(8,128)S(1)} %pad_maximum_fusion.16), channel_id=1, source_target_pairs={{0,32},{32,0},{64,96},{96,64},{1,33},{33,1},{65,97},{97,65},{2,34}... | collective-permute-start | bytes 786440 | tf_op jit(solution)/shard_map/ppermute | solution.py:24
  209.1 26.4 %collective-permute-start.66 = (f32[8,64,256]{2,1,0:T(8,128)S(1)}, f32[8,64,256]{2,1,0:T(8,128)S(1)}, u32[]{:S(2)}, u32[]{:S(2)}) collective-permute-start(f32[8,64,256]{2,1,0:T(8,128)S(1)} %pad_maximum_fusion.4.refs_6_), channel_id=1, source_target_pairs={{0,24},{8,16},{16,8},{24,0},{1,25},{9,17},{17,9},{25,1},{2,26},{10... | collective-permute-start | bytes 1572872 | tf_op jit(solution)/shard_map/ppermute | solution.py:24
  211.3 24.3 %collective-permute-start.70 = (f32[8,64,256]{2,1,0:T(8,128)S(1)}, f32[8,64,256]{2,1,0:T(8,128)}, u32[]{:S(2)}, u32[]{:S(2)}) collective-permute-start(f32[8,64,256]{2,1,0:T(8,128)S(1)} %pad_maximum_fusion.5.refs_8_), channel_id=1, source_target_pairs={{0,8},{8,0},{16,24},{24,16},{1,9},{9,1},{17,25},{25,17},{2,10},{10... | collective-permute-start | bytes 1572872 | tf_op jit(solution)/shard_map/ppermute | solution.py:24
  212.4 9.0 %collective-permute-start.62 = (f32[128,256]{1,0:T(8,128)S(1)}, f32[128,256]{1,0:T(8,128)S(1)}, u32[]{:S(2)}, u32[]{:S(2)}) collective-permute-start(f32[128,256]{1,0:T(8,128)S(1)} %add_add_fusion.3), channel_id=1, source_target_pairs={{0,1},{1,0},{2,3},{3,2},{4,5},{5,4},{6,7},{7,6},{8,9},{9,8},{10,11... | collective-permute-start | bytes 393224 | tf_op jit(solution)/shard_map/ppermute | solution.py:24
  220.6 15.0 %collective-permute-start.74 = (f32[8,64,256]{2,1,0:T(8,128)S(1)}, f32[8,64,256]{2,1,0:T(8,128)}, u32[]{:S(2)}, u32[]{:S(2)}) collective-permute-start(f32[8,64,256]{2,1,0:T(8,128)S(1)} %pad_maximum_fusion.6.refs_10_), channel_id=1, source_target_pairs={{0,96},{32,64},{64,32},{96,0},{1,97},{33,65},{65,33},{97,1},{2,98}... | collective-permute-start | bytes 1572872 | tf_op jit(solution)/shard_map/ppermute | solution.py:24
  221.0 14.6 %collective-permute-start.78 = (f32[8,64,256]{2,1,0:T(8,128)S(1)}, f32[8,64,256]{2,1,0:T(8,128)}, u32[]{:S(2)}, u32[]{:S(2)}) collective-permute-start(f32[8,64,256]{2,1,0:T(8,128)S(1)} %pad_maximum_fusion.7.refs_12_), channel_id=1, source_target_pairs={{0,32},{32,0},{64,96},{96,64},{1,33},{33,1},{65,97},{97,65},{2,34}... | collective-permute-start | bytes 1572872 | tf_op jit(solution)/shard_map/ppermute | solution.py:24
  253.8 8.2 %collective-permute-start.82 = (f32[2,128,256]{2,1,0:T(8,128)S(1)}, f32[2,128,256]{2,1,0:T(8,128)S(1)}, u32[]{:S(2)}, u32[]{:S(2)}) collective-permute-start(f32[2,128,256]{2,1,0:T(8,128)S(1)} %get-tuple-element.57), channel_id=1, source_target_pairs={{0,2},{2,0},{4,6},{6,4},{1,3},{3,1},{5,7},{7,5},{8,10},{10,8},{12,... | collective-permute-start | bytes 786440 | tf_op jit(solution)/shard_map/ppermute | solution.py:24
  255.5 12.1 %collective-permute-start.80 = (f32[2,128,256]{2,1,0:T(8,128)S(1)}, f32[2,128,256]{2,1,0:T(8,128)S(1)}, u32[]{:S(2)}, u32[]{:S(2)}) collective-permute-start(f32[2,128,256]{2,1,0:T(8,128)S(1)} %get-tuple-element.59), channel_id=1, source_target_pairs={{0,6},{2,4},{4,2},{6,0},{1,7},{3,5},{5,3},{7,1},{8,14},{10,12},{12... | collective-permute-start | bytes 786440 | tf_op jit(solution)/shard_map/ppermute | solution.py:24
  261.9 8.6 %collective-permute-start.83 = (f32[1,128,256]{2,1,0:T(8,128)S(1)}, f32[1,128,256]{2,1,0:T(8,128)S(1)}, u32[]{:S(2)}, u32[]{:S(2)}) collective-permute-start(f32[1,128,256]{2,1,0:T(8,128)S(1)} %slice_add_fusion.36), channel_id=1, source_target_pairs={{0,6},{2,4},{4,2},{6,0},{1,7},{3,5},{5,3},{7,1},{8,14},{10,12},{12... | collective-permute-start | bytes 393224 | tf_op jit(solution)/shard_map/ppermute | solution.py:24
  276.1 6.8 %collective-permute-start.85 = (f32[2,128,256]{2,1,0:T(8,128)S(1)}, f32[2,128,256]{2,1,0:T(8,128)S(1)}, u32[]{:S(2)}, u32[]{:S(2)}) collective-permute-start(f32[2,128,256]{2,1,0:T(8,128)S(1)} %pad_maximum_fusion.18.refs_4_), channel_id=1, source_target_pairs={{0,6},{2,4},{4,2},{6,0},{1,7},{3,5},{5,3},{7,1},{8,14},{10,12},{12... | collective-permute-start | bytes 786440 | tf_op jit(solution)/shard_map/ppermute | solution.py:24
  277.6 9.6 %collective-permute-start.87 = (f32[2,128,256]{2,1,0:T(8,128)S(1)}, f32[2,128,256]{2,1,0:T(8,128)S(1)}, u32[]{:S(2)}, u32[]{:S(2)}) collective-permute-start(f32[2,128,256]{2,1,0:T(8,128)S(1)} %pad_maximum_fusion.19.refs_6_), channel_id=1, source_target_pairs={{0,2},{2,0},{4,6},{6,4},{1,3},{3,1},{5,7},{7,5},{8,10},{10,8},{12,... | collective-permute-start | bytes 786440 | tf_op jit(solution)/shard_map/ppermute | solution.py:24
  277.9 9.6 %collective-permute-start.88 = (f32[2,128,256]{2,1,0:T(8,128)S(1)}, f32[2,128,256]{2,1,0:T(8,128)S(1)}, u32[]{:S(2)}, u32[]{:S(2)}) collective-permute-start(f32[2,128,256]{2,1,0:T(8,128)S(1)} %pad_maximum_fusion.18.refs_4_), channel_id=1, source_target_pairs={{0,1},{1,0},{2,3},{3,2},{4,5},{5,4},{6,7},{7,6},{8,9},{9,8},{10,11... | collective-permute-start | bytes 786440 | tf_op jit(solution)/shard_map/ppermute | solution.py:24
  299.2 15.3 %collective-permute-start.92 = (f32[8,64,256]{2,1,0:T(8,128)}, f32[8,64,256]{2,1,0:T(8,128)S(1)}, u32[]{:S(2)}, u32[]{:S(2)}) collective-permute-start(f32[8,64,256]{2,1,0:T(8,128)} %get-tuple-element.38), channel_id=1, source_target_pairs={{0,24},{8,16},{16,8},{24,0},{1,25},{9,17},{17,9},{25,1},{2,26},{10... | collective-permute-start | bytes 1572872 | tf_op jit(solution)/shard_map/ppermute | solution.py:24
  301.6 15.3 %collective-permute-start.96 = (f32[8,64,256]{2,1,0:T(8,128)}, f32[8,64,256]{2,1,0:T(8,128)S(1)}, u32[]{:S(2)}, u32[]{:S(2)}) collective-permute-start(f32[8,64,256]{2,1,0:T(8,128)} %get-tuple-element.40), channel_id=1, source_target_pairs={{0,8},{8,0},{16,24},{24,16},{1,9},{9,1},{17,25},{25,17},{2,10},{10... | collective-permute-start | bytes 1572872 | tf_op jit(solution)/shard_map/ppermute | solution.py:24
  304.8 13.2 %collective-permute-start.100 = (f32[8,64,256]{2,1,0:T(8,128)}, f32[8,64,256]{2,1,0:T(8,128)S(1)}, u32[]{:S(2)}, u32[]{:S(2)}) collective-permute-start(f32[8,64,256]{2,1,0:T(8,128)} %get-tuple-element.42), channel_id=1, source_target_pairs={{0,96},{32,64},{64,32},{96,0},{1,97},{33,65},{65,33},{97,1},{2,98}... | collective-permute-start | bytes 1572872 | tf_op jit(solution)/shard_map/ppermute | solution.py:24
  305.6 15.4 %collective-permute-start.104 = (f32[8,64,256]{2,1,0:T(8,128)}, f32[8,64,256]{2,1,0:T(8,128)S(1)}, u32[]{:S(2)}, u32[]{:S(2)}) collective-permute-start(f32[8,64,256]{2,1,0:T(8,128)} %get-tuple-element.44), channel_id=1, source_target_pairs={{0,32},{32,0},{64,96},{96,64},{1,33},{33,1},{65,97},{97,65},{2,34}... | collective-permute-start | bytes 1572872 | tf_op jit(solution)/shard_map/ppermute | solution.py:24
  315.6 8.0 %collective-permute-start.93 = (f32[4,64,256]{2,1,0:T(8,128)S(1)}, f32[4,64,256]{2,1,0:T(8,128)S(1)}, u32[]{:S(2)}, u32[]{:S(2)}) collective-permute-start(f32[4,64,256]{2,1,0:T(8,128)S(1)} %get-tuple-element.61), channel_id=1, source_target_pairs={{0,8},{8,0},{16,24},{24,16},{1,9},{9,1},{17,25},{25,17},{2,10},{10... | collective-permute-start | bytes 786440 | tf_op jit(solution)/shard_map/ppermute | solution.py:24
  316.9 10.6 %collective-permute-start.97 = (f32[4,64,256]{2,1,0:T(8,128)S(1)}, f32[4,64,256]{2,1,0:T(8,128)S(1)}, u32[]{:S(2)}, u32[]{:S(2)}) collective-permute-start(f32[4,64,256]{2,1,0:T(8,128)S(1)} %get-tuple-element.63), channel_id=1, source_target_pairs={{0,24},{8,16},{16,8},{24,0},{1,25},{9,17},{17,9},{25,1},{2,26},{10... | collective-permute-start | bytes 786440 | tf_op jit(solution)/shard_map/ppermute | solution.py:24
  318.2 9.8 %collective-permute-start.101 = (f32[4,64,256]{2,1,0:T(8,128)S(1)}, f32[4,64,256]{2,1,0:T(8,128)S(1)}, u32[]{:S(2)}, u32[]{:S(2)}) collective-permute-start(f32[4,64,256]{2,1,0:T(8,128)S(1)} %get-tuple-element.65), channel_id=1, source_target_pairs={{0,32},{32,0},{64,96},{96,64},{1,33},{33,1},{65,97},{97,65},{2,34}... | collective-permute-start | bytes 786440 | tf_op jit(solution)/shard_map/ppermute | solution.py:24
  321.0 8.5 %collective-permute-start.105 = (f32[4,64,256]{2,1,0:T(8,128)S(1)}, f32[4,64,256]{2,1,0:T(8,128)S(1)}, u32[]{:S(2)}, u32[]{:S(2)}) collective-permute-start(f32[4,64,256]{2,1,0:T(8,128)S(1)} %get-tuple-element.67), channel_id=1, source_target_pairs={{0,96},{32,64},{64,32},{96,0},{1,97},{33,65},{65,33},{97,1},{2,98}... | collective-permute-start | bytes 786440 | tf_op jit(solution)/shard_map/ppermute | solution.py:24
  323.6 7.9 %collective-permute-start.94 = (f32[2,64,256]{2,1,0:T(8,128)S(1)}, f32[2,64,256]{2,1,0:T(8,128)S(1)}, u32[]{:S(2)}, u32[]{:S(2)}) collective-permute-start(f32[2,64,256]{2,1,0:T(8,128)S(1)} %get-tuple-element.77), channel_id=1, source_target_pairs={{0,96},{32,64},{64,32},{96,0},{1,97},{33,65},{65,33},{97,1},{2,98}... | collective-permute-start | bytes 393224 | tf_op jit(solution)/shard_map/ppermute | solution.py:24
  329.6 7.6 %collective-permute-start.106 = (f32[2,64,256]{2,1,0:T(8,128)S(1)}, f32[2,64,256]{2,1,0:T(8,128)S(1)}, u32[]{:S(2)}, u32[]{:S(2)}) collective-permute-start(f32[2,64,256]{2,1,0:T(8,128)S(1)} %get-tuple-element.83), channel_id=1, source_target_pairs={{0,8},{8,0},{16,24},{24,16},{1,9},{9,1},{17,25},{25,17},{2,10},{10... | collective-permute-start | bytes 393224 | tf_op jit(solution)/shard_map/ppermute | solution.py:24
  349.1 8.8 %collective-permute-start.109 = (f32[128,256]{1,0:T(8,128)S(1)}, f32[128,256]{1,0:T(8,128)S(1)}, u32[]{:S(2)}, u32[]{:S(2)}) collective-permute-start(f32[128,256]{1,0:T(8,128)S(1)} %dynamic-slice_add_fusion), channel_id=1, source_target_pairs={{0,32},{32,64},{64,96},{96,0},{1,33},{33,65},{65,97},{97,1},{2,34}... | collective-permute-start | bytes 393224 | tf_op jit(solution)/shard_map/ppermute | solution.py:48
  359.2 9.1 %collective-permute-start.112 = (f32[128,256]{1,0:T(8,128)S(1)}, f32[128,256]{1,0:T(8,128)S(1)}, u32[]{:S(2)}, u32[]{:S(2)}) collective-permute-start(f32[128,256]{1,0:T(8,128)S(1)} %add_add_fusion.2), channel_id=1, source_target_pairs={{0,8},{8,16},{16,24},{24,0},{1,9},{9,17},{17,25},{25,1},{2,10},{10... | collective-permute-start | bytes 393224 | tf_op jit(solution)/shard_map/ppermute | solution.py:48
  370.6 9.3 %collective-permute-start.115 = (f32[128,256]{1,0:T(8,128)S(1)}, f32[128,256]{1,0:T(8,128)S(1)}, u32[]{:S(2)}, u32[]{:S(2)}) collective-permute-start(f32[128,256]{1,0:T(8,128)S(1)} %add_add_fusion.1), channel_id=1, source_target_pairs={{0,2},{2,4},{4,6},{6,0},{1,3},{3,5},{5,7},{7,1},{8,10},{10,12},{12... | collective-permute-start | bytes 393224 | tf_op jit(solution)/shard_map/ppermute | solution.py:48
  (95 other events, 667.5 us)

commit v3 on v2

--- a/solution.py
+++ b/solution.py
@@ -16,7 +16,7 @@
 BLK = 128
 HALF = 64
 CHUNK = 32
-UNROLL = 8
+UNROLL = 16
 
 
 def flip(value, step):
@@ -40,16 +40,9 @@
 
 X1, X3, Y1, Y3, Z1, Z3 = [(axis, mask) for axis in "xyz" for mask in (1, 3)]
 CORE = ("c", 1)
-ROW_STEPS = [[X1, X3, Y1, Y3], [X3, X1, Y3, Y1], [Y1, Y3, X1, X3], [Y3, Y1, X3, X1]]
+LIGHT = [[X1, X3], [Y1, Y3]]
+HEAVY = [[Y1, Y3], [Y3, Y1], [X1, X3], [X3, X1]]
 COL_STEPS = [[Z1, Z3], [Z3, Z1]]
-
-
-def shift(value, axis, amount):
-    return lax.ppermute(value, axis, [(i, (i + amount) % 4) for i in range(4)])
-
-
-def ring_sum(value, axis):
-    return (value + shift(value, axis, 1)) + (shift(value, axis, 2) + shift(value, axis, 3))
 
 
 def flip_bits(mine, other):
@@ -58,7 +51,7 @@
 
 
 def swapped(index):
-    return (index & 5) * 2 + (index & 10) // 2
+    return (index & 3) + (index & 4) * 2 + (index & 8) // 2
 
 
 def split(value):
@@ -72,8 +65,9 @@
     )
 
 
-def lane_sums(block):
-    return nt_dot(jnp.ones((8, block.shape[1]), F32), block)[0:1, :]
+def lane_sums(total):
+    lanes = total.shape[-1]
+    return nt_dot(jnp.ones((8, lanes), F32), total[...].reshape(-1, lanes))[0:1, :]
 
 
 def live_tile(tiles_ref, slot, first, count):
@@ -102,8 +96,7 @@
 
     @pl.when(step == pl.num_programs(0) - 1)
     def _():
-        for block in range(total.shape[0]):
-            out_ref[block : block + 1, :] = lane_sums(total[block])
+        out_ref[...] = lane_sums(total)
 
 
 def chunk_map(step, count_ref, *_):
@@ -114,13 +107,13 @@
     slots = tiles.shape[0]
     return pl.pallas_call(
         rowsum_kernel,
-        out_shape=jax.ShapeDtypeStruct((out_blocks, BLK), F32),
+        out_shape=jax.ShapeDtypeStruct((1, out_blocks * BLK), F32),
         grid_spec=pltpu.PrefetchScalarGridSpec(
             num_scalar_prefetch=2,
             grid=(slots // CHUNK,),
             in_specs=[pl.BlockSpec((CHUNK, BLK, BLK), chunk_map)]
             + [pl.BlockSpec(memory_space=pl.ANY)] * len(after),
-            out_specs=pl.BlockSpec((out_blocks, BLK), lambda s, *_: (0, 0)),
+            out_specs=pl.BlockSpec((1, out_blocks * BLK), lambda s, *_: (0, 0)),
             scratch_shapes=[pltpu.VMEM((out_blocks, BLK, BLK), F32)],
         ),
         cost_estimate=pl.CostEstimate(flops=10**10, bytes_accessed=2**23, transcendentals=0),
@@ -167,7 +160,7 @@
     refs = refs[5:]
     if not first_pass:
         factor_ref, refs = refs[0], refs[1:]
-    pieces, (keep_ref, send_ref), refs = refs[:8], refs[8:10], refs[10:]
+    pieces, targets, refs = refs[:8], refs[8:10], refs[10:]
     source, total = refs[:2]
     tilde = refs[2] if first_pass else None
     step = pl.program_id(0)
@@ -197,15 +190,15 @@
 
     @pl.when(step == pl.num_programs(0) - 1)
     def _():
-        rows = keep_ref.shape[1]
+        rows = targets[0].shape[1]
+        lines = lane_sums(tilde) if first_pass else None
         for number in range(16):
             if first_pass:
-                line = lane_sums(tilde[number])
+                line = lines[:, number * BLK : (number + 1) * BLK]
                 total[number * rows + BLK : (number + 1) * rows, :BLK] = jnp.broadcast_to(
                     line, (rows - BLK, BLK)
                 )
-            target = keep_ref if number < 8 else send_ref
-            target[number % 8] = total[number * rows : (number + 1) * rows, :]
+            targets[number // 8][number % 8] = total[number * rows : (number + 1) * rows, :]
 
 
 def whole(shape):
@@ -224,13 +217,13 @@
         scratch.append(pltpu.VMEM((16, BLK, BLK), F32))
     return pl.pallas_call(
         functools.partial(forward_kernel, first_pass),
-        out_shape=(out, out),
+        out_shape=(out,) * 2,
         grid_spec=pltpu.PrefetchScalarGridSpec(
             num_scalar_prefetch=3,
             grid=(slots // CHUNK,),
             in_specs=[pl.BlockSpec((CHUNK, BLK, BLK), chunk_map)]
             + [whole(a.shape) for a in [inverse] + extra + list(pieces)],
-            out_specs=(whole(out.shape), whole(out.shape)),
+            out_specs=(whole(out.shape),) * 2,
             scratch_shapes=scratch,
         ),
         cost_estimate=pl.CostEstimate(
@@ -292,10 +285,15 @@
 PANEL = 32
 
 
-def inverse_factor_kernel(gram_ref, out_ref, work, columns, multiplier, right):
-    size = gram_ref.shape[0]
+def inverse_factor_kernel(one_ref, two_ref, out_ref, work, columns, multiplier, right):
+    size = out_ref.shape[0]
     lanes = columns.shape[-1]
-    work[:, :size] = gram_ref[...]
+    half, quarter = size // 2, size // 4
+    work[:half, :half] = one_ref[:half]
+    work[:quarter, half:size] = one_ref[half:]
+    work[quarter:half, half:size] = two_ref[:quarter]
+    work[half:, half:size] = two_ref[quarter:]
+    work[half:, :half] = jnp.zeros((half, half), F32)
     row_at = lax.broadcasted_iota(jnp.int32, (size, size), 0)
     lane_at = lax.broadcasted_iota(jnp.int32, (size, size), 1)
     work[:, size:] = (row_at == lane_at).astype(F32)
@@ -337,12 +335,12 @@
     out_ref[...] = work[:, size:]
 
 
-def inverse_factor(gram):
-    size = gram.shape[0]
+def inverse_factor(one, two):
+    size = 2 * one.shape[1]
     return pl.pallas_call(
         inverse_factor_kernel,
         out_shape=jax.ShapeDtypeStruct((size, size), F32),
-        in_specs=[pl.BlockSpec(memory_space=pltpu.VMEM)],
+        in_specs=[pl.BlockSpec(memory_space=pltpu.VMEM)] * 2,
         out_specs=pl.BlockSpec(memory_space=pltpu.VMEM),
         scratch_shapes=[
             pltpu.VMEM((size, 2 * size), F32),
@@ -351,23 +349,33 @@
             pltpu.VMEM((PANEL, BLK), F32),
         ],
         cost_estimate=pl.CostEstimate(flops=2**34, bytes_accessed=2**19, transcendentals=0),
-    )(gram)
-
-
-def quarters(value):
-    return [value[None, q * HALF : (q + 1) * HALF] for q in range(4)]
-
-
-def gather_row(value):
-    return sum([gather(part, steps) for part, steps in zip(quarters(value), ROW_STEPS)], [])
-
-
-def gather_two(value, steps):
-    return jnp.concatenate(gather(value, steps[:2]))
+    )(one, two)
+
+
+def gather_light(value):
+    return [
+        jnp.concatenate(gather(value[None, half * BLK : (half + 1) * BLK], LIGHT[half]))
+        for half in range(2)
+    ]
+
+
+def gather_heavy(halves):
+    pieces = []
+    for number, steps in enumerate(HEAVY):
+        row = number % 2 * HALF
+        pieces += gather(halves[number // 2][:, row : row + HALF], steps)
+    return pieces
 
 
 def scatter_row(outs):
-    parts = [scatter(outs[2 * q], outs[2 * q + 1], ROW_STEPS[q])[0] for q in range(4)]
+    parts = []
+    for half in range(2):
+        pair = [
+            scatter(outs[2 * number], outs[2 * number + 1], HEAVY[number])
+            for number in (2 * half, 2 * half + 1)
+        ]
+        pair = jnp.concatenate(pair, axis=1)
+        parts.append(scatter(pair[:2], pair[2:], LIGHT[half])[0])
     return jnp.concatenate(parts, axis=0)
 
 
@@ -390,15 +398,15 @@
 def gram_sum(gram):
     half = gram.shape[0] // 2
     core = lax.axis_index("c")
-    kept = lax.dynamic_slice_in_dim(gram, core * half, half, 0)
-    sent = lax.dynamic_slice_in_dim(gram, (1 - core) * half, half, 0)
-    value = kept + flip(sent, CORE)
-    for axis in "xyz":
-        value = ring_sum(value, axis)
+    halves = [
+        jnp.concatenate([gram[:half, :half], gram[: half // 2, half:]]),
+        jnp.concatenate([gram[half // 2 : half, half:], gram[half:, half:]]),
+    ]
+    value = jnp.where(core == 0, *halves) + flip(jnp.where(core == 0, *halves[::-1]), CORE)
+    for step in (X1, X3, Y1, Y3, Z1, Z3):
+        value = value + flip(value, step)
     other = flip(value, CORE)
-    return jnp.where(
-        core == 0, jnp.concatenate([value, other]), jnp.concatenate([other, value])
-    )
+    return jnp.where(core == 0, value, other), jnp.where(core == 0, other, value)
 
 
 def local(trial_vectors, tiles, tile_rows, tile_cols, tile_count):
@@ -411,7 +419,8 @@
     row = tile_rows.reshape(slots)
     col = tile_cols.reshape(slots)
     near, far = flip_bits(z, row // 4)
-    slab = (((row // 2) % 2) ^ core) * 8 + jnp.where(row % 2 == 0, near + 2 * far, 4 + far + 2 * near)
+    part = row % 2
+    slab = ((row // 2) % 2 ^ core) * 8 + jnp.where(part == 0, near + 2 * far, 4 + far + 2 * near)
     near_x, far_x = flip_bits(x, col // 8)
     near_y, far_y = flip_bits(y, (col // 2) % 4)
     at_x, at_y = near_x + 2 * far_x, near_y + 2 * far_y
@@ -420,15 +429,15 @@
     put_later = slab * BLK
     put_backward = member * BLK
 
-    begun = [gather_two(part, steps) for part, steps in zip(quarters(trial_vectors), ROW_STEPS)]
-    pieces = sum([gather(part, steps[2:]) for part, steps in zip(begun, ROW_STEPS)], [])
+    begun = gather_light(trial_vectors)
+    pieces = gather_heavy(begun)
 
     sums = rowsum_call(
-        count, (slab // 8) * 8 + (near + 2 * far) * 2 + row % 2, tiles, 16, begun
+        count, (slab // 8) * 8 + (near + 2 * far) * 2 + part, tiles, 16, begun
     ).reshape(2, 2, 2, 2, BLK)
     got = sums[0] + flip(sums[1], CORE)
     inverse_own = 1.0 / (1.0 + scatter(got[0], got[1], COL_STEPS[0])[0])
-    gathered = jnp.concatenate(gather(inverse_own[None], ROW_STEPS[0]))
+    gathered = jnp.concatenate(gather(inverse_own[None], LIGHT[0] + LIGHT[1]))
     inverse = jnp.concatenate(
         [gathered[:, 0], gathered[:, 1].reshape(4, 4, BLK).swapaxes(0, 1).reshape(16, BLK)]
     )
@@ -438,7 +447,7 @@
     factor = None
     scale = None
     for iteration in range(ITERS):
-        keep, send = forward_call(
+        outs = forward_call(
             count,
             put_first if iteration == 0 else put_later,
             member,
@@ -447,7 +456,7 @@
             factor,
             pieces,
         )
-        one, two = scatter_col(keep, send)
+        one, two = scatter_col(*outs)
         if iteration == 0:
             tilde = jnp.concatenate([one[BLK, :BLK], two[BLK, :BLK]]).reshape(2 * BLK, 1)
             scale = inverse_own / (inverse_own * (inverse_own + tilde))
@@ -463,8 +472,8 @@
             preferred_element_type=F32,
         )
         if iteration + 1 < ITERS:
-            pieces = gather_row(reduced)
-        factor = inverse_factor(gram_sum(gram))
+            pieces = gather_heavy(gather_light(reduced))
+        factor = inverse_factor(*gram_sum(gram))
         vectors = nt_dot(reduced, factor)
     total_nodes = 2 * BLK * 128
     return vectors * math.sqrt(total_nodes)

time: 406 us -> 394 us (0.970)
  starting transfers between devices: 186 us -> 162 us
  waiting for transfers between devices: 110 us -> 127 us
  Pallas kernels: 76.6 us -> 72 us
    ppermute x101 -> x97, waiting for transfers between devices: 74.7 us -> 127 us  [flip(): lax.ppermute(value, axis, [(i, i ^ mask) for i in range(2 if axis == 'c'...]
    ppermute x18 -> x0, waiting for transfers between devices: 34.9 us -> none  [shift(): return lax.ppermute(value, axis, [(i, (i + amount) % 4) for i in range(4)])]
    ppermute x18 -> x0, starting transfers between devices: 18.2 us -> none  [shift(): return lax.ppermute(value, axis, [(i, (i + amount) % 4) for i in range(4)])]
    ppermute x101 -> x97, starting transfers between devices: 168 us -> 162 us  [flip(): lax.ppermute(value, axis, [(i, i ^ mask) for i in range(2 if axis == 'c'...]
  transfers between devices with their start and end apart: 119 -> 97, of which waited for: 60 -> 56; matrix products, arithmetic and copies ran while one was open for 3% -> 3% of each run, Pallas kernels for 3% -> 3%
where the time goes in v3:
time: 394 us; the launch traced here: 387 us
  starting transfers between devices  162 us (41%)
  waiting for transfers between devices  127 us (32%)
  Pallas kernels  72 us (18%)
  other arithmetic  14.8 us (4%)
  local copies, waits for them, and re-layouts  4.58 us (1%)
    ppermute x97, starting transfers between devices, flip(): lax.ppermute(value, axis, [(i, i ^ mask) for i in range(2 if axis == 'c'...  162 us
    ppermute x97, waiting for transfers between devices, flip(): lax.ppermute(value, axis, [(i, i ^ mask) for i in range(2 if axis == 'c'...  127 us
    pallas_call x2, Pallas kernels, inverse_factor(): pl.pallas_call(inverse_factor_kernel, out_shape=jax.ShapeDtypeStruct((siz...  26.6 us
    pallas_call x2, Pallas kernels, forward_call(): pl.pallas_call(functools.partial(forward_kernel, first_pass), out_shape=(...  22.7 us
    pallas_call x2, Pallas kernels, backward_call(): pl.pallas_call(backward_kernel, out_shape=(out,) * 8, grid_spec=pltpu.Pre...  17.8 us
  transfers between devices with their start and end apart: 97, of which 56 were waited for; matrix products, arithmetic and copies ran while one was open for 3% of the time, Pallas kernels for 3%

profile of v3, /device:TPU:1, one launch (start us, length us, event | category | flops | bytes accessed | tf_op | source)
XLA Modules:
  0.0 386.5 jit_solution(12165010505151628554)
XLA Ops:
  6.0 3.1 collective-permute-start.3
  9.1 2.6 collective-permute-start.1
  17.2 4.9 %shard_map.55 = f32[1,2048]{1,0:T(1,128)} custom-call(s32[1]{0:T(128)} %bitcast.105.count_ref, s32[128]{0:T(128)} %get-tuple-element.88.put_ref, f32[128,128,128]{2,1,0:T(8,128)} %bitcast.119, f32[4,128,256]{2,1,0:T(8,128)} %pad_maximum_fusion.refs_0_, f32[4,128,256]{2,1,0:T(8,128)} %pad_maximum_fusion.1.refs_1_), custom_call_target="tpu_custom_call" | custom-call | flops 10000000000 | bytes 8388608 | tf_op jit(solution)/shard_map/pallas_call | solution.py:108
  22.9 2.7 collective-permute-start.4
  26.5 3.8 collective-permute-start.5
  33.8 2.8 collective-permute-start.17
  38.2 2.6 collective-permute-start.13
  49.9 5.9 %collective-permute-done.10 = f32[8,2,128]{2,0,1:T(8,128)S(1)} collective-permute-done((f32[8,2,128]{2,0,1:T(8,128)S(1)}, f32[8,2,128]{2,0,1:T(8,128)S(1)}, u32[]{:S(2)}, u32[]{:S(2)}) %collective-permute-start.10) | collective-permute-done | bytes 8224 | tf_op jit(solution)/shard_map/ppermute | solution.py:24
  57.2 10.3 %shard_map.56 = (f32[8,136,256]{2,1,0:T(8,128)}, f32[8,136,256]{2,1,0:T(8,128)}) custom-call(s32[1]{0:T(128)} %bitcast.106.refs_0_, s32[256]{0:T(256)} %pad_add_fusion.refs_1_, s32[128]{0:T(128)} %get-tuple-element.46.refs_2_, f32[128,128,128]{2,1,0:T(8,128)} %bitcast.120, f32[32,128]{1,0:T(8,128)} %pad_maximum_fusion.26.refs_4_, f32[8,64,256]{2,1,0:T(8,128)} %copy-done.15, ...), custom_call_target="tpu_custom_call" | custom-call | flops 6442450944 | bytes 16777216 | tf_op jit(solution)/shard_map/pallas_call | solution.py:218
  67.5 6.5 %collective-permute-start.19 = (f32[8,136,256]{2,1,0:T(8,128)}, f32[8,136,256]{2,1,0:T(8,128)S(1)}, u32[]{:S(2)}, u32[]{:S(2)}) collective-permute-start(f32[8,136,256]{2,1,0:T(8,128)} %get-tuple-element.26), channel_id=1, source_target_pairs={{0,1},{1,0},{2,3},{3,2},{4,5},{5,4},{6,7},{7,6},{8,9},{9,8},{10,11... | collective-permute-start | bytes 3342344 | tf_op jit(solution)/shard_map/ppermute | solution.py:24
  74.0 2.6 collective-permute-done.19
  78.0 3.3 collective-permute-start.20
  81.3 4.5 %collective-permute-done.22 = f32[2,136,256]{2,1,0:T(8,128)S(1)} collective-permute-done((f32[2,136,256]{2,1,0:T(8,128)S(1)}, f32[2,136,256]{2,1,0:T(8,128)S(1)}, u32[]{:S(2)}, u32[]{:S(2)}) %collective-permute-start.22) | collective-permute-done | bytes 278560 | tf_op jit(solution)/shard_map/ppermute | solution.py:24
  85.9 3.3 collective-permute-start.23
  89.3 2.7 collective-permute-done.23
  95.1 2.6 collective-permute-done.24
  99.5 5.1 %collective-permute-start.28 = (f32[2,128,256]{2,1,0:T(8,128)S(1)}, f32[2,128,256]{2,1,0:T(8,128)S(1)}, u32[]{:S(2)}, u32[]{:S(2)}) collective-permute-start(f32[2,128,256]{2,1,0:T(8,128)S(1)} %pad_maximum_fusion.14.refs_4_), channel_id=1, source_target_pairs={{0,1},{1,0},{2,3},{3,2},{4,5},{5,4},{6,7},{7,6},{8,9},{9,8},{10,11... | collective-permute-start | bytes 786440 | tf_op jit(solution)/shard_map/ppermute | solution.py:24
  104.7 4.4 %collective-permute-start.29 = (f32[2,128,256]{2,1,0:T(8,128)S(1)}, f32[2,128,256]{2,1,0:T(8,128)S(1)}, u32[]{:S(2)}, u32[]{:S(2)}) collective-permute-start(f32[2,128,256]{2,1,0:T(8,128)S(1)} %collective-permute-done.25.refs_5_), channel_id=1, source_target_pairs={{0,1},{1,0},{2,3},{3,2},{4,5},{5,4},{6,7},{7,6},{8,9},{9,8},{10,11... | collective-permute-start | bytes 786440 | tf_op jit(solution)/shard_map/ppermute | solution.py:24
  111.4 8.9 %shard_map.57 = (f32[8,64,256]{2,1,0:T(8,128)}, f32[8,64,256]{2,1,0:T(8,128)}, f32[8,64,256]{2,1,0:T(8,128)}, f32[8,64,256]{2,1,0:T(8,128)}, f32[8,64,256]{2,1,0...) custom-call(s32[1]{0:T(128)} %bitcast.107.refs_0_, s32[128]{0:T(128)} %get-tuple-element.45.refs_1_, ...), custom_call_target="tpu_custom_call" | custom-call | flops 6442450944 | bytes 16777216 | tf_op jit(solution)/shard_map/pallas_call | solution.py:265
  120.3 2.5 collective-permute-start.32
  122.8 2.8 collective-permute-start.38
  125.6 3.8 collective-permute-start.40
  129.4 5.5 %collective-permute-done.32 = f32[8,64,256]{2,1,0:T(8,128)S(1)} collective-permute-done((f32[8,64,256]{2,1,0:T(8,128)}, f32[8,64,256]{2,1,0:T(8,128)S(1)}, u32[]{:S(2)}, u32[]{:S(2)}) %collective-permute-start.32) | collective-permute-done | bytes 524320 | tf_op jit(solution)/shard_map/ppermute | solution.py:24
  137.1 2.5 collective-permute-start.35
  139.7 2.7 collective-permute-start.39
  142.4 4.7 %collective-permute-start.41 = (f32[4,64,256]{2,1,0:T(8,128)S(1)}, f32[4,64,256]{2,1,0:T(8,128)S(1)}, u32[]{:S(2)}, u32[]{:S(2)}) collective-permute-start(f32[4,64,256]{2,1,0:T(8,128)S(1)} %slice_add_fusion.16), channel_id=1, source_target_pairs={{0,96},{32,64},{64,32},{96,0},{1,97},{33,65},{65,33},{97,1},{2,98}... | collective-permute-start | bytes 786440 | tf_op jit(solution)/shard_map/ppermute | solution.py:24
  148.4 3.5 collective-permute-done.41
  152.1 5.4 %collective-permute-done.36 = f32[2,128,256]{2,1,0:T(8,128)S(1)} collective-permute-done((f32[2,128,256]{2,1,0:T(8,128)S(1)}, f32[2,128,256]{2,1,0:T(8,128)S(1)}, u32[]{:S(2)}, u32[]{:S(2)}) %collective-permute-start.36) | collective-permute-done | bytes 262176 | tf_op jit(solution)/shard_map/ppermute | solution.py:24
  159.0 2.8 collective-permute-done.37
  163.8 6.2 %collective-permute-start.44 = (f32[192,128]{1,0:T(8,128)S(1)}, f32[192,128]{1,0:T(8,128)S(1)}, u32[]{:S(2)}, u32[]{:S(2)}) collective-permute-start(f32[192,128]{1,0:T(8,128)S(1)} %slice_select_fusion.1), channel_id=1, source_target_pairs={{0,1},{1,0},{2,3},{3,2},{4,5},{5,4},{6,7},{7,6},{8,9},{9,8},{10,11... | collective-permute-start | bytes 294920 | tf_op jit(solution)/shard_map/ppermute | solution.py:24
  171.7 3.5 collective-permute-done.52
  175.3 3.0 collective-permute-start.53
  180.4 5.4 %collective-permute-done.46 = f32[192,128]{1,0:T(8,128)S(1)} collective-permute-done((f32[192,128]{1,0:T(8,128)S(1)}, f32[192,128]{1,0:T(8,128)S(1)}, u32[]{:S(2)}, u32[]{:S(2)}) %collective-permute-start.46) | collective-permute-done | bytes 98336 | tf_op jit(solution)/shard_map/ppermute | solution.py:24
  186.5 2.9 collective-permute-done.47
  189.9 2.4 collective-permute-start.56
  204.7 6.7 %collective-permute-start.51 = (f32[192,128]{1,0:T(8,128)S(1)}, f32[192,128]{1,0:T(8,128)S(1)}, u32[]{:S(2)}, u32[]{:S(2)}) collective-permute-start(f32[192,128]{1,0:T(8,128)S(1)} %add.380), channel_id=1, source_target_pairs={{0,1},{1,0},{2,3},{3,2},{4,5},{5,4},{6,7},{7,6},{8,9},{9,8},{10,11... | collective-permute-start | bytes 294920 | tf_op jit(solution)/shard_map/ppermute | solution.py:24
  213.0 13.3 %shard_map.58.refs_5_ = f32[256,256]{1,0:T(8,128)} custom-call(f32[192,128]{1,0:T(8,128)} %get-tuple-element.79.one_ref, f32[192,128]{1,0:T(8,128)} %get-tuple-element.78.two_ref), custom_call_target="tpu_custom_call" | custom-call | flops 17179869184 | bytes 524288 | tf_op jit(solution)/shard_map/pallas_call | solution.py:340
  227.2 12.4 %shard_map.59 = (f32[8,128,256]{2,1,0:T(8,128)}, f32[8,128,256]{2,1,0:T(8,128)}) custom-call(s32[1]{0:T(128)} %bitcast.108.refs_0_, s32[128]{0:T(128)} %get-tuple-element.89.refs_1_, s32[128]{0:T(128)} %get-tuple-element.46.refs_2_, f32[128,128,128]{2,1,0:T(8,128)} %bitcast.122, f32[32,128]{1,0:T(8,128)} %pad_maximum_fusion.26.refs_4_, ...), custom_call_target="tpu_custom_call" | custom-call | flops 6442450944 | bytes 16777216 | tf_op jit(solution)/shard_map/pallas_call | solution.py:218
  239.6 2.3 collective-permute-start.64
  241.9 2.5 collective-permute-done.64
  247.4 6.1 %collective-permute-done.67 = f32[2,128,256]{2,1,0:T(8,128)S(1)} collective-permute-done((f32[2,128,256]{2,1,0:T(8,128)S(1)}, f32[2,128,256]{2,1,0:T(8,128)S(1)}, u32[]{:S(2)}, u32[]{:S(2)}) %collective-permute-start.67) | collective-permute-done | bytes 262176 | tf_op jit(solution)/shard_map/ppermute | solution.py:24
  256.2 2.5 collective-permute-done.68
  262.0 2.7 collective-permute-done.69
  266.6 4.9 %collective-permute-start.73 = (f32[2,128,256]{2,1,0:T(8,128)S(1)}, f32[2,128,256]{2,1,0:T(8,128)S(1)}, u32[]{:S(2)}, u32[]{:S(2)}) collective-permute-start(f32[2,128,256]{2,1,0:T(8,128)S(1)} %pad_maximum_fusion.18.refs_4_), channel_id=1, source_target_pairs={{0,1},{1,0},{2,3},{3,2},{4,5},{5,4},{6,7},{7,6},{8,9},{9,8},{10,11... | collective-permute-start | bytes 786440 | tf_op jit(solution)/shard_map/ppermute | solution.py:24
  271.4 4.2 %collective-permute-start.74 = (f32[2,128,256]{2,1,0:T(8,128)S(1)}, f32[2,128,256]{2,1,0:T(8,128)S(1)}, u32[]{:S(2)}, u32[]{:S(2)}) collective-permute-start(f32[2,128,256]{2,1,0:T(8,128)S(1)} %collective-permute-done.70.refs_5_), channel_id=1, source_target_pairs={{0,1},{1,0},{2,3},{3,2},{4,5},{5,4},{6,7},{7,6},{8,9},{9,8},{10,11... | collective-permute-start | bytes 786440 | tf_op jit(solution)/shard_map/ppermute | solution.py:24
  277.9 8.9 %shard_map.60 = (f32[8,64,256]{2,1,0:T(8,128)}, f32[8,64,256]{2,1,0:T(8,128)}, f32[8,64,256]{2,1,0:T(8,128)}, f32[8,64,256]{2,1,0:T(8,128)}, f32[8,64,256]{2,1,0...) custom-call(s32[1]{0:T(128)} %bitcast.109.refs_0_, s32[128]{0:T(128)} %get-tuple-element.45.refs_1_, ...), custom_call_target="tpu_custom_call" | custom-call | flops 6442450944 | bytes 16777216 | tf_op jit(solution)/shard_map/pallas_call | solution.py:265
  287.9 3.2 collective-permute-start.83
  291.2 2.9 collective-permute-start.85
  294.0 7.4 %collective-permute-done.77 = f32[8,64,256]{2,1,0:T(8,128)S(1)} collective-permute-done((f32[8,64,256]{2,1,0:T(8,128)}, f32[8,64,256]{2,1,0:T(8,128)S(1)}, u32[]{:S(2)}, u32[]{:S(2)}) %collective-permute-start.77) | collective-permute-done | bytes 524320 | tf_op jit(solution)/shard_map/ppermute | solution.py:24
  304.2 2.5 collective-permute-start.84
  306.8 4.8 %collective-permute-start.86 = (f32[4,64,256]{2,1,0:T(8,128)S(1)}, f32[4,64,256]{2,1,0:T(8,128)S(1)}, u32[]{:S(2)}, u32[]{:S(2)}) collective-permute-start(f32[4,64,256]{2,1,0:T(8,128)S(1)} %slice_add_fusion.4), channel_id=1, source_target_pairs={{0,96},{32,64},{64,32},{96,0},{1,97},{33,65},{65,33},{97,1},{2,98}... | collective-permute-start | bytes 786440 | tf_op jit(solution)/shard_map/ppermute | solution.py:24
  313.7 2.7 collective-permute-done.86
  316.5 2.6 collective-permute-start.87
  319.0 3.0 collective-permute-done.81
  323.5 2.7 collective-permute-done.82
  328.3 6.3 %collective-permute-start.89 = (f32[192,128]{1,0:T(8,128)S(1)}, f32[192,128]{1,0:T(8,128)S(1)}, u32[]{:S(2)}, u32[]{:S(2)}) collective-permute-start(f32[192,128]{1,0:T(8,128)S(1)} %slice_select_fusion), channel_id=1, source_target_pairs={{0,1},{1,0},{2,3},{3,2},{4,5},{5,4},{6,7},{7,6},{8,9},{9,8},{10,11... | collective-permute-start | bytes 294920 | tf_op jit(solution)/shard_map/ppermute | solution.py:24
  335.6 4.0 %collective-permute-done.90 = f32[192,128]{1,0:T(8,128)S(1)} collective-permute-done((f32[192,128]{1,0:T(8,128)S(1)}, f32[192,128]{1,0:T(8,128)S(1)}, u32[]{:S(2)}, u32[]{:S(2)}) %collective-permute-start.90) | collective-permute-done | bytes 98336 | tf_op jit(solution)/shard_map/ppermute | solution.py:24
  339.7 3.0 collective-permute-start.91
  344.8 3.5 collective-permute-done.92
  348.3 2.4 collective-permute-start.93
  350.7 2.3 collective-permute-done.93
  357.7 4.4 %collective-permute-done.95 = f32[192,128]{1,0:T(8,128)S(1)} collective-permute-done((f32[192,128]{1,0:T(8,128)S(1)}, f32[192,128]{1,0:T(8,128)S(1)}, u32[]{:S(2)}, u32[]{:S(2)}) %collective-permute-start.95) | collective-permute-done | bytes 98336 | tf_op jit(solution)/shard_map/ppermute | solution.py:24
  362.1 7.0 %collective-permute-start.96 = (f32[192,128]{1,0:T(8,128)S(1)}, f32[192,128]{1,0:T(8,128)S(1)}, u32[]{:S(2)}, u32[]{:S(2)}) collective-permute-start(f32[192,128]{1,0:T(8,128)S(1)} %add.417), channel_id=1, source_target_pairs={{0,1},{1,0},{2,3},{3,2},{4,5},{5,4},{6,7},{7,6},{8,9},{9,8},{10,11... | collective-permute-start | bytes 294920 | tf_op jit(solution)/shard_map/ppermute | solution.py:24
  370.7 13.3 %shard_map.61 = f32[256,256]{1,0:T(8,128)} custom-call(f32[192,128]{1,0:T(8,128)} %get-tuple-element.77.one_ref, f32[192,128]{1,0:T(8,128)} %get-tuple-element.76.two_ref), custom_call_target="tpu_custom_call" | custom-call | flops 17179869184 | bytes 524288 | tf_op jit(solution)/shard_map/pallas_call | solution.py:340
  (335 shorter events, 97.3 us)
Async XLA Ops:
  3.2 5.9 %collective-permute-start = (f32[1,128,256]{2,1,0:T(8,128)S(1)}, f32[1,128,256]{2,1,0:T(8,128)S(1)}, u32[]{:S(2)}, u32[]{:S(2)}) collective-permute-start(f32[1,128,256]{2,1,0:T(8,128)S(1)} %get-tuple-element.75), channel_id=1, source_target_pairs={{0,32},{32,0},{64,96},{96,64},{1,33},{33,1},{65,97},{97,65},{2,34}... | collective-permute-start | bytes 393224 | tf_op jit(solution)/shard_map/ppermute | solution.py:24
  6.0 8.1 %collective-permute-start.3 = (f32[2,128,256]{2,1,0:T(8,128)S(1)}, f32[2,128,256]{2,1,0:T(8,128)S(1)}, u32[]{:S(2)}, u32[]{:S(2)}) collective-permute-start(f32[2,128,256]{2,1,0:T(8,128)S(1)} %pad_maximum_fusion.13), channel_id=1, source_target_pairs={{0,24},{8,16},{16,8},{24,0},{1,25},{9,17},{17,9},{25,1},{2,26},{10... | collective-permute-start | bytes 786440 | tf_op jit(solution)/shard_map/ppermute | solution.py:24
  9.1 7.3 %collective-permute-start.1 = (f32[2,128,256]{2,1,0:T(8,128)S(1)}, f32[2,128,256]{2,1,0:T(8,128)S(1)}, u32[]{:S(2)}, u32[]{:S(2)}) collective-permute-start(f32[2,128,256]{2,1,0:T(8,128)S(1)} %pad_maximum_fusion.12), channel_id=1, source_target_pairs={{0,96},{32,64},{64,32},{96,0},{1,97},{33,65},{65,33},{97,1},{2,98}... | collective-permute-start | bytes 786440 | tf_op jit(solution)/shard_map/ppermute | solution.py:24
  33.8 10.4 %collective-permute-start.17 = (f32[4,64,256]{2,1,0:T(8,128)S(1)}, f32[4,64,256]{2,1,0:T(8,128)S(1)}, u32[]{:S(2)}, u32[]{:S(2)}) collective-permute-start(f32[4,64,256]{2,1,0:T(8,128)S(1)} %get-tuple-element.64), channel_id=1, source_target_pairs={{0,96},{32,64},{64,32},{96,0},{1,97},{33,65},{65,33},{97,1},{2,98}... | collective-permute-start | bytes 786440 | tf_op jit(solution)/shard_map/ppermute | solution.py:24
  36.7 5.7 %collective-permute-start.15 = (f32[4,64,256]{2,1,0:T(8,128)S(1)}, f32[4,64,256]{2,1,0:T(8,128)S(1)}, u32[]{:S(2)}, u32[]{:S(2)}) collective-permute-start(f32[4,64,256]{2,1,0:T(8,128)S(1)} %get-tuple-element.65), channel_id=1, source_target_pairs={{0,32},{32,0},{64,96},{96,64},{1,33},{33,1},{65,97},{97,65},{2,34}... | collective-permute-start | bytes 786440 | tf_op jit(solution)/shard_map/ppermute | solution.py:24
  38.2 8.5 %collective-permute-start.13 = (f32[4,64,256]{2,1,0:T(8,128)S(1)}, f32[4,64,256]{2,1,0:T(8,128)S(1)}, u32[]{:S(2)}, u32[]{:S(2)}) collective-permute-start(f32[4,64,256]{2,1,0:T(8,128)S(1)} %get-tuple-element.66), channel_id=1, source_target_pairs={{0,24},{8,16},{16,8},{24,0},{1,25},{9,17},{17,9},{25,1},{2,26},{10... | collective-permute-start | bytes 786440 | tf_op jit(solution)/shard_map/ppermute | solution.py:24
  41.3 6.3 %collective-permute-start.9 = (f32[4,2,128]{2,0,1:T(4,128)S(1)}, f32[4,2,128]{2,0,1:T(4,128)S(1)}, u32[]{:S(2)}, u32[]{:S(2)}) collective-permute-start(f32[4,2,128]{2,0,1:T(4,128)S(1)} %pad_maximum_fusion.28), channel_id=1, source_target_pairs={{0,8},{8,0},{16,24},{24,16},{1,9},{9,1},{17,25},{25,17},{2,10},{10... | collective-permute-start | bytes 12296 | tf_op jit(solution)/shard_map/ppermute | solution.py:24
  42.4 14.0 %collective-permute-start.16 = (f32[8,64,256]{2,1,0:T(8,128)S(1)}, f32[8,64,256]{2,1,0:T(8,128)S(1)}, u32[]{:S(2)}, u32[]{:S(2)}) collective-permute-start(f32[8,64,256]{2,1,0:T(8,128)S(1)} %pad_maximum_fusion.4.refs_9_), channel_id=1, source_target_pairs={{0,96},{32,64},{64,32},{96,0},{1,97},{33,65},{65,33},{97,1},{2,98}... | collective-permute-start | bytes 1572872 | tf_op jit(solution)/shard_map/ppermute | solution.py:24
  44.3 12.1 %collective-permute-start.18 = (f32[8,64,256]{2,1,0:T(8,128)S(1)}, f32[8,64,256]{2,1,0:T(8,128)}, u32[]{:S(2)}, u32[]{:S(2)}) collective-permute-start(f32[8,64,256]{2,1,0:T(8,128)S(1)} %pad_maximum_fusion.5.refs_11_), channel_id=1, source_target_pairs={{0,32},{32,0},{64,96},{96,64},{1,33},{33,1},{65,97},{97,65},{2,34}... | collective-permute-start | bytes 1572872 | tf_op jit(solution)/shard_map/ppermute | solution.py:24
  46.0 10.4 %collective-permute-start.12 = (f32[8,64,256]{2,1,0:T(8,128)S(1)}, f32[8,64,256]{2,1,0:T(8,128)}, u32[]{:S(2)}, u32[]{:S(2)}) collective-permute-start(f32[8,64,256]{2,1,0:T(8,128)S(1)} %pad_maximum_fusion.2.refs_5_), channel_id=1, source_target_pairs={{0,24},{8,16},{16,8},{24,0},{1,25},{9,17},{17,9},{25,1},{2,26},{10... | collective-permute-start | bytes 1572872 | tf_op jit(solution)/shard_map/ppermute | solution.py:24
  46.7 10.3 %collective-permute-start.14 = (f32[8,64,256]{2,1,0:T(8,128)S(1)}, f32[8,64,256]{2,1,0:T(8,128)}, u32[]{:S(2)}, u32[]{:S(2)}) collective-permute-start(f32[8,64,256]{2,1,0:T(8,128)S(1)} %pad_maximum_fusion.3.refs_7_), channel_id=1, source_target_pairs={{0,8},{8,0},{16,24},{24,16},{1,9},{9,1},{17,25},{25,17},{2,10},{10... | collective-permute-start | bytes 1572872 | tf_op jit(solution)/shard_map/ppermute | solution.py:24
  47.7 8.1 %collective-permute-start.10 = (f32[8,2,128]{2,0,1:T(8,128)S(1)}, f32[8,2,128]{2,0,1:T(8,128)S(1)}, u32[]{:S(2)}, u32[]{:S(2)}) collective-permute-start(f32[8,2,128]{2,0,1:T(8,128)S(1)} %pad_maximum_fusion.27), channel_id=1, source_target_pairs={{0,24},{8,16},{16,8},{24,0},{1,25},{9,17},{17,9},{25,1},{2,26},{10... | collective-permute-start | bytes 24584 | tf_op jit(solution)/shard_map/ppermute | solution.py:24
  67.5 9.1 %collective-permute-start.19 = (f32[8,136,256]{2,1,0:T(8,128)}, f32[8,136,256]{2,1,0:T(8,128)S(1)}, u32[]{:S(2)}, u32[]{:S(2)}) collective-permute-start(f32[8,136,256]{2,1,0:T(8,128)} %get-tuple-element.26), channel_id=1, source_target_pairs={{0,1},{1,0},{2,3},{3,2},{4,5},{5,4},{6,7},{7,6},{8,9},{9,8},{10,11... | collective-permute-start | bytes 3342344 | tf_op jit(solution)/shard_map/ppermute | solution.py:24
  77.9 8.0 %collective-permute-start.22 = (f32[2,136,256]{2,1,0:T(8,128)S(1)}, f32[2,136,256]{2,1,0:T(8,128)S(1)}, u32[]{:S(2)}, u32[]{:S(2)}) collective-permute-start(f32[2,136,256]{2,1,0:T(8,128)S(1)} %get-tuple-element.53), channel_id=1, source_target_pairs={{0,2},{2,0},{4,6},{6,4},{1,3},{3,1},{5,7},{7,5},{8,10},{10,8},{12,... | collective-permute-start | bytes 835592 | tf_op jit(solution)/shard_map/ppermute | solution.py:24
  78.0 11.2 %collective-permute-start.20 = (f32[2,136,256]{2,1,0:T(8,128)S(1)}, f32[2,136,256]{2,1,0:T(8,128)S(1)}, u32[]{:S(2)}, u32[]{:S(2)}) collective-permute-start(f32[2,136,256]{2,1,0:T(8,128)S(1)} %get-tuple-element.55), channel_id=1, source_target_pairs={{0,6},{2,4},{4,2},{6,0},{1,7},{3,5},{5,3},{7,1},{8,14},{10,12},{12... | collective-permute-start | bytes 835592 | tf_op jit(solution)/shard_map/ppermute | solution.py:24
  85.9 6.1 %collective-permute-start.23 = (f32[1,136,256]{2,1,0:T(8,128)S(1)}, f32[1,136,256]{2,1,0:T(8,128)S(1)}, u32[]{:S(2)}, u32[]{:S(2)}) collective-permute-start(f32[1,136,256]{2,1,0:T(8,128)S(1)} %slice_add_fusion.24), channel_id=1, source_target_pairs={{0,6},{2,4},{4,2},{6,0},{1,7},{3,5},{5,3},{7,1},{8,14},{10,12},{12... | collective-permute-start | bytes 417800 | tf_op jit(solution)/shard_map/ppermute | solution.py:24
  97.7 7.0 %collective-permute-start.25 = (f32[2,128,256]{2,1,0:T(8,128)S(1)}, f32[2,128,256]{2,1,0:T(8,128)S(1)}, u32[]{:S(2)}, u32[]{:S(2)}) collective-permute-start(f32[2,128,256]{2,1,0:T(8,128)S(1)} %pad_maximum_fusion.14.refs_4_), channel_id=1, source_target_pairs={{0,6},{2,4},{4,2},{6,0},{1,7},{3,5},{5,3},{7,1},{8,14},{10,12},{12... | collective-permute-start | bytes 786440 | tf_op jit(solution)/shard_map/ppermute | solution.py:24
  99.0 10.1 %collective-permute-start.27 = (f32[2,128,256]{2,1,0:T(8,128)S(1)}, f32[2,128,256]{2,1,0:T(8,128)S(1)}, u32[]{:S(2)}, u32[]{:S(2)}) collective-permute-start(f32[2,128,256]{2,1,0:T(8,128)S(1)} %pad_maximum_fusion.15.refs_6_), channel_id=1, source_target_pairs={{0,2},{2,0},{4,6},{6,4},{1,3},{3,1},{5,7},{7,5},{8,10},{10,8},{12,... | collective-permute-start | bytes 786440 | tf_op jit(solution)/shard_map/ppermute | solution.py:24
  99.5 9.7 %collective-permute-start.28 = (f32[2,128,256]{2,1,0:T(8,128)S(1)}, f32[2,128,256]{2,1,0:T(8,128)S(1)}, u32[]{:S(2)}, u32[]{:S(2)}) collective-permute-start(f32[2,128,256]{2,1,0:T(8,128)S(1)} %pad_maximum_fusion.14.refs_4_), channel_id=1, source_target_pairs={{0,1},{1,0},{2,3},{3,2},{4,5},{5,4},{6,7},{7,6},{8,9},{9,8},{10,11... | collective-permute-start | bytes 786440 | tf_op jit(solution)/shard_map/ppermute | solution.py:24
  104.7 5.6 %collective-permute-start.29 = (f32[2,128,256]{2,1,0:T(8,128)S(1)}, f32[2,128,256]{2,1,0:T(8,128)S(1)}, u32[]{:S(2)}, u32[]{:S(2)}) collective-permute-start(f32[2,128,256]{2,1,0:T(8,128)S(1)} %collective-permute-done.25.refs_5_), channel_id=1, source_target_pairs={{0,1},{1,0},{2,3},{3,2},{4,5},{5,4},{6,7},{7,6},{8,9},{9,8},{10,11... | collective-permute-start | bytes 786440 | tf_op jit(solution)/shard_map/ppermute | solution.py:24
  120.3 14.6 %collective-permute-start.32 = (f32[8,64,256]{2,1,0:T(8,128)}, f32[8,64,256]{2,1,0:T(8,128)S(1)}, u32[]{:S(2)}, u32[]{:S(2)}) collective-permute-start(f32[8,64,256]{2,1,0:T(8,128)} %get-tuple-element.28), channel_id=1, source_target_pairs={{0,24},{8,16},{16,8},{24,0},{1,25},{9,17},{17,9},{25,1},{2,26},{10... | collective-permute-start | bytes 1572872 | tf_op jit(solution)/shard_map/ppermute | solution.py:24
  122.8 13.3 %collective-permute-start.34 = (f32[8,64,256]{2,1,0:T(8,128)}, f32[8,64,256]{2,1,0:T(8,128)S(1)}, u32[]{:S(2)}, u32[]{:S(2)}) collective-permute-start(f32[8,64,256]{2,1,0:T(8,128)} %get-tuple-element.30), channel_id=1, source_target_pairs={{0,8},{8,0},{16,24},{24,16},{1,9},{9,1},{17,25},{25,17},{2,10},{10... | collective-permute-start | bytes 1572872 | tf_op jit(solution)/shard_map/ppermute | solution.py:24
  122.8 16.8 %collective-permute-start.38 = (f32[8,64,256]{2,1,0:T(8,128)}, f32[8,64,256]{2,1,0:T(8,128)S(1)}, u32[]{:S(2)}, u32[]{:S(2)}) collective-permute-start(f32[8,64,256]{2,1,0:T(8,128)} %get-tuple-element.32), channel_id=1, source_target_pairs={{0,96},{32,64},{64,32},{96,0},{1,97},{33,65},{65,33},{97,1},{2,98}... | collective-permute-start | bytes 1572872 | tf_op jit(solution)/shard_map/ppermute | solution.py:24
  125.6 16.8 %collective-permute-start.40 = (f32[8,64,256]{2,1,0:T(8,128)}, f32[8,64,256]{2,1,0:T(8,128)S(1)}, u32[]{:S(2)}, u32[]{:S(2)}) collective-permute-start(f32[8,64,256]{2,1,0:T(8,128)} %get-tuple-element.34), channel_id=1, source_target_pairs={{0,32},{32,0},{64,96},{96,64},{1,33},{33,1},{65,97},{97,65},{2,34}... | collective-permute-start | bytes 1572872 | tf_op jit(solution)/shard_map/ppermute | solution.py:24
  136.0 11.1 %collective-permute-start.33 = (f32[4,64,256]{2,1,0:T(8,128)S(1)}, f32[4,64,256]{2,1,0:T(8,128)S(1)}, u32[]{:S(2)}, u32[]{:S(2)}) collective-permute-start(f32[4,64,256]{2,1,0:T(8,128)S(1)} %slice_add_fusion.22), channel_id=1, source_target_pairs={{0,8},{8,0},{16,24},{24,16},{1,9},{9,1},{17,25},{25,17},{2,10},{10... | collective-permute-start | bytes 786440 | tf_op jit(solution)/shard_map/ppermute | solution.py:24
  137.1 10.1 %collective-permute-start.35 = (f32[4,64,256]{2,1,0:T(8,128)S(1)}, f32[4,64,256]{2,1,0:T(8,128)S(1)}, u32[]{:S(2)}, u32[]{:S(2)}) collective-permute-start(f32[4,64,256]{2,1,0:T(8,128)S(1)} %slice_add_fusion.20), channel_id=1, source_target_pairs={{0,24},{8,16},{16,8},{24,0},{1,25},{9,17},{17,9},{25,1},{2,26},{10... | collective-permute-start | bytes 786440 | tf_op jit(solution)/shard_map/ppermute | solution.py:24
  139.7 8.7 %collective-permute-start.39 = (f32[4,64,256]{2,1,0:T(8,128)S(1)}, f32[4,64,256]{2,1,0:T(8,128)S(1)}, u32[]{:S(2)}, u32[]{:S(2)}) collective-permute-start(f32[4,64,256]{2,1,0:T(8,128)S(1)} %slice_add_fusion.18), channel_id=1, source_target_pairs={{0,32},{32,0},{64,96},{96,64},{1,33},{33,1},{65,97},{97,65},{2,34}... | collective-permute-start | bytes 786440 | tf_op jit(solution)/shard_map/ppermute | solution.py:24
  142.4 9.5 %collective-permute-start.41 = (f32[4,64,256]{2,1,0:T(8,128)S(1)}, f32[4,64,256]{2,1,0:T(8,128)S(1)}, u32[]{:S(2)}, u32[]{:S(2)}) collective-permute-start(f32[4,64,256]{2,1,0:T(8,128)S(1)} %slice_add_fusion.16), channel_id=1, source_target_pairs={{0,96},{32,64},{64,32},{96,0},{1,97},{33,65},{65,33},{97,1},{2,98}... | collective-permute-start | bytes 786440 | tf_op jit(solution)/shard_map/ppermute | solution.py:24
  147.3 10.3 %collective-permute-start.36 = (f32[2,128,256]{2,1,0:T(8,128)S(1)}, f32[2,128,256]{2,1,0:T(8,128)S(1)}, u32[]{:S(2)}, u32[]{:S(2)}) collective-permute-start(f32[2,128,256]{2,1,0:T(8,128)S(1)} %fusion.3), channel_id=1, source_target_pairs={{0,96},{32,64},{64,32},{96,0},{1,97},{33,65},{65,33},{97,1},{2,98}... | collective-permute-start | bytes 786440 | tf_op jit(solution)/shard_map/ppermute | solution.py:24
  152.0 6.8 %collective-permute-start.42 = (f32[2,128,256]{2,1,0:T(8,128)S(1)}, f32[2,128,256]{2,1,0:T(8,128)S(1)}, u32[]{:S(2)}, u32[]{:S(2)}) collective-permute-start(f32[2,128,256]{2,1,0:T(8,128)S(1)} %fusion.2), channel_id=1, source_target_pairs={{0,24},{8,16},{16,8},{24,0},{1,25},{9,17},{17,9},{25,1},{2,26},{10... | collective-permute-start | bytes 786440 | tf_op jit(solution)/shard_map/ppermute | solution.py:24
  163.8 7.1 %collective-permute-start.44 = (f32[192,128]{1,0:T(8,128)S(1)}, f32[192,128]{1,0:T(8,128)S(1)}, u32[]{:S(2)}, u32[]{:S(2)}) collective-permute-start(f32[192,128]{1,0:T(8,128)S(1)} %slice_select_fusion.1), channel_id=1, source_target_pairs={{0,1},{1,0},{2,3},{3,2},{4,5},{5,4},{6,7},{7,6},{8,9},{9,8},{10,11... | collective-permute-start | bytes 294920 | tf_op jit(solution)/shard_map/ppermute | solution.py:24
  171.0 7.3 %collective-permute-start.45 = (f32[192,128]{1,0:T(8,128)S(1)}, f32[192,128]{1,0:T(8,128)S(1)}, u32[]{:S(2)}, u32[]{:S(2)}) collective-permute-start(f32[192,128]{1,0:T(8,128)S(1)} %select_add_fusion.1), channel_id=1, source_target_pairs={{0,32},{32,0},{64,96},{96,64},{1,33},{33,1},{65,97},{97,65},{2,34}... | collective-permute-start | bytes 294920 | tf_op jit(solution)/shard_map/ppermute | solution.py:24
  175.3 14.5 %collective-permute-start.53 = (f32[2,128,256]{2,1,0:T(8,128)S(1)}, f32[2,128,256]{2,1,0:T(8,128)S(1)}, u32[]{:S(2)}, u32[]{:S(2)}) collective-permute-start(f32[2,128,256]{2,1,0:T(8,128)S(1)} %pad_maximum_fusion.16), channel_id=1, source_target_pairs={{0,96},{32,64},{64,32},{96,0},{1,97},{33,65},{65,33},{97,1},{2,98}... | collective-permute-start | bytes 786440 | tf_op jit(solution)/shard_map/ppermute | solution.py:24
  178.3 7.8 %collective-permute-start.58 = (f32[1,128,256]{2,1,0:T(8,128)S(1)}, f32[1,128,256]{2,1,0:T(8,128)S(1)}, u32[]{:S(2)}, u32[]{:S(2)}) collective-permute-start(f32[1,128,256]{2,1,0:T(8,128)S(1)} %get-tuple-element.70), channel_id=1, source_target_pairs={{0,8},{8,0},{16,24},{24,16},{1,9},{9,1},{17,25},{25,17},{2,10},{10... | collective-permute-start | bytes 393224 | tf_op jit(solution)/shard_map/ppermute | solution.py:24
  178.3 7.5 %collective-permute-start.46 = (f32[192,128]{1,0:T(8,128)S(1)}, f32[192,128]{1,0:T(8,128)S(1)}, u32[]{:S(2)}, u32[]{:S(2)}) collective-permute-start(f32[192,128]{1,0:T(8,128)S(1)} %add.375), channel_id=1, source_target_pairs={{0,96},{32,64},{64,32},{96,0},{1,97},{33,65},{65,33},{97,1},{2,98}... | collective-permute-start | bytes 294920 | tf_op jit(solution)/shard_map/ppermute | solution.py:24
  186.1 7.2 %collective-permute-start.59 = (f32[2,128,256]{2,1,0:T(8,128)S(1)}, f32[2,128,256]{2,1,0:T(8,128)S(1)}, u32[]{:S(2)}, u32[]{:S(2)}) collective-permute-start(f32[2,128,256]{2,1,0:T(8,128)S(1)} %pad_maximum_fusion.17), channel_id=1, source_target_pairs={{0,24},{8,16},{16,8},{24,0},{1,25},{9,17},{17,9},{25,1},{2,26},{10... | collective-permute-start | bytes 786440 | tf_op jit(solution)/shard_map/ppermute | solution.py:24
  189.4 6.1 %collective-permute-start.48 = (f32[192,128]{1,0:T(8,128)S(1)}, f32[192,128]{1,0:T(8,128)S(1)}, u32[]{:S(2)}, u32[]{:S(2)}) collective-permute-start(f32[192,128]{1,0:T(8,128)S(1)} %add.377), channel_id=1, source_target_pairs={{0,24},{8,16},{16,8},{24,0},{1,25},{9,17},{17,9},{25,1},{2,26},{10... | collective-permute-start | bytes 294920 | tf_op jit(solution)/shard_map/ppermute | solution.py:24
  189.9 11.6 %collective-permute-start.56 = (f32[4,64,256]{2,1,0:T(8,128)S(1)}, f32[4,64,256]{2,1,0:T(8,128)S(1)}, u32[]{:S(2)}, u32[]{:S(2)}) collective-permute-start(f32[4,64,256]{2,1,0:T(8,128)S(1)} %get-tuple-element.62), channel_id=1, source_target_pairs={{0,24},{8,16},{16,8},{24,0},{1,25},{9,17},{17,9},{25,1},{2,26},{10... | collective-permute-start | bytes 786440 | tf_op jit(solution)/shard_map/ppermute | solution.py:24
  192.3 8.7 %collective-permute-start.54 = (f32[4,64,256]{2,1,0:T(8,128)S(1)}, f32[4,64,256]{2,1,0:T(8,128)S(1)}, u32[]{:S(2)}, u32[]{:S(2)}) collective-permute-start(f32[4,64,256]{2,1,0:T(8,128)S(1)} %get-tuple-element.63), channel_id=1, source_target_pairs={{0,8},{8,0},{16,24},{24,16},{1,9},{9,1},{17,25},{25,17},{2,10},{10... | collective-permute-start | bytes 786440 | tf_op jit(solution)/shard_map/ppermute | solution.py:24
  197.7 5.6 %collective-permute-start.60 = (f32[4,64,256]{2,1,0:T(8,128)S(1)}, f32[4,64,256]{2,1,0:T(8,128)S(1)}, u32[]{:S(2)}, u32[]{:S(2)}) collective-permute-start(f32[4,64,256]{2,1,0:T(8,128)S(1)} %get-tuple-element.61), channel_id=1, source_target_pairs={{0,32},{32,0},{64,96},{96,64},{1,33},{33,1},{65,97},{97,65},{2,34}... | collective-permute-start | bytes 786440 | tf_op jit(solution)/shard_map/ppermute | solution.py:24
  197.8 13.6 %collective-permute-start.62 = (f32[4,64,256]{2,1,0:T(8,128)S(1)}, f32[4,64,256]{2,1,0:T(8,128)S(1)}, u32[]{:S(2)}, u32[]{:S(2)}) collective-permute-start(f32[4,64,256]{2,1,0:T(8,128)S(1)} %get-tuple-element.60), channel_id=1, source_target_pairs={{0,96},{32,64},{64,32},{96,0},{1,97},{33,65},{65,33},{97,1},{2,98}... | collective-permute-start | bytes 786440 | tf_op jit(solution)/shard_map/ppermute | solution.py:24
  201.1 25.3 %collective-permute-start.55 = (f32[8,64,256]{2,1,0:T(8,128)S(1)}, f32[8,64,256]{2,1,0:T(8,128)S(1)}, u32[]{:S(2)}, u32[]{:S(2)}) collective-permute-start(f32[8,64,256]{2,1,0:T(8,128)S(1)} %pad_maximum_fusion.7.refs_6_), channel_id=1, source_target_pairs={{0,24},{8,16},{16,8},{24,0},{1,25},{9,17},{17,9},{25,1},{2,26},{10... | collective-permute-start | bytes 1572872 | tf_op jit(solution)/shard_map/ppermute | solution.py:24
  201.5 24.8 %collective-permute-start.57 = (f32[8,64,256]{2,1,0:T(8,128)S(1)}, f32[8,64,256]{2,1,0:T(8,128)}, u32[]{:S(2)}, u32[]{:S(2)}) collective-permute-start(f32[8,64,256]{2,1,0:T(8,128)S(1)} %pad_maximum_fusion.8.refs_8_), channel_id=1, source_target_pairs={{0,8},{8,0},{16,24},{24,16},{1,9},{9,1},{17,25},{25,17},{2,10},{10... | collective-permute-start | bytes 1572872 | tf_op jit(solution)/shard_map/ppermute | solution.py:24
  203.3 23.0 %collective-permute-start.61 = (f32[8,64,256]{2,1,0:T(8,128)S(1)}, f32[8,64,256]{2,1,0:T(8,128)}, u32[]{:S(2)}, u32[]{:S(2)}) collective-permute-start(f32[8,64,256]{2,1,0:T(8,128)S(1)} %pad_maximum_fusion.10.refs_10_), channel_id=1, source_target_pairs={{0,96},{32,64},{64,32},{96,0},{1,97},{33,65},{65,33},{97,1},{2,98}... | collective-permute-start | bytes 1572872 | tf_op jit(solution)/shard_map/ppermute | solution.py:24
  204.7 7.6 %collective-permute-start.51 = (f32[192,128]{1,0:T(8,128)S(1)}, f32[192,128]{1,0:T(8,128)S(1)}, u32[]{:S(2)}, u32[]{:S(2)}) collective-permute-start(f32[192,128]{1,0:T(8,128)S(1)} %add.380), channel_id=1, source_target_pairs={{0,1},{1,0},{2,3},{3,2},{4,5},{5,4},{6,7},{7,6},{8,9},{9,8},{10,11... | collective-permute-start | bytes 294920 | tf_op jit(solution)/shard_map/ppermute | solution.py:24
  211.5 14.9 %collective-permute-start.63 = (f32[8,64,256]{2,1,0:T(8,128)S(1)}, f32[8,64,256]{2,1,0:T(8,128)}, u32[]{:S(2)}, u32[]{:S(2)}) collective-permute-start(f32[8,64,256]{2,1,0:T(8,128)S(1)} %pad_maximum_fusion.11.refs_12_), channel_id=1, source_target_pairs={{0,32},{32,0},{64,96},{96,64},{1,33},{33,1},{65,97},{97,65},{2,34}... | collective-permute-start | bytes 1572872 | tf_op jit(solution)/shard_map/ppermute | solution.py:24
  245.8 7.7 %collective-permute-start.67 = (f32[2,128,256]{2,1,0:T(8,128)S(1)}, f32[2,128,256]{2,1,0:T(8,128)S(1)}, u32[]{:S(2)}, u32[]{:S(2)}) collective-permute-start(f32[2,128,256]{2,1,0:T(8,128)S(1)} %get-tuple-element.57), channel_id=1, source_target_pairs={{0,2},{2,0},{4,6},{6,4},{1,3},{3,1},{5,7},{7,5},{8,10},{10,8},{12,... | collective-permute-start | bytes 786440 | tf_op jit(solution)/shard_map/ppermute | solution.py:24
  247.4 8.7 %collective-permute-start.65 = (f32[2,128,256]{2,1,0:T(8,128)S(1)}, f32[2,128,256]{2,1,0:T(8,128)S(1)}, u32[]{:S(2)}, u32[]{:S(2)}) collective-permute-start(f32[2,128,256]{2,1,0:T(8,128)S(1)} %get-tuple-element.59), channel_id=1, source_target_pairs={{0,6},{2,4},{4,2},{6,0},{1,7},{3,5},{5,3},{7,1},{8,14},{10,12},{12... | collective-permute-start | bytes 786440 | tf_op jit(solution)/shard_map/ppermute | solution.py:24
  264.7 6.7 %collective-permute-start.70 = (f32[2,128,256]{2,1,0:T(8,128)S(1)}, f32[2,128,256]{2,1,0:T(8,128)S(1)}, u32[]{:S(2)}, u32[]{:S(2)}) collective-permute-start(f32[2,128,256]{2,1,0:T(8,128)S(1)} %pad_maximum_fusion.18.refs_4_), channel_id=1, source_target_pairs={{0,6},{2,4},{4,2},{6,0},{1,7},{3,5},{5,3},{7,1},{8,14},{10,12},{12... | collective-permute-start | bytes 786440 | tf_op jit(solution)/shard_map/ppermute | solution.py:24
  266.0 9.6 %collective-permute-start.72 = (f32[2,128,256]{2,1,0:T(8,128)S(1)}, f32[2,128,256]{2,1,0:T(8,128)S(1)}, u32[]{:S(2)}, u32[]{:S(2)}) collective-permute-start(f32[2,128,256]{2,1,0:T(8,128)S(1)} %pad_maximum_fusion.19.refs_6_), channel_id=1, source_target_pairs={{0,2},{2,0},{4,6},{6,4},{1,3},{3,1},{5,7},{7,5},{8,10},{10,8},{12,... | collective-permute-start | bytes 786440 | tf_op jit(solution)/shard_map/ppermute | solution.py:24
  266.6 9.3 %collective-permute-start.73 = (f32[2,128,256]{2,1,0:T(8,128)S(1)}, f32[2,128,256]{2,1,0:T(8,128)S(1)}, u32[]{:S(2)}, u32[]{:S(2)}) collective-permute-start(f32[2,128,256]{2,1,0:T(8,128)S(1)} %pad_maximum_fusion.18.refs_4_), channel_id=1, source_target_pairs={{0,1},{1,0},{2,3},{3,2},{4,5},{5,4},{6,7},{7,6},{8,9},{9,8},{10,11... | collective-permute-start | bytes 786440 | tf_op jit(solution)/shard_map/ppermute | solution.py:24
  271.4 5.4 %collective-permute-start.74 = (f32[2,128,256]{2,1,0:T(8,128)S(1)}, f32[2,128,256]{2,1,0:T(8,128)S(1)}, u32[]{:S(2)}, u32[]{:S(2)}) collective-permute-start(f32[2,128,256]{2,1,0:T(8,128)S(1)} %collective-permute-done.70.refs_5_), channel_id=1, source_target_pairs={{0,1},{1,0},{2,3},{3,2},{4,5},{5,4},{6,7},{7,6},{8,9},{9,8},{10,11... | collective-permute-start | bytes 786440 | tf_op jit(solution)/shard_map/ppermute | solution.py:24
  286.8 14.6 %collective-permute-start.77 = (f32[8,64,256]{2,1,0:T(8,128)}, f32[8,64,256]{2,1,0:T(8,128)S(1)}, u32[]{:S(2)}, u32[]{:S(2)}) collective-permute-start(f32[8,64,256]{2,1,0:T(8,128)} %get-tuple-element.38), channel_id=1, source_target_pairs={{0,24},{8,16},{16,8},{24,0},{1,25},{9,17},{17,9},{25,1},{2,26},{10... | collective-permute-start | bytes 1572872 | tf_op jit(solution)/shard_map/ppermute | solution.py:24
  287.4 15.3 %collective-permute-start.79 = (f32[8,64,256]{2,1,0:T(8,128)}, f32[8,64,256]{2,1,0:T(8,128)S(1)}, u32[]{:S(2)}, u32[]{:S(2)}) collective-permute-start(f32[8,64,256]{2,1,0:T(8,128)} %get-tuple-element.40), channel_id=1, source_target_pairs={{0,8},{8,0},{16,24},{24,16},{1,9},{9,1},{17,25},{25,17},{2,10},{10... | collective-permute-start | bytes 1572872 | tf_op jit(solution)/shard_map/ppermute | solution.py:24
  287.9 16.3 %collective-permute-start.83 = (f32[8,64,256]{2,1,0:T(8,128)}, f32[8,64,256]{2,1,0:T(8,128)S(1)}, u32[]{:S(2)}, u32[]{:S(2)}) collective-permute-start(f32[8,64,256]{2,1,0:T(8,128)} %get-tuple-element.42), channel_id=1, source_target_pairs={{0,96},{32,64},{64,32},{96,0},{1,97},{33,65},{65,33},{97,1},{2,98}... | collective-permute-start | bytes 1572872 | tf_op jit(solution)/shard_map/ppermute | solution.py:24
  291.2 15.6 %collective-permute-start.85 = (f32[8,64,256]{2,1,0:T(8,128)}, f32[8,64,256]{2,1,0:T(8,128)S(1)}, u32[]{:S(2)}, u32[]{:S(2)}) collective-permute-start(f32[8,64,256]{2,1,0:T(8,128)} %get-tuple-element.44), channel_id=1, source_target_pairs={{0,32},{32,0},{64,96},{96,64},{1,33},{33,1},{65,97},{97,65},{2,34}... | collective-permute-start | bytes 1572872 | tf_op jit(solution)/shard_map/ppermute | solution.py:24
  302.5 9.1 %collective-permute-start.78 = (f32[4,64,256]{2,1,0:T(8,128)S(1)}, f32[4,64,256]{2,1,0:T(8,128)S(1)}, u32[]{:S(2)}, u32[]{:S(2)}) collective-permute-start(f32[4,64,256]{2,1,0:T(8,128)S(1)} %slice_add_fusion.10), channel_id=1, source_target_pairs={{0,8},{8,0},{16,24},{24,16},{1,9},{9,1},{17,25},{25,17},{2,10},{10... | collective-permute-start | bytes 786440 | tf_op jit(solution)/shard_map/ppermute | solution.py:24
  303.7 8.0 %collective-permute-start.80 = (f32[4,64,256]{2,1,0:T(8,128)S(1)}, f32[4,64,256]{2,1,0:T(8,128)S(1)}, u32[]{:S(2)}, u32[]{:S(2)}) collective-permute-start(f32[4,64,256]{2,1,0:T(8,128)S(1)} %slice_add_fusion.8), channel_id=1, source_target_pairs={{0,24},{8,16},{16,8},{24,0},{1,25},{9,17},{17,9},{25,1},{2,26},{10... | collective-permute-start | bytes 786440 | tf_op jit(solution)/shard_map/ppermute | solution.py:24
  304.2 9.4 %collective-permute-start.84 = (f32[4,64,256]{2,1,0:T(8,128)S(1)}, f32[4,64,256]{2,1,0:T(8,128)S(1)}, u32[]{:S(2)}, u32[]{:S(2)}) collective-permute-start(f32[4,64,256]{2,1,0:T(8,128)S(1)} %slice_add_fusion.6), channel_id=1, source_target_pairs={{0,32},{32,0},{64,96},{96,64},{1,33},{33,1},{65,97},{97,65},{2,34}... | collective-permute-start | bytes 786440 | tf_op jit(solution)/shard_map/ppermute | solution.py:24
  306.8 9.6 %collective-permute-start.86 = (f32[4,64,256]{2,1,0:T(8,128)S(1)}, f32[4,64,256]{2,1,0:T(8,128)S(1)}, u32[]{:S(2)}, u32[]{:S(2)}) collective-permute-start(f32[4,64,256]{2,1,0:T(8,128)S(1)} %slice_add_fusion.4), channel_id=1, source_target_pairs={{0,96},{32,64},{64,32},{96,0},{1,97},{33,65},{65,33},{97,1},{2,98}... | collective-permute-start | bytes 786440 | tf_op jit(solution)/shard_map/ppermute | solution.py:24
  311.8 10.2 %collective-permute-start.81 = (f32[2,128,256]{2,1,0:T(8,128)S(1)}, f32[2,128,256]{2,1,0:T(8,128)S(1)}, u32[]{:S(2)}, u32[]{:S(2)}) collective-permute-start(f32[2,128,256]{2,1,0:T(8,128)S(1)} %fusion.1), channel_id=1, source_target_pairs={{0,96},{32,64},{64,32},{96,0},{1,97},{33,65},{65,33},{97,1},{2,98}... | collective-permute-start | bytes 786440 | tf_op jit(solution)/shard_map/ppermute | solution.py:24
  316.5 6.8 %collective-permute-start.87 = (f32[2,128,256]{2,1,0:T(8,128)S(1)}, f32[2,128,256]{2,1,0:T(8,128)S(1)}, u32[]{:S(2)}, u32[]{:S(2)}) collective-permute-start(f32[2,128,256]{2,1,0:T(8,128)S(1)} %fusion), channel_id=1, source_target_pairs={{0,24},{8,16},{16,8},{24,0},{1,25},{9,17},{17,9},{25,1},{2,26},{10... | collective-permute-start | bytes 786440 | tf_op jit(solution)/shard_map/ppermute | solution.py:24
  328.3 7.3 %collective-permute-start.89 = (f32[192,128]{1,0:T(8,128)S(1)}, f32[192,128]{1,0:T(8,128)S(1)}, u32[]{:S(2)}, u32[]{:S(2)}) collective-permute-start(f32[192,128]{1,0:T(8,128)S(1)} %slice_select_fusion), channel_id=1, source_target_pairs={{0,1},{1,0},{2,3},{3,2},{4,5},{5,4},{6,7},{7,6},{8,9},{9,8},{10,11... | collective-permute-start | bytes 294920 | tf_op jit(solution)/shard_map/ppermute | solution.py:24
  362.1 7.9 %collective-permute-start.96 = (f32[192,128]{1,0:T(8,128)S(1)}, f32[192,128]{1,0:T(8,128)S(1)}, u32[]{:S(2)}, u32[]{:S(2)}) collective-permute-start(f32[192,128]{1,0:T(8,128)S(1)} %add.417), channel_id=1, source_target_pairs={{0,1},{1,0},{2,3},{3,2},{4,5},{5,4},{6,7},{7,6},{8,9},{9,8},{10,11... | collective-permute-start | bytes 294920 | tf_op jit(solution)/shard_map/ppermute | solution.py:24
  (74 other events, 510.0 us)
